TPU v7x, 32 devices: a whole 2x2x4 slice. The times are simulated.
32 devices in a mesh: grid: 8 (over z, y), probe: 4 (over x, core).
Axes of the slice: x: 2, y: 2, z: 4, core: 2. Of those that a mesh axis runs over, the one named last changes fastest.
Arguments:
- probes: float32 [2048, 8, 2048], P('grid', 'probe'), may hold values from -6 to 6
- corr_lengths: float32 [2], replicated, may hold values from 32 to 256
- footprints: bfloat16 [2048, 16, 128], P('grid'), may hold values from 4.863739e-05 to 0.001953125
- reading_slab: int32 [2048, 1], P('grid'), may hold values from 0 to 7; in each aligned block of 256 rows (0 to 255, 256 to 511, ...) at most 64 rows name the same one
- reading_band: int32 [2048], P('grid'), may hold values from 0 to 15
- reading_tile: int32 [2048], P('grid'), may hold values from 0 to 15
Outputs:
- smoothed: float32 [2048, 8, 2048], P('grid', 'probe')
- sketch: float32 [2048, 8], P('grid', 'probe')
- factor: float32 [8, 8], replicated
- basis: float32 [2048, 8], P('grid', 'probe')
Inputs may be any that keep to these rules, and one draw needn't show every extreme that they name: `reading_slab`: among the 256 readings of one owner (aligned blocks of rows), no slab index is named by more than 64 readings, and in every draw some slab index of some owner is named by exactly 64.
All inputs are finite; a program needn't handle non-finite values.
Results may differ from a plain program's by a relative error of at most 0.00065.
Values may be sent and summed in bfloat16 or wider, within the bound.
No kernel may reach another device: no remote copies, remote signals or barrier semaphores. Data moves between devices by JAX's collectives and lax.ppermute only.
A program may use at most 128 MiB of HBM per device.

v0:
```python
import math

import jax
import jax.numpy as jnp
from jax import lax
from jax.sharding import PartitionSpec as P


def from_partner(value, axis, distance):
    mask = 2**distance
    pairs = [(source, source ^ mask) for source in range(lax.axis_size(axis))]
    return lax.ppermute(value, axis, pairs)


def wavenumbers(index_vals, length):
    signed_vals = jnp.where(index_vals < length // 2, index_vals, index_vals - length)
    return signed_vals.astype(jnp.float32) * (2.0 * math.pi / length)


def angle_table(row_index, col_index, length):
    product = row_index[:, None] * col_index[None, :] % length
    return product.astype(jnp.float32) * (2.0 * math.pi / length)


def split_length(length):
    lead_size = 1
    for divisor in range(1, math.isqrt(length) + 1):
        if length % divisor == 0:
            lead_size = divisor
    return lead_size


def part_table(count, direction):
    steps_here = jnp.arange(count, dtype=jnp.int32)
    angles = angle_table(steps_here, steps_here, count)
    cosine = jnp.cos(angles)
    sine_part = direction * jnp.sin(angles)
    return jnp.stack(
        [jnp.stack([cosine, -sine_part], axis=1), jnp.stack([sine_part, cosine], axis=1)]
    )


def dft_front(stacked, direction):
    length = stacked.shape[1]
    batch_width = stacked.shape[2]
    lead_size = split_length(length)
    tail_size = length // lead_size
    blocks_in = stacked.reshape(2, lead_size, tail_size, batch_width)
    section_one = jnp.einsum(
        "pkqa,qabr->pkbr",
        part_table(lead_size, direction),
        blocks_in,
        precision=lax.Precision.HIGHEST,
    )
    twiddle = angle_table(
        jnp.arange(lead_size, dtype=jnp.int32), jnp.arange(tail_size, dtype=jnp.int32), length
    )
    turn_cos = jnp.cos(twiddle)[:, :, None]
    turn_sin = (direction * jnp.sin(twiddle))[:, :, None]
    turned = jnp.stack(
        [
            section_one[0] * turn_cos - section_one[1] * turn_sin,
            section_one[0] * turn_sin + section_one[1] * turn_cos,
        ]
    )
    result = jnp.einsum(
        "pmqb,qkbr->pmkr", part_table(tail_size, direction), turned, precision=lax.Precision.HIGHEST
    )
    return result.reshape(2, length, batch_width)


def transform_right(operands, direction, with_imag):
    real_in = operands[0]
    imag_in = operands[1] if len(operands) > 1 else jnp.zeros_like(real_in)
    result = dft_front(jnp.stack([real_in.T, imag_in.T]), direction)
    if with_imag:
        return (result[0].T, result[1].T)
    return (result[0].T, None)


def transform_left(stacked, direction):
    length = stacked.shape[0] // 2
    result = dft_front(stacked.reshape(2, length, stacked.shape[1]), direction)
    return (result[0], result[1])


def local(probes, corr_lengths, footprints, reading_slab, reading_band, reading_tile):
    slab_rows, per_dev, width = probes.shape
    slab_count = lax.axis_size("grid")
    height = slab_rows * slab_count
    cols_dev = width // slab_count
    grid_at = lax.axis_index("grid")
    wave_y = wavenumbers(jnp.arange(height, dtype=jnp.int32), height)
    wave_x = wavenumbers(grid_at * cols_dev + jnp.arange(cols_dev, dtype=jnp.int32), width)
    spectrum_shape = (
        1.0 + (corr_lengths[0] * wave_y)[:, None] ** 2 + (corr_lengths[1] * wave_x)[None, :] ** 2
    ) ** (-0.75)
    power = lax.psum(jnp.sum(spectrum_shape * spectrum_shape), "grid")
    spectral_filter = spectrum_shape * lax.rsqrt(power / (height * width))
    flat_probes = probes.reshape(slab_rows * per_dev, width)
    spec_real, spec_imag = transform_right((flat_probes,), -1.0, True)
    spectra = jnp.stack(
        [spec_real.reshape(slab_rows, per_dev, width), spec_imag.reshape(slab_rows, per_dev, width)]
    )
    column_block = lax.all_to_all(spectra, "grid", split_axis=3, concat_axis=1, tiled=True)
    item_here = column_block.shape[2]
    stacked = column_block.reshape(2 * height, item_here * cols_dev)
    col_real, col_imag = transform_left(stacked, -1.0)
    filter_cols = jnp.tile(spectral_filter, (1, item_here))
    back_real, back_imag = transform_left(
        jnp.concatenate([col_real * filter_cols, col_imag * filter_cols], axis=0), 1.0
    )
    filtered = jnp.stack([back_real, back_imag]).reshape(2, height, item_here, cols_dev)
    mixed = lax.all_to_all(filtered, "grid", split_axis=1, concat_axis=3, tiled=True)
    mixed_real = mixed[0].reshape(-1, width)
    mixed_imag = mixed[1].reshape(-1, width)
    inverse_scale = 1.0 / (height * width)
    out_real, unused_imag = transform_right((mixed_real, mixed_imag), 1.0, False)
    smoothed = out_real.reshape(slab_rows, per_dev, width) * inverse_scale
    field_b = smoothed.astype(jnp.bfloat16)
    read_count, band_rows, tile_cols = footprints.shape
    band_count = slab_rows // band_rows
    tile_count = width // tile_cols
    block_total = band_count * tile_count
    field_blocks = field_b.reshape(band_count, band_rows, per_dev, tile_count, tile_cols)
    field_blocks = field_blocks.transpose(1, 4, 0, 3, 2).reshape(
        band_rows * tile_cols, block_total * per_dev
    )
    capacity = 2 * read_count // slab_count
    target = reading_slab[:, 0]
    onehot = (target[:, None] == jnp.arange(slab_count, dtype=jnp.int32)[None, :]).astype(jnp.int32)
    slot_index = jnp.sum(jnp.cumsum(onehot, axis=0) * onehot, axis=1) - 1
    block_index = reading_band * tile_count + reading_tile
    flat_prints = footprints.reshape(read_count, band_rows * tile_cols)
    send_prints = (
        jnp.zeros((slab_count, capacity, band_rows * tile_cols), jnp.bfloat16)
        .at[target, slot_index]
        .set(flat_prints)
    )
    send_index = (
        jnp.zeros((slab_count, capacity), jnp.int32).at[target, slot_index].set(block_index)
    )
    recv_prints, recv_index = (
        lax.all_to_all(send_prints, "grid", split_axis=0, concat_axis=0, tiled=True),
        lax.all_to_all(send_index, "grid", split_axis=0, concat_axis=0, tiled=True),
    )
    values = jnp.dot(
        recv_prints.reshape(slab_count * capacity, band_rows * tile_cols),
        field_blocks,
        preferred_element_type=jnp.float32,
    )
    values = values.reshape(slab_count * capacity, block_total, per_dev)
    selector = (
        recv_index.reshape(-1)[:, None] == jnp.arange(block_total, dtype=jnp.int32)[None, :]
    ).astype(jnp.float32)
    partial_read = jnp.sum(values * selector[:, :, None], axis=1).reshape(
        slab_count, capacity, per_dev
    )
    returned = lax.all_to_all(partial_read, "grid", split_axis=0, concat_axis=0, tiled=True)
    sketch = returned[target, slot_index]
    full_sketch = lax.all_gather(sketch, "probe", axis=1, tiled=True)
    total_rows = read_count * slab_count
    local_gram = jnp.dot(full_sketch.T, full_sketch, precision=lax.Precision.HIGHEST) / total_rows
    lower_factor = jnp.linalg.cholesky(local_gram)
    for level in range(slab_count.bit_length() - 1):
        partner = from_partner(lower_factor, "grid", level)
        lower_factor = jnp.linalg.cholesky(
            jnp.dot(lower_factor, lower_factor.T, precision=lax.Precision.HIGHEST)
            + jnp.dot(partner, partner.T, precision=lax.Precision.HIGHEST)
        )
    factor = lower_factor.T
    solved = jax.scipy.linalg.solve_triangular(lower_factor, full_sketch.T, lower=True)
    lane_at = lax.axis_index("probe")
    basis_cols = lax.dynamic_slice_in_dim(solved, lane_at * per_dev, per_dev, 0).T
    return (smoothed, sketch, factor, basis_cols)


def solution(mesh):
    in_specs = (
        P("grid", "probe", None),
        P(),
        P("grid", None, None),
        P("grid", None),
        P("grid"),
        P("grid"),
    )
    out_specs = (P("grid", "probe", None), P("grid", "probe"), P(), P("grid", "probe"))
    return jax.shard_map(local, mesh=mesh, in_specs=in_specs, out_specs=out_specs, check_vma=False)
```

profile of v0, /device:TPU:0, one launch (start us, length us, event | category | flops | bytes accessed | tf_op | source)
XLA Modules:
  0.0 841.6 jit_solution(7328061356385280359)
XLA Ops:
  1.5 6.0 reshape.437
  7.5 5.3 copy.229
  12.9 3.2 stack.87.clone
  16.1 13.1 %fusion.24 = f32[2,32,64,512]{3,1,2,0:T(8,128)S(1)} fusion(f32[2,32,64,512]{3,2,1,0:T(8,128)S(1)} %bitcast.241, f32[1,32,2,32]{3,1,2,0:T(8,128)S(1)} %get-tuple-element.52, f32[1,32,2,32]{3,1,2,0:T(8,128)S(1)} %get-tuple-element.53), kind=kOutput, calls=%fused_computation.47 | convolution fusion | flops 1610616832 | bytes 16793600 | tf_op jit(solution)/shard_map/pkqa,qabr->pkbr/dot_general | solution.py:49
  32.2 12.6 %fusion.27 = f32[2,64,32,512]{3,1,2,0:T(8,128)S(1)} fusion(f32[2,32,64,512]{3,1,2,0:T(8,128)S(1)} %pad_maximum_fusion, f32[1,64,2,64]{3,1,2,0:T(8,128)S(1)} %get-tuple-element.48, f32[1,64,2,64]{3,1,2,0:T(8,128)S(1)} %get-tuple-element.49), kind=kOutput, calls=%fused_computation.48 | convolution fusion | flops 3221241856 | bytes 16842752 | tf_op jit(solution)/shard_map/pmqb,qkbr->pmkr/dot_general | solution.py:66
  44.9 3.4 fusion.133
  48.3 4.4 copy.165
  52.7 5.4 copy.166
  58.0 5.8 stack_reshape.6
  63.8 6.5 copy.167
  70.4 5.3 copy.168
  75.7 5.8 stack_reshape.7
  81.6 8.5 %pad_maximum_fusion.1 = f32[2,256,2,2048]{3,2,1,0:T(2,128)} fusion(f32[1,256,2,2048]{3,2,1,0:T(2,128)} %stack_reshape.7, f32[1,256,2,2048]{3,2,1,0:T(2,128)} %stack_reshape.6), kind=kLoop, calls=%fused_computation.4 | loop fusion | flops 2097152 | bytes 16777216 | tf_op jit(solution)/shard_map/stack | solution.py:102
  90.0 17.1 %copy.169 = f32[2,256,2,2048]{1,2,0,3:T(2,128)} copy(f32[2,256,2,2048]{3,2,1,0:T(2,128)} %pad_maximum_fusion.1) | data formatting | bytes 16777216 | tf_op jit(solution)/shard_map/stack | solution.py:102
  107.1 7.4 all-to-all-start
  118.3 160.6 %psum.7 = f32[]{:T(128)} all-reduce(f32[]{:T(128)} %multiply_reduce_fusion), channel_id=1, replica_groups=mesh['grid'=8,'probe'=4] {'grid'}, use_global_device_ids=true, to_apply=%region_1.2 | all-reduce | flops 1 | bytes 8 | tf_op jit(solution)/shard_map/psum | solution.py:98
  282.1 2.5 copy.230
  286.7 38.7 %scatter_fusion.1 = s32[8,64]{1,0:T(8,128)} fusion(s32[8,64]{1,0:T(8,128)} %broadcast_in_dim.5, s32[256]{0:T(256)S(1)} %bitcast.239, s32[256]{0:T(256)S(1)} %multiply_add_fusion.4), kind=kCustom, calls=%fused_computation.2 | custom fusion | bytes 5120 | tf_op jit(solution)/shard_map/scatter | solution.py:141
  325.5 31.3 %all-to-all-start.3 = ((s32[8,1,64]{2,1,0:T(1,128)}), s32[8,1,64]{2,1,0:T(1,128)S(1)}, u32[]{:S(2)}, u32[]{:S(2)}) async-start(s32[8,1,64]{2,1,0:T(1,128)} %bitcast.80), calls=%async_computation.3 | async-start | bytes 8192 | tf_op jit(solution)/shard_map/all_to_all | solution.py:145
  356.8 17.2 %copy.170 = f32[2,256,2,8,256]{4,2,1,3,0:T(2,128)} copy(f32[2,256,2,8,256]{1,2,0,4,3:T(2,128)} %bitcast.33) | data formatting | bytes 16777216 | tf_op jit(solution)/shard_map/all_to_all | solution.py:105
  374.0 11.5 %reshape_reshape_reshape.3 = f32[2,32,64,512]{3,2,1,0:T(8,128)} reshape(f32[2,8,256,2,256]{4,3,2,1,0:T(2,128)} %bitcast.244) | data formatting | bytes 16777216 | tf_op jit(solution)/shard_map/reshape;reshape;reshape | solution.py:48
  385.4 17.0 %fusion.30 = f32[2,32,64,512]{3,1,2,0:T(8,128)S(1)} fusion(f32[2,32,64,512]{3,2,1,0:T(8,128)} %reshape_reshape_reshape.3, f32[1,32,2,32]{3,1,2,0:T(8,128)S(1)} %get-tuple-element.52, f32[1,32,2,32]{3,1,2,0:T(8,128)S(1)} %get-tuple-element.53), kind=kOutput, calls=%fused_computation.49 | convolution fusion | flops 1610616832 | bytes 16793600 | tf_op jit(solution)/shard_map/pkqa,qabr->pkbr/dot_general | solution.py:49
  405.9 12.6 %fusion.33 = f32[2,64,32,512]{3,1,2,0:T(8,128)S(1)} fusion(f32[2,32,64,512]{3,1,2,0:T(8,128)S(1)} %pad_maximum_fusion.2, f32[1,64,2,64]{3,1,2,0:T(8,128)S(1)} %get-tuple-element.48, f32[1,64,2,64]{3,1,2,0:T(8,128)S(1)} %get-tuple-element.49), kind=kOutput, calls=%fused_computation.50 | convolution fusion | flops 3221241856 | bytes 16842752 | tf_op jit(solution)/shard_map/pmqb,qkbr->pmkr/dot_general | solution.py:66
  418.5 4.3 fusion.132
  422.8 4.8 copy.173
  427.6 4.4 copy.174
  432.0 7.4 bitcast_multiply_fusion.1
  439.4 4.4 pad_maximum_fusion.3
  443.9 12.7 %fusion.36 = f32[2,32,64,512]{3,1,2,0:T(8,128)S(1)} fusion(f32[2,32,64,512]{3,2,1,0:T(8,128)S(1)} %bitcast.242, f32[1,32,2,32]{3,1,2,0:T(8,128)S(1)} %get-tuple-element.54, f32[1,32,2,32]{3,1,2,0:T(8,128)S(1)} %get-tuple-element.51), kind=kOutput, calls=%fused_computation.51 | convolution fusion | flops 1610616832 | bytes 16793600 | tf_op jit(solution)/shard_map/pkqa,qabr->pkbr/dot_general | solution.py:49
  460.0 12.6 %fusion.39 = f32[2,64,32,512]{3,1,2,0:T(8,128)S(1)} fusion(f32[2,32,64,512]{3,1,2,0:T(8,128)S(1)} %pad_maximum_fusion.4, f32[1,64,2,64]{3,1,2,0:T(8,128)S(1)} %get-tuple-element.50, f32[1,64,2,64]{3,1,2,0:T(8,128)S(1)} %get-tuple-element.47), kind=kOutput, calls=%fused_computation.52 | convolution fusion | flops 3221241856 | bytes 16842752 | tf_op jit(solution)/shard_map/pmqb,qkbr->pmkr/dot_general | solution.py:66
  472.7 3.4 fusion.131
  476.1 4.4 copy.177
  480.5 5.9 stack.184
  486.4 6.6 copy.178
  493.0 5.9 stack.185
  498.8 5.8 pad_maximum_fusion.5
  504.6 5.9 copy.179
  510.5 6.1 all-to-all-start.1
  518.5 45.4 %scatter_fusion = bf16[8,64,2048]{2,1,0:T(8,128)(2,1)} fusion(bf16[8,64,2048]{2,1,0:T(8,128)(2,1)} %broadcast_in_dim.4, s32[256]{0:T(256)S(1)} %bitcast.240, bf16[256,2048]{1,0:T(8,128)(2,1)S(1)} %bitcast.263), kind=kCustom, calls=%fused_computation.1 | custom fusion | bytes 3147776 | tf_op jit(solution)/shard_map/scatter | solution.py:138
  563.9 132.6 %all-to-all-done.1 = f32[2,2048,2,256]{3,2,0,1:T(2,128)} async-done(((f32[2,2048,2,256]{3,2,0,1:T(2,128)}), f32[2,2048,2,256]{3,2,0,1:T(2,128)}, u32[]{:S(2)}, u32[]{:S(2)}) %all-to-all-start.1) | async-done | bytes 8388640 | tf_op jit(solution)/shard_map/all_to_all | solution.py:114
  696.5 4.8 all-to-all-start.2
  702.6 8.2 copy.288
  710.9 3.0 fusion.130
  713.8 3.9 copy.231
  717.7 5.3 copy.181
  723.1 6.7 copy.183
  729.8 4.0 copy.232
  733.7 5.5 copy.182
  739.2 4.8 copy.184
  744.0 8.3 fusion.45
  755.5 12.9 %fusion.42 = f32[2,64,32,512]{3,1,2,0:T(8,128)S(1)} fusion(f32[2,32,64,512]{3,1,2,0:T(8,128)S(1)} %pad_maximum_fusion.6, f32[1,64,2,64]{3,1,2,0:T(8,128)S(1)} %get-tuple-element.50, f32[1,64,2,64]{3,1,2,0:T(8,128)S(1)} %get-tuple-element.47), kind=kOutput, calls=%fused_computation.53 | convolution fusion | flops 3221241856 | bytes 16842752 | tf_op jit(solution)/shard_map/pmqb,qkbr->pmkr/dot_general | solution.py:66
  768.4 2.8 fusion.128
  772.4 2.4 copy.189
  774.8 2.2 copy.234
  778.5 2.7 dot_general.61
  781.2 3.8 fusion.52
  785.7 6.2 all-to-all-start.4
  791.9 6.5 copy.186
  798.5 5.4 copy.187
  803.9 5.8 mul.801
  813.1 5.2 all-gather
  820.6 2.1 collective-permute-start
  826.5 2.1 collective-permute-start.1
  832.5 3.0 collective-permute-start.2
  (116 shorter events, 47.0 us)
Async XLA Ops:
  107.1 7.4 copy-start.7
  107.1 218.4 %all-to-all-start = ((f32[2,256,2,2048]{1,2,0,3:T(2,128)}), f32[2,256,2,2048]{1,2,0,3:T(2,128)}, u32[]{:S(2)}, u32[]{:S(2)}) async-start(f32[2,256,2,2048]{1,2,0,3:T(2,128)} %copy.169), calls=%async_computation | async-start | bytes 16777216 | tf_op jit(solution)/shard_map/all_to_all | solution.py:105
  282.0 2.5 copy-start.6
  282.1 3.4 copy-start.8
  282.1 3.4 copy-start.9
  325.5 185.0 %all-to-all-start.3 = ((s32[8,1,64]{2,1,0:T(1,128)}), s32[8,1,64]{2,1,0:T(1,128)S(1)}, u32[]{:S(2)}, u32[]{:S(2)}) async-start(s32[8,1,64]{2,1,0:T(1,128)} %bitcast.80), calls=%async_computation.3 | async-start | bytes 8192 | tf_op jit(solution)/shard_map/all_to_all | solution.py:145
  422.8 4.8 copy-start.4
  427.6 4.4 copy-start.1
  510.5 6.1 copy-start.5
  510.5 186.0 %all-to-all-start.1 = ((f32[2,2048,2,256]{3,2,0,1:T(2,128)}), f32[2,2048,2,256]{3,2,0,1:T(2,128)}, u32[]{:S(2)}, u32[]{:S(2)}) async-start(f32[2,2048,2,256]{3,2,0,1:T(2,128)} %copy.179), calls=%async_computation.1 | async-start | bytes 16777216 | tf_op jit(solution)/shard_map/all_to_all | solution.py:114
  696.5 84.6 %all-to-all-start.2 = ((bf16[8,64,2048]{2,1,0:T(8,128)(2,1)}), bf16[8,64,2048]{2,1,0:T(8,128)(2,1)}, u32[]{:S(2)}, u32[]{:S(2)}) async-start(bf16[8,64,2048]{2,1,0:T(8,128)(2,1)} %scatter_fusion), calls=%async_computation.2 | async-start | bytes 4194304 | tf_op jit(solution)/shard_map/all_to_all | solution.py:144
  723.1 6.7 copy-start.3
  739.2 4.8 copy-start.2
  785.7 24.0 %all-to-all-start.4 = ((f32[8,1,128]{2,1,0:T(1,128)}), f32[8,1,128]{2,1,0:T(1,128)S(1)}, u32[]{:S(2)}, u32[]{:S(2)}) async-start(f32[8,1,128]{2,1,0:T(1,128)} %reshape.495), calls=%async_computation.4 | async-start | bytes 8192 | tf_op jit(solution)/shard_map/all_to_all | solution.py:159
  803.9 7.2 copy-start
  820.6 3.7 collective-permute-start
  826.5 3.7 collective-permute-start.1
  832.5 4.6 collective-permute-start.2
where the time goes:
time: 857 us; the launch traced here: 842 us
  local copies, waits for them, and re-layouts  309 us (36%)
  blocking collectives  166 us (19%)
  waiting for transfers between devices  136 us (16%)
  matrix products  107 us (12%)
  starting transfers between devices  62.9 us (7%)
  other arithmetic  57.4 us (7%)
    psum x1, blocking collectives, local(): power = lax.psum(jnp.sum(spectrum_shape * spectrum_shape), 'grid')  161 us
    all_to_all x1, waiting for transfers between devices, local(): lax.all_to_all(filtered, 'grid', split_axis=1, concat_axis=3, tiled=True)  133 us
    dot_general x4, matrix products, dft_front(): jnp.einsum('pkqa,qabr->pkbr', part_table(lead_size, direction), blocks_in...  51.1 us
    dot_general x4, matrix products, dft_front(): jnp.einsum('pmqb,qkbr->pmkr', part_table(tail_size, direction), turned, p...  50.8 us
    scatter x1, local copies, waits for them, and re-layouts, local(): send_prints = jnp.zeros((slab_count, capacity, band_rows * tile_cols), jn...  45.4 us
    scatter x1, local copies, waits for them, and re-layouts, local(): jnp.zeros((slab_count, capacity), jnp.int32).at[target, slot_index]  38.7 us
    all_to_all x1, starting transfers between devices, local(): lax.all_to_all(send_index, 'grid', split_axis=0, concat_axis=0, tiled=True)  31.3 us
    another operation x3, local copies, waits for them, and re-layouts, local(): jnp.stack([spec_real.reshape(slab_rows, per_dev, width), spec_imag.reshap...  28.7 us
  transfers between devices with their start and end apart: 8, of which 4 were waited for; matrix products, arithmetic and copies ran while one was open for 41% of the time, Pallas kernels for 0%

commit v1 on v0

v1 whole, which is shorter than its diff:
```python
import math

import jax
import jax.numpy as jnp
import ml_dtypes
import numpy as np
from jax import lax
from jax.experimental import pallas as pl
from jax.experimental.pallas import tpu as pltpu
from jax.sharding import PartitionSpec as P

RADIX = 8
STEPS = 64.0
TOP = 32700.0
TILE = 64
SUB = 16
LANES = 128
F32 = jnp.float32
BF16 = jnp.bfloat16
I16 = jnp.int16


def dft_blocks(length):
    grid = np.outer(np.arange(length), np.arange(length)) % length
    cosine, sine = np.cos(2 * np.pi * grid / length), np.sin(2 * np.pi * grid / length)
    forward = np.block([[cosine, -sine], [sine, cosine]]).astype(np.float32)
    lead = forward.astype(ml_dtypes.bfloat16)
    trail = (forward - lead.astype(np.float32)).astype(ml_dtypes.bfloat16)
    return lead, trail, lead.T.copy(), trail.T.copy()


def twiddles(length):
    short = length // RADIX
    angle = 2 * np.pi * np.outer(np.arange(RADIX), np.arange(short)) / length
    return np.concatenate([np.cos(angle), -np.sin(angle)]).astype(np.float32)


def turn(pair, sign):
    return (pair[1], -pair[0]) if sign < 0 else (-pair[1], pair[0])


def add(one, two):
    return (one[0] + two[0], one[1] + two[1])


def sub(one, two):
    return (one[0] - two[0], one[1] - two[1])


def dft8(x, sign):
    half = math.sqrt(0.5)
    a0, a1 = add(x[0], x[4]), sub(x[0], x[4])
    a2, a3 = add(x[2], x[6]), turn(sub(x[2], x[6]), sign)
    b0, b1 = add(x[1], x[5]), sub(x[1], x[5])
    b2, b3 = add(x[3], x[7]), turn(sub(x[3], x[7]), sign)
    even, odd = add(a0, a2), add(b0, b2)
    side, cross = sub(a0, a2), turn(sub(b0, b2), sign)
    c1, d1 = add(a1, a3), add(b1, b3)
    c3, d3 = sub(a1, a3), sub(b1, b3)
    t1, t3 = turn(d1, sign), turn(d3, sign)
    w1 = (half * (d1[0] + t1[0]), half * (d1[1] + t1[1]))
    w3 = (half * (t3[0] - d3[0]), half * (t3[1] - d3[1]))
    return [
        add(even, odd), add(c1, w1), add(side, cross), add(c3, w3),
        sub(even, odd), sub(c1, w1), sub(side, cross), sub(c3, w3),
    ]


def spin(pair, cosine, sine):
    return (pair[0] * cosine - pair[1] * sine, pair[0] * sine + pair[1] * cosine)


def split(value):
    lead = value.astype(BF16)
    return lead, (value - lead.astype(F32)).astype(BF16)


def dot(one, two):
    return jnp.dot(one, two, preferred_element_type=F32)


def encode(value):
    top = jnp.maximum(jnp.max(jnp.abs(value), axis=0, keepdims=True), 1e-30)
    exponent = jnp.ceil(jnp.log2(top) * STEPS)
    code = jnp.round(value * (jnp.exp2(exponent * (-1.0 / STEPS)) * TOP))
    return code.astype(jnp.int32).astype(I16), exponent


def scales(exponent):
    return jnp.exp2(exponent.astype(jnp.int32).astype(F32) * (1.0 / STEPS)) * (1.0 / TOP)


def rows_kernel(slabs, chunks, me_ref, x_ref, lead_ref, trail_ref, turn_ref, *rest):
    outs, (stack, marks, high, low) = rest[: slabs * chunks], rest[slabs * chunks:]
    step, last = pl.program_id(0), pl.num_programs(0) - 1
    short = turn_ref.shape[1]
    halves, tile = short // LANES, high.shape[0] // RADIX
    rows = (outs[0].shape[0] - RADIX) // 2
    width = outs[0].shape[1]
    stride = 2 * RADIX * halves
    for start in range(0, tile, SUB):
        for half in range(halves):
            values = []
            for n1 in range(RADIX):
                at = start * stride + (n1 * halves + half) * 2
                values.append(
                    tuple(x_ref[pl.ds(at + part, SUB, stride=stride), :] for part in range(2))
                )
            mixed = dft8(values, -1)
            for k1 in range(RADIX):
                lanes = slice(half * LANES, (half + 1) * LANES)
                pair = mixed[k1]
                if k1:
                    pair = spin(
                        pair, turn_ref[k1:k1 + 1, lanes], turn_ref[RADIX + k1:RADIX + k1 + 1, lanes]
                    )
                for part in range(2):
                    at = part * short + half * LANES
                    lead, trail = split(pair[part])
                    high[k1 * tile + start:k1 * tile + start + SUB, at:at + LANES] = lead
                    low[k1 * tile + start:k1 * tile + start + SUB, at:at + LANES] = trail
    spectrum = (
        dot(high[...], lead_ref[...]) + dot(low[...], lead_ref[...]) + dot(high[...], trail_ref[...])
    )
    own = short * RADIX // slabs
    for slab in range(slabs):
        k1, base = slab * own // short, slab * own % short
        for chunk in range(chunks):
            for part in range(2):
                at = part * short + base + chunk * width
                code, exponent = encode(
                    spectrum[k1 * tile:(k1 + 1) * tile, at:at + width]
                )
                place = pl.multiple_of(part * rows + step * tile, SUB)
                stack[chunk, slab, pl.ds(place, tile), :] = code
                marks[chunk, slab, pl.ds(2 * step + part, 1), :] = exponent

    @pl.when(step == last)
    def _():
        for chunk in range(chunks):
            for hop in range(slabs):
                slab = me_ref[0] ^ hop
                out = outs[chunk * slabs + hop]
                out[:2 * rows, :] = stack[chunk, slab]
                out[2 * rows:, :] = marks[chunk, slab].astype(jnp.int32).astype(I16)


def columns_kernel(slabs, chunk, length, me_ref, corr_ref, *rest):
    ins, rest = rest[:slabs], rest[slabs:]
    back_lead, back_trail, lead, trail, turn_ref = rest[:5]
    outs, (stack, scale, field, high, low) = rest[5:5 + slabs], rest[5 + slabs:]
    me = me_ref[0]
    short = length // RADIX
    rows = stack.shape[1] // 2
    width = stack.shape[2]
    tile = min(TILE, rows)
    group = high.shape[2] // width
    for hop in range(slabs):
        stack[me ^ hop] = ins[hop][:2 * rows, :]
        scale[me ^ hop] = scales(ins[hop][2 * rows:, :])
    for start in range(0, short, SUB):
        values = []
        for n1 in range(RADIX):
            slab, row = divmod(n1 * short + start, rows)
            mark = 2 * (row // tile)
            values.append(
                tuple(
                    stack[slab, part * rows + row:part * rows + row + SUB, :].astype(jnp.int32).astype(F32)
                    * scale[slab, mark + part:mark + part + 1, :]
                    for part in range(2)
                )
            )
        mixed = dft8(values, -1)
        for k1 in range(RADIX):
            pair = mixed[k1]
            if k1:
                pair = spin(
                    pair,
                    turn_ref[start:start + SUB, k1:k1 + 1],
                    turn_ref[start:start + SUB, RADIX + k1:RADIX + k1 + 1],
                )
            at = (k1 % group) * width
            for part in range(2):
                one, two = split(pair[part])
                place = slice(part * short + start, part * short + start + SUB)
                high[k1 // group, place, at:at + width] = one
                low[k1 // group, place, at:at + width] = two
    place = me * (length // slabs) + chunk * width
    lane = place + lax.broadcasted_iota(jnp.int32, (1, width), 1)
    wave_x = (lane // short) + RADIX * (lane % short)
    wave_x = jnp.where(wave_x < length // 2, wave_x, wave_x - length).astype(F32)
    unit = 2.0 * math.pi / length
    across = (corr_ref[1] * (wave_x * unit)) ** 2 + 1.0
    count = lax.broadcasted_iota(jnp.int32, (short, 1), 0)
    for pair_at in range(RADIX // group):
        one, two = high[pair_at], low[pair_at]
        spectrum = dot(lead[...], one) + dot(lead[...], two) + dot(trail[...], one)
        for slot in range(group):
            k1 = pair_at * group + slot
            wave_y = k1 + RADIX * count
            wave_y = jnp.where(wave_y < length // 2, wave_y, wave_y - length).astype(F32)
            down = (corr_ref[0] * (wave_y * unit)) ** 2
            root = lax.rsqrt(down + across)
            shape = root * root * lax.rsqrt(root)
            lanes = slice(slot * width, (slot + 1) * width)
            for part in range(2):
                place = slice(part * short, (part + 1) * short)
                one, two = split(spectrum[place, lanes] * shape)
                high[pair_at, place, lanes] = one
                low[pair_at, place, lanes] = two
        one, two = high[pair_at], low[pair_at]
        spectrum = (
            dot(back_lead[...], one) + dot(back_lead[...], two) + dot(back_trail[...], one)
        )
        for slot in range(group):
            k1 = pair_at * group + slot
            lanes = slice(slot * width, (slot + 1) * width)
            pair = (spectrum[:short, lanes], spectrum[short:, lanes])
            if k1:
                pair = spin(
                    pair, turn_ref[:, k1:k1 + 1], -turn_ref[:, RADIX + k1:RADIX + k1 + 1]
                )
            for part in range(2):
                field[part, k1 * short:(k1 + 1) * short, :] = pair[part]
    for start in range(0, short, SUB):
        values = [
            tuple(
                field[part, k1 * short + start:k1 * short + start + SUB, :] for part in range(2)
            )
            for k1 in range(RADIX)
        ]
        mixed = dft8(values, 1)
        for n1 in range(RADIX):
            for part in range(2):
                field[part, n1 * short + start:n1 * short + start + SUB, :] = mixed[n1][part]
    for slab in range(slabs):
        for at in range(rows // tile):
            for part in range(2):
                begin = slab * rows + at * tile
                code, exponent = encode(field[part, begin:begin + tile, :])
                stack[slab, part * rows + at * tile:part * rows + (at + 1) * tile, :] = code
                scale[slab, 2 * at + part:2 * at + part + 1, :] = exponent
    for hop in range(slabs):
        outs[hop][:2 * rows, :] = stack[me ^ hop]
        outs[hop][2 * rows:, :] = scale[me ^ hop].astype(jnp.int32).astype(I16)


def finish_kernel(slabs, chunks, me_ref, gain_ref, *rest):
    ins, rest = rest[:slabs * chunks], rest[slabs * chunks:]
    lead_ref, trail_ref, turn_ref, prints_ref, index_ref, out_ref, value_ref = rest[:7]
    stack, scale, high, low, field, blocks = rest[7:]
    step, last = pl.program_id(0), pl.num_programs(0) - 1
    short = turn_ref.shape[1]
    halves, tile = short // LANES, high.shape[0] // RADIX
    rows = stack.shape[2] // 2
    width = stack.shape[3]
    stride = 2 * RADIX * halves

    @pl.when(step == 0)
    def _():
        for chunk in range(chunks):
            for hop in range(slabs):
                slab = me_ref[0] ^ hop
                stack[chunk, slab] = ins[chunk * slabs + hop][:2 * rows, :]
                scale[chunk, slab] = scales(ins[chunk * slabs + hop][2 * rows:, :])

    own = short * RADIX // slabs
    for slab in range(slabs):
        k1, base = slab * own // short, slab * own % short
        for chunk in range(chunks):
            for part in range(2):
                place = pl.multiple_of(part * rows + step * tile, SUB)
                value = (
                    stack[chunk, slab, pl.ds(place, tile), :].astype(jnp.int32).astype(F32)
                    * scale[chunk, slab, pl.ds(2 * step + part, 1), :]
                )
                at = part * short + base + chunk * width
                one, two = split(value)
                high[k1 * tile:(k1 + 1) * tile, at:at + width] = one
                low[k1 * tile:(k1 + 1) * tile, at:at + width] = two
    mixed = (
        dot(high[...], lead_ref[...]) + dot(low[...], lead_ref[...]) + dot(high[...], trail_ref[...])
    )
    gain = gain_ref[0]
    for start in range(0, tile, SUB):
        for half in range(halves):
            lanes = slice(half * LANES, (half + 1) * LANES)
            values = []
            for k1 in range(RADIX):
                place = slice(k1 * tile + start, k1 * tile + start + SUB)
                at = half * LANES
                pair = (mixed[place, at:at + LANES], mixed[place, short + at:short + at + LANES])
                if k1:
                    pair = spin(
                        pair, turn_ref[k1:k1 + 1, lanes], -turn_ref[RADIX + k1:RADIX + k1 + 1, lanes]
                    )
                values.append(pair)
            done = dft8(values, 1)
            for n1 in range(RADIX):
                column = n1 * halves + half
                for part in range(2):
                    value = done[n1][part] * gain
                    out_ref[pl.ds(start * stride + column * 2 + part, SUB, stride=stride), :] = value
                    place = pl.multiple_of(step * tile + start, SUB)
                    field[part * RADIX * halves + column, pl.ds(place, SUB), :] = value

    @pl.when(step == last)
    def _():
        band_rows = prints_ref.shape[0] // LANES
        bands = field.shape[1] // band_rows
        count = field.shape[0]
        for column in range(count):
            for row in range(band_rows):
                piece = field[column, pl.ds(row, bands, stride=band_rows), :]
                blocks[column * bands:(column + 1) * bands, row * LANES:(row + 1) * LANES] = (
                    piece.astype(BF16)
                )
        values = dot(blocks[...], prints_ref[...])
        each = count // 2 * bands
        chosen = lax.broadcasted_iota(jnp.int32, (each, 1), 0) == index_ref[...]
        for part in range(2):
            value_ref[part:part + 1, :] = jnp.sum(
                jnp.where(chosen, values[part * each:(part + 1) * each, :], 0.0), axis=0, keepdims=True
            )


def pack_kernel(source_ref, prints_ref, out_ref, semaphore):
    out_ref[...] = jnp.zeros_like(out_ref)
    count = out_ref.shape[0]

    def begin(at, carry):
        @pl.when(source_ref[at] >= 0)
        def _():
            pltpu.make_async_copy(
                prints_ref.at[source_ref[at]], out_ref.at[at], semaphore
            ).start()
        return carry

    def end(at, carry):
        @pl.when(source_ref[at] >= 0)
        def _():
            pltpu.make_async_copy(
                prints_ref.at[source_ref[at]], out_ref.at[at], semaphore
            ).wait()
        return carry

    lax.fori_loop(0, count, begin, 0)
    lax.fori_loop(0, count, end, 0)


def small_kernel(slabs, lanes_q, each, total, row_ref, all_ref, pick_ref, sketch_ref, factor_ref, basis_ref, own):
    probes = lanes_q * each
    tiles = all_ref.shape[1] // each
    gram = {}
    for one in range(probes):
        for two in range(one + 1):
            sum_here = None
            for slab in range(slabs):
                left = all_ref[slab * lanes_q + one // each, (one % each) * tiles:(one % each + 1) * tiles, :]
                right = all_ref[slab * lanes_q + two // each, (two % each) * tiles:(two % each + 1) * tiles, :]
                term = left * right
                sum_here = term if sum_here is None else sum_here + term
            sum_here = jnp.sum(jnp.sum(sum_here, axis=0, keepdims=True), axis=1, keepdims=True)
            gram[one, two] = sum_here * (1.0 / total)
    lower, inverse = {}, {}
    for at in range(probes):
        left = gram[at, at]
        for back in range(at):
            left = left - lower[at, back] * lower[at, back]
        root = jnp.sqrt(left)
        lower[at, at] = root
        inverse[at] = 1.0 / root
        for down in range(at + 1, probes):
            value = gram[down, at]
            for back in range(at):
                value = value - lower[down, back] * lower[at, back]
            lower[down, at] = value * inverse[at]
    row = lax.broadcasted_iota(jnp.int32, (probes, probes), 0)
    column = lax.broadcasted_iota(jnp.int32, (probes, probes), 1)
    factor = jnp.zeros((probes, probes), F32)
    for one in range(probes):
        for two in range(one + 1):
            factor = jnp.where((row == two) & (column == one), lower[one, two], factor)
    factor_ref[...] = factor
    for slab in range(slabs):
        for one in range(probes):
            own[one:one + 1, slab * LANES:(slab + 1) * LANES] = all_ref[
                slab * lanes_q + one // each, pl.ds((one % each) * tiles + row_ref[0], 1), :
            ]
    value = own[...]
    first = value.astype(BF16)
    rest = value - first.astype(F32)
    second = rest.astype(BF16)
    third = (rest - second.astype(F32)).astype(BF16)
    sketch = dot(first, pick_ref[...]) + dot(second, pick_ref[...]) + dot(third, pick_ref[...])
    sketch_ref[...] = sketch
    solved = []
    for at in range(probes):
        value = sketch[at:at + 1, :]
        for back in range(at):
            value = value - lower[at, back] * solved[back]
        solved.append(value * inverse[at])
        basis_ref[at:at + 1, :] = solved[at]


def vmem():
    return pl.BlockSpec(memory_space=pltpu.VMEM)


def smem():
    return pl.BlockSpec(memory_space=pltpu.SMEM)


def params():
    return pltpu.CompilerParams(vmem_limit_bytes=56 << 20)


def filter_power(corr_lengths, height, width):
    wave_y = jnp.arange(height // 2 + 1, dtype=jnp.int32)
    wave_x = jnp.arange(width // 2 + 1, dtype=jnp.int32)
    weight_y = jnp.where((wave_y == 0) | (wave_y == height // 2), 1.0, 2.0)
    weight_x = jnp.where((wave_x == 0) | (wave_x == width // 2), 1.0, 2.0)
    down = (corr_lengths[0] * (wave_y.astype(F32) * (2.0 * math.pi / height))) ** 2
    across = (corr_lengths[1] * (wave_x.astype(F32) * (2.0 * math.pi / width))) ** 2
    root = lax.rsqrt(1.0 + down[:, None] + across[None, :])
    return jnp.sum(root * root * root * (weight_y[:, None] * weight_x[None, :]))


def exchange(blocks):
    slabs = len(blocks)
    order = sorted(range(1, slabs), key=lambda hop: (-(hop * 2 // slabs), -(hop * 4 // slabs % 2)))
    arrived = [blocks[0]] + [None] * (slabs - 1)
    for hop in order:
        pairs = [(source, source ^ hop) for source in range(slabs)]
        arrived[hop] = lax.ppermute(blocks[hop], "grid", pairs)
    return arrived


def local(probes, corr_lengths, footprints, reading_slab, reading_band, reading_tile):
    rows, each, width = probes.shape
    slabs, lanes_q = lax.axis_size("grid"), lax.axis_size("probe")
    me, lane_at = lax.axis_index("grid"), lax.axis_index("probe")
    height = rows * slabs
    short = width // RADIX
    own = width // slabs
    cut = min(LANES, own)
    chunks = own // cut
    tile = min(TILE, rows)
    halves = short // LANES
    lead, trail, back_lead, back_trail = (jnp.asarray(part) for part in dft_blocks(short))
    turn_x = jnp.asarray(twiddles(width))
    turn_y = jnp.asarray(twiddles(height).T.copy())
    me_list = me.reshape(1).astype(jnp.int32)
    column_tiles = width // LANES
    flat = (
        probes.reshape(rows, each, column_tiles, LANES)
        .transpose(0, 2, 1, 3)
        .reshape(rows * each * column_tiles, LANES)
    )
    payload = jax.ShapeDtypeStruct((2 * rows + RADIX, cut), I16)

    def whole(shape):
        return pl.BlockSpec(shape, lambda step: (0,) * len(shape))

    sent = pl.pallas_call(
        lambda *refs: rows_kernel(slabs, chunks, *refs),
        grid=(rows // tile,),
        in_specs=[
            smem(),
            pl.BlockSpec((tile * each * column_tiles, LANES), lambda step: (step, 0)),
            whole(lead.shape),
            whole(trail.shape),
            whole(turn_x.shape),
        ],
        out_specs=[whole(payload.shape)] * (chunks * slabs),
        out_shape=[payload] * (chunks * slabs),
        scratch_shapes=[
            pltpu.VMEM((chunks, slabs, 2 * rows, cut), I16),
            pltpu.VMEM((chunks, slabs, RADIX, cut), F32),
            pltpu.VMEM((RADIX * tile, 2 * short), BF16),
            pltpu.VMEM((RADIX * tile, 2 * short), BF16),
        ],
        compiler_params=params(),
        name="rows_forward",
    )(me_list, flat, lead, trail, turn_x)

    arrived = []
    for chunk in range(chunks):
        arrived.append(exchange(sent[chunk * slabs:(chunk + 1) * slabs]))

    read_count, band_rows, tile_cols = footprints.shape
    band_count = rows // band_rows
    tile_count = width // tile_cols
    capacity = 2 * read_count // slabs
    share = capacity // lanes_q
    target = reading_slab[:, 0]
    reading = jnp.arange(read_count, dtype=jnp.int32)
    onehot = (target[:, None] == jnp.arange(slabs, dtype=jnp.int32)[None, :]).astype(F32)
    before = (reading[:, None] > reading[None, :]).astype(F32)
    slot = jnp.sum(jnp.dot(before, onehot) * onehot, axis=1).astype(jnp.int32)
    place = target * capacity + slot
    code = reading_tile * band_count + reading_band
    wanted = (
        jnp.arange(slabs, dtype=jnp.int32)[:, None] * capacity
        + lane_at * share
        + jnp.arange(share, dtype=jnp.int32)[None, :]
    ).reshape(-1)
    source = jnp.max(
        jnp.where(wanted[:, None] == place[None, :], reading[None, :], -1), axis=1
    )
    packed = pl.pallas_call(
        pack_kernel,
        in_specs=[smem(), pl.BlockSpec(memory_space=pl.ANY)],
        out_specs=vmem(),
        out_shape=jax.ShapeDtypeStruct((slabs * share, band_rows, tile_cols), BF16),
        scratch_shapes=[pltpu.SemaphoreType.DMA],
        compiler_params=params(),
        name="pack_prints",
    )(source, footprints)
    shared = lax.all_to_all(
        packed.reshape(slabs, share, band_rows, tile_cols), "grid", split_axis=0, concat_axis=0, tiled=True
    )
    prints = lax.all_gather(shared, "probe", axis=0, tiled=False)
    slots = slabs * capacity
    prints = prints.transpose(3, 4, 1, 0, 2).reshape(band_rows * tile_cols, slots)
    listed = lax.all_gather(jnp.stack([place, code]), "grid", axis=0, tiled=False)
    here = me * capacity + jnp.arange(capacity, dtype=jnp.int32)
    index = jnp.max(
        jnp.where(here[None, :, None] == listed[:, 0, None, :], listed[:, 1, None, :], 0), axis=2
    ).reshape(1, slots)

    gain = lax.rsqrt(filter_power(corr_lengths, height, width) / (height * width)) / (height * width)

    returned = []
    group = 256 // cut if cut % LANES == 0 else 1
    for chunk in range(chunks):
        results = pl.pallas_call(
            lambda *refs, chunk=chunk: columns_kernel(slabs, chunk, height, *refs),
            in_specs=[smem(), smem()] + [vmem()] * (slabs + 5),
            out_specs=[vmem()] * slabs,
            out_shape=[payload] * slabs,
            scratch_shapes=[
                pltpu.VMEM((slabs, 2 * rows, cut), I16),
                pltpu.VMEM((slabs, RADIX, cut), F32),
                pltpu.VMEM((2, height, cut), F32),
                pltpu.VMEM((RADIX // group, 2 * short, group * cut), BF16),
                pltpu.VMEM((RADIX // group, 2 * short, group * cut), BF16),
            ],
            compiler_params=params(),
            name="columns",
        )(me_list, corr_lengths, *arrived[chunk], lead, trail, back_lead, back_trail, turn_y)
        returned += exchange(results)

    smoothed, values = pl.pallas_call(
        lambda *refs: finish_kernel(slabs, chunks, *refs),
        grid=(rows // tile,),
        in_specs=[smem(), smem()]
        + [whole(payload.shape)] * (chunks * slabs)
        + [
            whole(lead.shape),
            whole(trail.shape),
            whole(turn_x.shape),
            whole(prints.shape),
            whole(index.shape),
        ],
        out_specs=[
            pl.BlockSpec((tile * each * column_tiles, LANES), lambda step: (step, 0)),
            whole((each, slots)),
        ],
        out_shape=[
            jax.ShapeDtypeStruct(flat.shape, F32),
            jax.ShapeDtypeStruct((each, slots), F32),
        ],
        scratch_shapes=[
            pltpu.VMEM((chunks, slabs, 2 * rows, cut), I16),
            pltpu.VMEM((chunks, slabs, RADIX, cut), F32),
            pltpu.VMEM((RADIX * tile, 2 * short), BF16),
            pltpu.VMEM((RADIX * tile, 2 * short), BF16),
            pltpu.VMEM((each * column_tiles, rows, LANES), F32),
            pltpu.VMEM((each * column_tiles * band_count, band_rows * tile_cols), BF16),
        ],
        compiler_params=params(),
        name="rows_back",
    )(me_list, gain.reshape(1), *returned, back_lead, back_trail, turn_x, prints, index)
    smoothed = (
        smoothed.reshape(rows, column_tiles, each, LANES).transpose(0, 2, 1, 3).reshape(rows, each, width)
    )

    group_count = slabs * lanes_q
    spread = jnp.broadcast_to(
        values.reshape(1, each * slots // LANES, LANES), (group_count, each * slots // LANES, LANES)
    )
    everyone = lax.all_to_all(spread, ("grid", "probe"), split_axis=0, concat_axis=0, tiled=True)
    offset = me * capacity
    lane_of = target * LANES + offset % LANES + slot
    pick = (jnp.arange(slabs * LANES, dtype=jnp.int32)[:, None] == lane_of[None, :]).astype(BF16)
    probe_count = each * lanes_q
    full, factor, basis = pl.pallas_call(
        lambda *refs: small_kernel(slabs, lanes_q, each, read_count * slabs, *refs),
        in_specs=[smem(), vmem(), vmem()],
        out_specs=[vmem()] * 3,
        out_shape=[
            jax.ShapeDtypeStruct((probe_count, read_count), F32),
            jax.ShapeDtypeStruct((probe_count, probe_count), F32),
            jax.ShapeDtypeStruct((probe_count, read_count), F32),
        ],
        scratch_shapes=[pltpu.VMEM((probe_count, slabs * LANES), F32)],
        compiler_params=params(),
        name="factor_basis",
    )((offset // LANES).reshape(1), everyone, pick)
    sketch = lax.dynamic_slice_in_dim(full, lane_at * each, each, 0).T
    basis = lax.dynamic_slice_in_dim(basis, lane_at * each, each, 0).T
    return (smoothed, sketch, factor, basis)


def solution(mesh):
    in_specs = (
        P("grid", "probe", None),
        P(),
        P("grid", None, None),
        P("grid", None),
        P("grid"),
        P("grid"),
    )
    out_specs = (P("grid", "probe", None), P("grid", "probe"), P(), P("grid", "probe"))
    return jax.shard_map(local, mesh=mesh, in_specs=in_specs, out_specs=out_specs, check_vma=False)
```

time: 857 us -> 217 us (0.25); the launches traced: 842 us -> 216 us
  local copies, waits for them, and re-layouts: 309 us -> 12.5 us
  blocking collectives: 166 us -> 48.2 us
  waiting for transfers between devices: 136 us -> 28.9 us
  matrix products: 107 us -> 0.95 us
  other arithmetic: 57.4 us -> 5.65 us
  Pallas kernels: 0 us -> 47.6 us
  between operations: 3.32 us -> 16.5 us
    psum x1 -> x0, blocking collectives: 161 us -> none  [local(): power = lax.psum(jnp.sum(spectrum_shape * spectrum_shape), 'grid')]
    all_to_all x5 -> x1, waiting for transfers between devices: 133 us -> 7.18 us  [local(): lax.all_to_all(spread, ('grid', 'probe'), split_axis=0, concat_axis=0, ti...]
    dot_general x16 -> x1, matrix products: 107 us -> 0.95 us  [local(): slot = jnp.sum(jnp.dot(before, onehot) * onehot, axis=1).astype(jnp.int32)]
    scatter x2 -> x0, local copies, waits for them, and re-layouts: 84 us -> none  [the longest x1 45.4 us: local(): send_prints = jnp.zeros((slab_count, capacity, band_rows * tile_cols), jn...]
    another operation x13 -> x0, local copies, waits for them, and re-layouts: 74.2 us -> none  [the longest x3 28.7 us: local(): jnp.stack([spec_real.reshape(slab_rows, per_dev, width), spec_imag.reshap...]
    all_to_all x5 -> x1, starting transfers between devices: 55.7 us -> 5.47 us  [local(): lax.all_to_all(spread, ('grid', 'probe'), split_axis=0, concat_axis=0, ti...]
    pallas_call x0 -> x6, Pallas kernels: none -> 47.6 us  [the longest x2 17.9 us: local(): pl.pallas_call(lambda *refs, chunk=chunk: columns_kernel(slabs, chunk, he...]
    slice x11 -> x2, local copies, waits for them, and re-layouts: 45.7 us -> 0.6 us  [the longest x1 0.58 us: filter_power(): corr_lengths[0] * (wave_y.astype(F32) * (2.0 * math.pi / height))]
  transfers between devices with their start and end apart: 8 -> 30, of which waited for: 4 -> 8; matrix products, arithmetic and copies ran while one was open for 41% -> 5% of each run, Pallas kernels for 0% -> 13%
where the time goes in v1:
time: 217 us; the launch traced here: 216 us
  starting transfers between devices  55.8 us (26%)
  blocking collectives  48.2 us (22%)
  Pallas kernels  47.6 us (22%)
  waiting for transfers between devices  28.9 us (13%)
  between operations  16.5 us (8%)
  local copies, waits for them, and re-layouts  12.5 us (6%)
  other arithmetic  5.65 us (3%)
    ppermute x28, starting transfers between devices, exchange(): arrived[hop] = lax.ppermute(blocks[hop], 'grid', pairs)  50.2 us
    all_gather x1, blocking collectives, local(): lax.all_gather(jnp.stack([place, code]), 'grid', axis=0, tiled=False)  26.2 us
    all_to_all x1, blocking collectives, local(): lax.all_to_all(packed.reshape(slabs, share, band_rows, tile_cols), 'grid'...  22.1 us
    ppermute x28, waiting for transfers between devices, exchange(): arrived[hop] = lax.ppermute(blocks[hop], 'grid', pairs)  21.7 us
    pallas_call x2, Pallas kernels, local(): pl.pallas_call(lambda *refs, chunk=chunk: columns_kernel(slabs, chunk, he...  17.9 us
    pallas_call x1, Pallas kernels, local(): pl.pallas_call(lambda *refs: finish_kernel(slabs, chunks, *refs), grid=(r...  12.9 us
    pallas_call x1, Pallas kernels, local(): pl.pallas_call(lambda *refs: rows_kernel(slabs, chunks, *refs), grid=(row...  10.5 us
    all_to_all x1, waiting for transfers between devices, local(): lax.all_to_all(spread, ('grid', 'probe'), split_axis=0, concat_axis=0, ti...  7.18 us
  transfers between devices with their start and end apart: 30, of which 8 were waited for; matrix products, arithmetic and copies ran while one was open for 5% of the time, Pallas kernels for 13%

profile of v1, /device:TPU:0, one launch (start us, length us, event | category | flops | bytes accessed | tf_op | source)
XLA Modules:
  0.0 216.1 jit_solution(7800751667963953371)
XLA Ops:
  7.2 0.0 all-gather.5.cloned.1.call-start
  7.2 0.9 fusion.2
  8.2 0.1 iota_add_fusion
  8.3 0.1 add.117
  8.3 0.7 add_add_fusion
  9.0 0.7 select_reduce_fusion.1.source_ref
  9.7 4.4 %pack_prints.1 = bf16[128,16,128]{2,1,0:T(8,128)(2,1)} custom-call(s32[128]{0:T(128)} %select_reduce_fusion.1.source_ref, bf16[256,16,128]{2,1,0:T(8,128)(2,1)} %prints_ref.1), custom_call_target="tpu_custom_call" | custom-call | tf_op jit(solution)/shard_map/pack_prints/pallas_call | solution.py:511
  14.1 0.0 copy-start.27
  14.1 0.0 copy-start.28
  14.1 22.1 %all_to_all.10 = bf16[8,16,16,128]{3,2,1,0:T(8,128)(2,1)} all-to-all(bf16[8,16,16,128]{3,2,1,0:T(8,128)(2,1)} %bitcast.45), channel_id=1, replica_groups=mesh['grid'=8,'probe'=4] {'grid'}, dimensions={0} | all-to-all | bytes 1048576 | tf_op jit(solution)/shard_map/all_to_all | solution.py:520
  36.2 0.0 all-gather.5.cloned.1.call-update
  36.2 10.5 %rows_forward.1 = (s16[520,128]{1,0:T(8,128)(2,1)}, s16[520,128]{1,0:T(8,128)(2,1)}, s16[520,128]{1,0:T(8,128)(2,1)}, s16[520,128]{1,0:T(8,128)(2,1)}, s16[520,1...) custom-call(s32[1]{0:T(128)} %bitcast.refs_0_, ...), custom_call_target="tpu_custom_call" | custom-call | tf_op jit(solution)/shard_map/rows_forward/pallas_call | solution.py:465
  46.7 1.5 collective-permute-start.14
  48.2 2.0 collective-permute-start.16
  50.2 1.1 collective-permute-start.17
  51.3 2.8 %collective-permute-start.18 = (s16[520,128]{1,0:T(8,128)(2,1)}, s16[520,128]{1,0:T(8,128)(2,1)S(1)}, u32[]{:S(2)}, u32[]{:S(2)}) collective-permute-start(s16[520,128]{1,0:T(8,128)(2,1)} %get-tuple-element.62), channel_id=1, source_target_pairs={{0,20},{4,16},{8,28},{12,24},{16,4},{20,0},{24,12},{28,8},{1,21},{... | collective-permute-start | bytes 399368 | tf_op jit(solution)/shard_map/ppermute | solution.py:435
  54.1 0.6 fusion.8
  56.0 2.9 %fusion.1 = f32[]{:T(128)} fusion(f32[1025]{0:T(1024)S(1)} %fusion.5, f32[1025]{0:T(1024)S(1)} %get-tuple-element.84, f32[1025]{0:T(1024)S(1)} %get-tuple-element.85), kind=kLoop, calls=%fused_computation.2 | loop fusion | flops 6303749 | bytes 12304 | tf_op jit(solution)/shard_map/reduce_sum | solution.py:426
  58.8 1.5 collective-permute-start.19
  60.3 2.4 %collective-permute-start.20 = (s16[520,128]{1,0:T(8,128)(2,1)}, s16[520,128]{1,0:T(8,128)(2,1)S(1)}, u32[]{:S(2)}, u32[]{:S(2)}) collective-permute-start(s16[520,128]{1,0:T(8,128)(2,1)} %get-tuple-element.64), channel_id=1, source_target_pairs={{0,28},{4,24},{8,20},{12,16},{16,12},{20,8},{24,4},{28,0},{1,29},{... | collective-permute-start | bytes 399368 | tf_op jit(solution)/shard_map/ppermute | solution.py:435
  62.7 1.5 collective-permute-start
  64.2 2.0 collective-permute-done.17.refs_6_
  66.2 5.4 %collective-permute-done.18.refs_7_ = s16[520,128]{1,0:T(8,128)(2,1)S(1)} collective-permute-done((s16[520,128]{1,0:T(8,128)(2,1)}, s16[520,128]{1,0:T(8,128)(2,1)S(1)}, u32[]{:S(2)}, u32[]{:S(2)}) %collective-permute-start.18) | collective-permute-done | bytes 133152 | tf_op jit(solution)/shard_map/ppermute | solution.py:435
  71.7 3.0 %collective-permute-start.3 = (s16[520,128]{1,0:T(8,128)(2,1)}, s16[520,128]{1,0:T(8,128)(2,1)S(1)}, u32[]{:S(2)}, u32[]{:S(2)}) collective-permute-start(s16[520,128]{1,0:T(8,128)(2,1)} %get-tuple-element.45), channel_id=1, source_target_pairs={{0,16},{4,20},{8,24},{12,28},{16,0},{20,4},{24,8},{28,12},{1,17},{... | collective-permute-start | bytes 399368 | tf_op jit(solution)/shard_map/ppermute | solution.py:435
  74.7 9.5 %collective-permute-start.4 = (s16[520,128]{1,0:T(8,128)(2,1)}, s16[520,128]{1,0:T(8,128)(2,1)S(1)}, u32[]{:S(2)}, u32[]{:S(2)}) collective-permute-start(s16[520,128]{1,0:T(8,128)(2,1)} %get-tuple-element.46), channel_id=1, source_target_pairs={{0,20},{4,16},{8,28},{12,24},{16,4},{20,0},{24,12},{28,8},{1,21},{... | collective-permute-start | bytes 399368 | tf_op jit(solution)/shard_map/ppermute | solution.py:435
  84.2 2.2 %collective-permute-start.5 = (s16[520,128]{1,0:T(8,128)(2,1)}, s16[520,128]{1,0:T(8,128)(2,1)S(1)}, u32[]{:S(2)}, u32[]{:S(2)}) collective-permute-start(s16[520,128]{1,0:T(8,128)(2,1)} %get-tuple-element.47), channel_id=1, source_target_pairs={{0,24},{4,28},{8,16},{12,20},{16,8},{20,12},{24,0},{28,4},{1,25},{... | collective-permute-start | bytes 399368 | tf_op jit(solution)/shard_map/ppermute | solution.py:435
  86.4 26.2 %all-gather.2 = s32[8,2,256]{2,1,0:T(2,128)S(1)} all-gather(s32[1,2,256]{2,1,0:T(2,128)S(1)} %add_bitcast_fusion), channel_id=3, replica_groups=mesh['grid'=8,'probe'=4] {'grid'}, dimensions={0}, use_global_device_ids=true | all-gather | bytes 18432 | tf_op jit(solution)/shard_map/all_gather | solution.py:526
  112.6 8.9 %columns.3 = (s16[520,128]{1,0:T(8,128)(2,1)}, s16[520,128]{1,0:T(8,128)(2,1)}, s16[520,128]{1,0:T(8,128)(2,1)}, s16[520,128]{1,0:T(8,128)(2,1)}, s16[520,128]{1...) custom-call(s32[1]{0:T(128)} %bitcast.refs_0_, f32[2]{0:T(128)} %refs_1_.3, ...), custom_call_target="tpu_custom_call" | custom-call | tf_op jit(solution)/shard_map/columns/pallas_call | solution.py:537
  121.5 1.3 collective-permute-start.6
  122.8 0.7 collective-permute-start.22
  123.6 2.7 %collective-permute-start.23 = (s16[520,128]{1,0:T(8,128)(2,1)}, s16[520,128]{1,0:T(8,128)(2,1)S(1)}, u32[]{:S(2)}, u32[]{:S(2)}) collective-permute-start(s16[520,128]{1,0:T(8,128)(2,1)} %get-tuple-element.68), channel_id=1, source_target_pairs={{0,12},{4,8},{8,4},{12,0},{16,28},{20,24},{24,20},{28,16},{1,13},{... | collective-permute-start | bytes 399368 | tf_op jit(solution)/shard_map/ppermute | solution.py:435
  126.3 1.3 collective-permute-start.24
  127.6 1.8 collective-permute-done.6.refs_9_
  129.5 0.6 copy-done.24
  130.1 8.9 %columns.2 = (s16[520,128]{1,0:T(8,128)(2,1)}, s16[520,128]{1,0:T(8,128)(2,1)}, s16[520,128]{1,0:T(8,128)(2,1)}, s16[520,128]{1,0:T(8,128)(2,1)}, s16[520,128]{1...) custom-call(s32[1]{0:T(128)} %bitcast.refs_0_, f32[2]{0:T(128)} %refs_1_.3, ...), custom_call_target="tpu_custom_call" | custom-call | tf_op jit(solution)/shard_map/columns/pallas_call | solution.py:537
  139.0 2.9 %collective-permute-start.26 = (s16[520,128]{1,0:T(8,128)(2,1)}, s16[520,128]{1,0:T(8,128)(2,1)S(1)}, u32[]{:S(2)}, u32[]{:S(2)}) collective-permute-start(s16[520,128]{1,0:T(8,128)(2,1)} %get-tuple-element.71), channel_id=1, source_target_pairs={{0,24},{4,28},{8,16},{12,20},{16,8},{20,12},{24,0},{28,4},{1,25},{... | collective-permute-start | bytes 399368 | tf_op jit(solution)/shard_map/ppermute | solution.py:435
  142.0 1.2 collective-permute-start.27
  143.1 1.2 collective-permute-start.10
  144.4 1.9 collective-permute-done.24.refs_14_
  146.3 0.5 collective-permute-start.11
  146.8 1.8 collective-permute-done.25.refs_15_
  148.5 8.4 %collective-permute-start.12 = (s16[520,128]{1,0:T(8,128)(2,1)}, s16[520,128]{1,0:T(8,128)(2,1)S(1)}, u32[]{:S(2)}, u32[]{:S(2)}) collective-permute-start(s16[520,128]{1,0:T(8,128)(2,1)} %get-tuple-element.55), channel_id=1, source_target_pairs={{0,24},{4,28},{8,16},{12,20},{16,8},{20,12},{24,0},{28,4},{1,25},{... | collective-permute-start | bytes 399368 | tf_op jit(solution)/shard_map/ppermute | solution.py:435
  156.9 1.2 collective-permute-start.13
  158.2 0.3 collective-permute-start.7
  158.5 6.3 %collective-permute-done.10.refs_6_ = s16[520,128]{1,0:T(8,128)(2,1)S(1)} collective-permute-done((s16[520,128]{1,0:T(8,128)(2,1)}, s16[520,128]{1,0:T(8,128)(2,1)S(1)}, u32[]{:S(2)}, u32[]{:S(2)}) %collective-permute-start.10) | collective-permute-done | bytes 133152 | tf_op jit(solution)/shard_map/ppermute | solution.py:435
  164.8 2.3 %collective-permute-done.11.refs_7_ = s16[520,128]{1,0:T(8,128)(2,1)S(1)} collective-permute-done((s16[520,128]{1,0:T(8,128)(2,1)}, s16[520,128]{1,0:T(8,128)(2,1)S(1)}, u32[]{:S(2)}, u32[]{:S(2)}) %collective-permute-start.11) | collective-permute-done | bytes 133152 | tf_op jit(solution)/shard_map/ppermute | solution.py:435
  167.2 1.1 collective-permute-start.9
  168.3 0.3 select_reduce_fusion
  168.6 0.7 reshape.138.refs_22_
  169.9 0.0 all-gather.5.cloned.1.call-done
  170.0 2.2 %copy.27 = bf16[16,128,8,4,16]{1,0,4,3,2:T(8,128)(2,1)S(1)} copy(bf16[16,128,8,4,16]{1,0,4,2,3:T(8,128)(2,1)} %bitcast.44) | data formatting | bytes 4194304 | tf_op jit(solution)/shard_map/transpose | solution.py:525
  172.1 0.5 copy.36
  172.8 2.6 %copy.28.refs_21_ = bf16[2048,512]{1,0:T(8,128)(2,1)} copy(bf16[2048,512]{0,1:T(8,128)(2,1)S(1)} %bitcast.42) | data formatting | bytes 4194304 | tf_op jit(solution)/shard_map/reshape | solution.py:525
  175.4 0.6 copy-done.20
  176.0 12.9 %rows_back.1 = (f32[8192,128]{1,0:T(8,128)}, f32[2,512]{1,0:T(2,128)}) custom-call(s32[1]{0:T(128)} %bitcast.refs_0_, f32[1]{0:T(128)} %bitcast.3.refs_1_, s16[520,128]{1,0:T(8,128)(2,1)} %get-tuple-element.49.refs_2_, s16[520,128]{1,0:T(8,128)(2,1)} %collective-permute-done.7.refs_3_, s16[520,128]{1,0:T(8,128)(2,1)} %collective-permute-done.8.refs_4_, ...), custom_call_target="tpu_custom_call" | custom-call | tf_op jit(solution)/shard_map/rows_back/pallas_call | solution.py:554
  188.9 0.7 broadcast_in_dim.61
  189.6 0.7 broadcast_in_dim.62
  190.2 5.5 %all-to-all-start.1 = ((f32[32,8,128]{2,1,0:T(8,128)}), f32[32,8,128]{2,1,0:T(8,128)S(1)}, u32[]{:S(2)}, u32[]{:S(2)}) async-start(f32[32,8,128]{2,1,0:T(8,128)} %broadcast_in_dim.62), calls=%async_computation.1 | async-start | bytes 262144 | tf_op jit(solution)/shard_map/all_to_all | solution.py:593
  195.7 1.0 fusion.3.refs_2_
  196.8 7.2 %all-to-all-done.1.refs_1_ = f32[32,8,128]{2,1,0:T(8,128)S(1)} async-done(((f32[32,8,128]{2,1,0:T(8,128)}), f32[32,8,128]{2,1,0:T(8,128)S(1)}, u32[]{:S(2)}, u32[]{:S(2)}) %all-to-all-start.1) | async-done | bytes 131104 | tf_op jit(solution)/shard_map/all_to_all | solution.py:593
  203.9 0.6 copy-done
  204.6 2.1 factor_basis.1
  206.7 1.3 dynamic-slice_bitcast_fusion
  207.9 1.3 dynamic-slice_bitcast_fusion.1
  (92 shorter events, 0.2 us)
Async XLA Ops:
  7.2 162.8 %all-gather.5.cloned.1.call-start = ((), (), s32[]{:S(2)}) async-start(), calls=%async_computation.2 | async-start | bytes 2621440 | tf_op jit(solution)/shard_map/all_gather | solution.py:523
  9.7 44.3 %copy-start.25 = (f32[2]{0:T(128)S(1)}, f32[2]{0:T(128)}, u32[]{:S(2)}) copy-start(f32[2]{0:T(128)} %refs_1_.3) | copy-start | bytes 28
  14.1 50.1 %copy-start.26 = (s32[256,1]{0,1:T(1,128)S(1)}, s32[256,1]{0,1:T(1,128)}, u32[]{:S(2)}) copy-start(s32[256,1]{0,1:T(1,128)} %param.15) | copy-start | bytes 3076
  14.1 72.2 %copy-start.27 = (s32[256]{0:T(256)S(1)}, s32[256]{0:T(256)}, u32[]{:S(2)}) copy-start(s32[256]{0:T(256)} %param.16) | copy-start | bytes 3076
  14.1 72.2 %copy-start.28 = (s32[256]{0:T(256)S(1)}, s32[256]{0:T(256)}, u32[]{:S(2)}) copy-start(s32[256]{0:T(256)} %param.17) | copy-start | bytes 3076
  46.7 74.9 %copy-start.29 = (s16[520,128]{1,0:T(8,128)(2,1)S(1)}, s16[520,128]{1,0:T(8,128)(2,1)}, u32[]{:S(2)}) copy-start(s16[520,128]{1,0:T(8,128)(2,1)} %get-tuple-element.48) | copy-start | bytes 399364
  46.7 12.1 %collective-permute-start.14 = (s16[520,128]{1,0:T(8,128)(2,1)}, s16[520,128]{1,0:T(8,128)(2,1)S(1)}, u32[]{:S(2)}, u32[]{:S(2)}) collective-permute-start(s16[520,128]{1,0:T(8,128)(2,1)} %get-tuple-element.58), channel_id=1, source_target_pairs={{0,4},{4,0},{8,12},{12,8},{16,20},{20,16},{24,28},{28,24},{1,5},{5... | collective-permute-start | bytes 399368 | tf_op jit(solution)/shard_map/ppermute | solution.py:435
  48.2 12.1 %collective-permute-start.15 = (s16[520,128]{1,0:T(8,128)(2,1)}, s16[520,128]{1,0:T(8,128)(2,1)S(1)}, u32[]{:S(2)}, u32[]{:S(2)}) collective-permute-start(s16[520,128]{1,0:T(8,128)(2,1)} %get-tuple-element.59), channel_id=1, source_target_pairs={{0,8},{4,12},{8,0},{12,4},{16,24},{20,28},{24,16},{28,20},{1,9},{5... | collective-permute-start | bytes 399368 | tf_op jit(solution)/shard_map/ppermute | solution.py:435
  48.2 14.5 %collective-permute-start.16 = (s16[520,128]{1,0:T(8,128)(2,1)}, s16[520,128]{1,0:T(8,128)(2,1)S(1)}, u32[]{:S(2)}, u32[]{:S(2)}) collective-permute-start(s16[520,128]{1,0:T(8,128)(2,1)} %get-tuple-element.60), channel_id=1, source_target_pairs={{0,12},{4,8},{8,4},{12,0},{16,28},{20,24},{24,20},{28,16},{1,13},{... | collective-permute-start | bytes 399368 | tf_op jit(solution)/shard_map/ppermute | solution.py:435
  50.2 16.0 %collective-permute-start.17 = (s16[520,128]{1,0:T(8,128)(2,1)}, s16[520,128]{1,0:T(8,128)(2,1)S(1)}, u32[]{:S(2)}, u32[]{:S(2)}) collective-permute-start(s16[520,128]{1,0:T(8,128)(2,1)} %get-tuple-element.61), channel_id=1, source_target_pairs={{0,16},{4,20},{8,24},{12,28},{16,0},{20,4},{24,8},{28,12},{1,17},{... | collective-permute-start | bytes 399368 | tf_op jit(solution)/shard_map/ppermute | solution.py:435
  51.3 20.3 %collective-permute-start.18 = (s16[520,128]{1,0:T(8,128)(2,1)}, s16[520,128]{1,0:T(8,128)(2,1)S(1)}, u32[]{:S(2)}, u32[]{:S(2)}) collective-permute-start(s16[520,128]{1,0:T(8,128)(2,1)} %get-tuple-element.62), channel_id=1, source_target_pairs={{0,20},{4,16},{8,28},{12,24},{16,4},{20,0},{24,12},{28,8},{1,21},{... | collective-permute-start | bytes 399368 | tf_op jit(solution)/shard_map/ppermute | solution.py:435
  58.8 53.7 %copy-start.10 = (s16[520,128]{1,0:T(8,128)(2,1)}, s16[520,128]{1,0:T(8,128)(2,1)S(1)}, u32[]{:S(2)}) copy-start(s16[520,128]{1,0:T(8,128)(2,1)S(1)} %collective-permute-done.14.refs_3_) | copy-start | bytes 399364
  58.8 12.8 %collective-permute-start.19 = (s16[520,128]{1,0:T(8,128)(2,1)}, s16[520,128]{1,0:T(8,128)(2,1)S(1)}, u32[]{:S(2)}, u32[]{:S(2)}) collective-permute-start(s16[520,128]{1,0:T(8,128)(2,1)} %get-tuple-element.63), channel_id=1, source_target_pairs={{0,24},{4,28},{8,16},{12,20},{16,8},{20,12},{24,0},{28,4},{1,25},{... | collective-permute-start | bytes 399368 | tf_op jit(solution)/shard_map/ppermute | solution.py:435
  60.3 52.2 %copy-start.11 = (s16[520,128]{1,0:T(8,128)(2,1)}, s16[520,128]{1,0:T(8,128)(2,1)S(1)}, u32[]{:S(2)}) copy-start(s16[520,128]{1,0:T(8,128)(2,1)S(1)} %collective-permute-done.15.refs_4_) | copy-start | bytes 399364
  60.3 14.4 %collective-permute-start.20 = (s16[520,128]{1,0:T(8,128)(2,1)}, s16[520,128]{1,0:T(8,128)(2,1)S(1)}, u32[]{:S(2)}, u32[]{:S(2)}) collective-permute-start(s16[520,128]{1,0:T(8,128)(2,1)} %get-tuple-element.64), channel_id=1, source_target_pairs={{0,28},{4,24},{8,20},{12,16},{16,12},{20,8},{24,4},{28,0},{1,29},{... | collective-permute-start | bytes 399368 | tf_op jit(solution)/shard_map/ppermute | solution.py:435
  62.7 49.8 %copy-start.14 = (s16[520,128]{1,0:T(8,128)(2,1)}, s16[520,128]{1,0:T(8,128)(2,1)S(1)}, u32[]{:S(2)}) copy-start(s16[520,128]{1,0:T(8,128)(2,1)S(1)} %collective-permute-done.16.refs_5_) | copy-start | bytes 399364
  62.7 21.4 %collective-permute-start = (s16[520,128]{1,0:T(8,128)(2,1)}, s16[520,128]{1,0:T(8,128)(2,1)S(1)}, u32[]{:S(2)}, u32[]{:S(2)}) collective-permute-start(s16[520,128]{1,0:T(8,128)(2,1)} %get-tuple-element.42), channel_id=1, source_target_pairs={{0,4},{4,0},{8,12},{12,8},{16,20},{20,16},{24,28},{28,24},{1,5},{5... | collective-permute-start | bytes 399368 | tf_op jit(solution)/shard_map/ppermute | solution.py:435
  66.2 46.3 %copy-start.15 = (s16[520,128]{1,0:T(8,128)(2,1)}, s16[520,128]{1,0:T(8,128)(2,1)S(1)}, u32[]{:S(2)}) copy-start(s16[520,128]{1,0:T(8,128)(2,1)S(1)} %collective-permute-done.17.refs_6_) | copy-start | bytes 399364
  66.2 55.3 %collective-permute-start.1 = (s16[520,128]{1,0:T(8,128)(2,1)}, s16[520,128]{1,0:T(8,128)(2,1)S(1)}, u32[]{:S(2)}, u32[]{:S(2)}) collective-permute-start(s16[520,128]{1,0:T(8,128)(2,1)} %get-tuple-element.43), channel_id=1, source_target_pairs={{0,8},{4,12},{8,0},{12,4},{16,24},{20,28},{24,16},{28,20},{1,9},{5... | collective-permute-start | bytes 399368 | tf_op jit(solution)/shard_map/ppermute | solution.py:435
  71.7 40.9 %copy-start.17 = (s16[520,128]{1,0:T(8,128)(2,1)}, s16[520,128]{1,0:T(8,128)(2,1)S(1)}, u32[]{:S(2)}) copy-start(s16[520,128]{1,0:T(8,128)(2,1)S(1)} %collective-permute-done.18.refs_7_) | copy-start | bytes 399364
  71.7 51.1 %collective-permute-start.2 = (s16[520,128]{1,0:T(8,128)(2,1)}, s16[520,128]{1,0:T(8,128)(2,1)S(1)}, u32[]{:S(2)}, u32[]{:S(2)}) collective-permute-start(s16[520,128]{1,0:T(8,128)(2,1)} %get-tuple-element.44), channel_id=1, source_target_pairs={{0,12},{4,8},{8,4},{12,0},{16,28},{20,24},{24,20},{28,16},{1,13},{... | collective-permute-start | bytes 399368 | tf_op jit(solution)/shard_map/ppermute | solution.py:435
  71.7 40.9 %copy-start.22 = (s16[520,128]{1,0:T(8,128)(2,1)}, s16[520,128]{1,0:T(8,128)(2,1)S(1)}, u32[]{:S(2)}) copy-start(s16[520,128]{1,0:T(8,128)(2,1)S(1)} %collective-permute-done.19.refs_8_) | copy-start | bytes 399364
  71.7 51.1 %collective-permute-start.3 = (s16[520,128]{1,0:T(8,128)(2,1)}, s16[520,128]{1,0:T(8,128)(2,1)S(1)}, u32[]{:S(2)}, u32[]{:S(2)}) collective-permute-start(s16[520,128]{1,0:T(8,128)(2,1)} %get-tuple-element.45), channel_id=1, source_target_pairs={{0,16},{4,20},{8,24},{12,28},{16,0},{20,4},{24,8},{28,12},{1,17},{... | collective-permute-start | bytes 399368 | tf_op jit(solution)/shard_map/ppermute | solution.py:435
  74.7 37.9 %copy-start.23 = (s16[520,128]{1,0:T(8,128)(2,1)}, s16[520,128]{1,0:T(8,128)(2,1)S(1)}, u32[]{:S(2)}) copy-start(s16[520,128]{1,0:T(8,128)(2,1)S(1)} %collective-permute-done.20.refs_9_) | copy-start | bytes 399364
  74.7 48.9 %collective-permute-start.4 = (s16[520,128]{1,0:T(8,128)(2,1)}, s16[520,128]{1,0:T(8,128)(2,1)S(1)}, u32[]{:S(2)}, u32[]{:S(2)}) collective-permute-start(s16[520,128]{1,0:T(8,128)(2,1)} %get-tuple-element.46), channel_id=1, source_target_pairs={{0,20},{4,16},{8,28},{12,24},{16,4},{20,0},{24,12},{28,8},{1,21},{... | collective-permute-start | bytes 399368 | tf_op jit(solution)/shard_map/ppermute | solution.py:435
  84.2 45.3 %copy-start.6 = (s16[520,128]{1,0:T(8,128)(2,1)}, s16[520,128]{1,0:T(8,128)(2,1)S(1)}, u32[]{:S(2)}) copy-start(s16[520,128]{1,0:T(8,128)(2,1)S(1)} %collective-permute-done.refs_3_) | copy-start | bytes 399364
  84.2 42.1 %collective-permute-start.5 = (s16[520,128]{1,0:T(8,128)(2,1)}, s16[520,128]{1,0:T(8,128)(2,1)S(1)}, u32[]{:S(2)}, u32[]{:S(2)}) collective-permute-start(s16[520,128]{1,0:T(8,128)(2,1)} %get-tuple-element.47), channel_id=1, source_target_pairs={{0,24},{4,28},{8,16},{12,20},{16,8},{20,12},{24,0},{28,4},{1,25},{... | collective-permute-start | bytes 399368 | tf_op jit(solution)/shard_map/ppermute | solution.py:435
  121.5 7.9 %copy-start.9 = (s16[520,128]{1,0:T(8,128)(2,1)}, s16[520,128]{1,0:T(8,128)(2,1)S(1)}, u32[]{:S(2)}) copy-start(s16[520,128]{1,0:T(8,128)(2,1)S(1)} %collective-permute-done.1.refs_4_) | copy-start | bytes 399364
  121.5 7.9 %collective-permute-start.6 = (s16[520,128]{1,0:T(8,128)(2,1)S(1)}, s16[520,128]{1,0:T(8,128)(2,1)S(1)}, u32[]{:S(2)}, u32[]{:S(2)}) collective-permute-start(s16[520,128]{1,0:T(8,128)(2,1)S(1)} %copy-done.29), channel_id=1, source_target_pairs={{0,28},{4,24},{8,20},{12,16},{16,12},{20,8},{24,4},{28,0},{1,29},{... | collective-permute-start | bytes 399368 | tf_op jit(solution)/shard_map/ppermute | solution.py:435
  122.8 6.7 %copy-start.13 = (s16[520,128]{1,0:T(8,128)(2,1)}, s16[520,128]{1,0:T(8,128)(2,1)S(1)}, u32[]{:S(2)}) copy-start(s16[520,128]{1,0:T(8,128)(2,1)S(1)} %collective-permute-done.2.refs_5_) | copy-start | bytes 399364
  122.8 16.2 %collective-permute-start.21 = (s16[520,128]{1,0:T(8,128)(2,1)}, s16[520,128]{1,0:T(8,128)(2,1)S(1)}, u32[]{:S(2)}, u32[]{:S(2)}) collective-permute-start(s16[520,128]{1,0:T(8,128)(2,1)} %get-tuple-element.66), channel_id=1, source_target_pairs={{0,4},{4,0},{8,12},{12,8},{16,20},{20,16},{24,28},{28,24},{1,5},{5... | collective-permute-start | bytes 399368 | tf_op jit(solution)/shard_map/ppermute | solution.py:435
  122.8 6.6 %copy-start.18 = (s16[520,128]{1,0:T(8,128)(2,1)}, s16[520,128]{1,0:T(8,128)(2,1)S(1)}, u32[]{:S(2)}) copy-start(s16[520,128]{1,0:T(8,128)(2,1)S(1)} %collective-permute-done.3.refs_6_) | copy-start | bytes 399364
  122.8 19.1 %collective-permute-start.22 = (s16[520,128]{1,0:T(8,128)(2,1)}, s16[520,128]{1,0:T(8,128)(2,1)S(1)}, u32[]{:S(2)}, u32[]{:S(2)}) collective-permute-start(s16[520,128]{1,0:T(8,128)(2,1)} %get-tuple-element.67), channel_id=1, source_target_pairs={{0,8},{4,12},{8,0},{12,4},{16,24},{20,28},{24,16},{28,20},{1,9},{5... | collective-permute-start | bytes 399368 | tf_op jit(solution)/shard_map/ppermute | solution.py:435
  123.6 5.9 %copy-start.19 = (s16[520,128]{1,0:T(8,128)(2,1)}, s16[520,128]{1,0:T(8,128)(2,1)S(1)}, u32[]{:S(2)}) copy-start(s16[520,128]{1,0:T(8,128)(2,1)S(1)} %collective-permute-done.4.refs_7_) | copy-start | bytes 399364
  123.6 19.6 %collective-permute-start.23 = (s16[520,128]{1,0:T(8,128)(2,1)}, s16[520,128]{1,0:T(8,128)(2,1)S(1)}, u32[]{:S(2)}, u32[]{:S(2)}) collective-permute-start(s16[520,128]{1,0:T(8,128)(2,1)} %get-tuple-element.68), channel_id=1, source_target_pairs={{0,12},{4,8},{8,4},{12,0},{16,28},{20,24},{24,20},{28,16},{1,13},{... | collective-permute-start | bytes 399368 | tf_op jit(solution)/shard_map/ppermute | solution.py:435
  126.3 3.2 %copy-start.21 = (s16[520,128]{1,0:T(8,128)(2,1)}, s16[520,128]{1,0:T(8,128)(2,1)S(1)}, u32[]{:S(2)}) copy-start(s16[520,128]{1,0:T(8,128)(2,1)S(1)} %collective-permute-done.5.refs_8_) | copy-start | bytes 399364
  126.3 20.0 %collective-permute-start.24 = (s16[520,128]{1,0:T(8,128)(2,1)}, s16[520,128]{1,0:T(8,128)(2,1)S(1)}, u32[]{:S(2)}, u32[]{:S(2)}) collective-permute-start(s16[520,128]{1,0:T(8,128)(2,1)} %get-tuple-element.69), channel_id=1, source_target_pairs={{0,16},{4,20},{8,24},{12,28},{16,0},{20,4},{24,8},{28,12},{1,17},{... | collective-permute-start | bytes 399368 | tf_op jit(solution)/shard_map/ppermute | solution.py:435
  129.4 0.7 copy-start.24
  129.4 19.1 %collective-permute-start.25 = (s16[520,128]{1,0:T(8,128)(2,1)}, s16[520,128]{1,0:T(8,128)(2,1)S(1)}, u32[]{:S(2)}, u32[]{:S(2)}) collective-permute-start(s16[520,128]{1,0:T(8,128)(2,1)} %get-tuple-element.70), channel_id=1, source_target_pairs={{0,20},{4,16},{8,28},{12,24},{16,4},{20,0},{24,12},{28,8},{1,21},{... | collective-permute-start | bytes 399368 | tf_op jit(solution)/shard_map/ppermute | solution.py:435
  139.0 33.7 %copy-start.1 = (s16[520,128]{1,0:T(8,128)(2,1)}, s16[520,128]{1,0:T(8,128)(2,1)S(1)}, u32[]{:S(2)}) copy-start(s16[520,128]{1,0:T(8,128)(2,1)S(1)} %collective-permute-done.21.refs_11_) | copy-start | bytes 399364
  139.0 17.9 %collective-permute-start.26 = (s16[520,128]{1,0:T(8,128)(2,1)}, s16[520,128]{1,0:T(8,128)(2,1)S(1)}, u32[]{:S(2)}, u32[]{:S(2)}) collective-permute-start(s16[520,128]{1,0:T(8,128)(2,1)} %get-tuple-element.71), channel_id=1, source_target_pairs={{0,24},{4,28},{8,16},{12,20},{16,8},{20,12},{24,0},{28,4},{1,25},{... | collective-permute-start | bytes 399368 | tf_op jit(solution)/shard_map/ppermute | solution.py:435
  142.0 30.8 %copy-start.2 = (s16[520,128]{1,0:T(8,128)(2,1)}, s16[520,128]{1,0:T(8,128)(2,1)S(1)}, u32[]{:S(2)}) copy-start(s16[520,128]{1,0:T(8,128)(2,1)S(1)} %collective-permute-done.22.refs_12_) | copy-start | bytes 399364
  142.0 16.2 %collective-permute-start.27 = (s16[520,128]{1,0:T(8,128)(2,1)}, s16[520,128]{1,0:T(8,128)(2,1)S(1)}, u32[]{:S(2)}, u32[]{:S(2)}) collective-permute-start(s16[520,128]{1,0:T(8,128)(2,1)} %get-tuple-element.72), channel_id=1, source_target_pairs={{0,28},{4,24},{8,20},{12,16},{16,12},{20,8},{24,4},{28,0},{1,29},{... | collective-permute-start | bytes 399368 | tf_op jit(solution)/shard_map/ppermute | solution.py:435
  143.1 29.6 %copy-start.3 = (s16[520,128]{1,0:T(8,128)(2,1)}, s16[520,128]{1,0:T(8,128)(2,1)S(1)}, u32[]{:S(2)}) copy-start(s16[520,128]{1,0:T(8,128)(2,1)S(1)} %collective-permute-done.23.refs_13_) | copy-start | bytes 399364
  143.1 21.7 %collective-permute-start.10 = (s16[520,128]{1,0:T(8,128)(2,1)}, s16[520,128]{1,0:T(8,128)(2,1)S(1)}, u32[]{:S(2)}, u32[]{:S(2)}) collective-permute-start(s16[520,128]{1,0:T(8,128)(2,1)} %get-tuple-element.53), channel_id=1, source_target_pairs={{0,16},{4,20},{8,24},{12,28},{16,0},{20,4},{24,8},{28,12},{1,17},{... | collective-permute-start | bytes 399368 | tf_op jit(solution)/shard_map/ppermute | solution.py:435
  146.3 26.4 %copy-start.4 = (s16[520,128]{1,0:T(8,128)(2,1)}, s16[520,128]{1,0:T(8,128)(2,1)S(1)}, u32[]{:S(2)}) copy-start(s16[520,128]{1,0:T(8,128)(2,1)S(1)} %collective-permute-done.24.refs_14_) | copy-start | bytes 399364
  146.3 20.9 %collective-permute-start.11 = (s16[520,128]{1,0:T(8,128)(2,1)}, s16[520,128]{1,0:T(8,128)(2,1)S(1)}, u32[]{:S(2)}, u32[]{:S(2)}) collective-permute-start(s16[520,128]{1,0:T(8,128)(2,1)} %get-tuple-element.54), channel_id=1, source_target_pairs={{0,20},{4,16},{8,28},{12,24},{16,4},{20,0},{24,12},{28,8},{1,21},{... | collective-permute-start | bytes 399368 | tf_op jit(solution)/shard_map/ppermute | solution.py:435
  148.5 24.2 %copy-start.5 = (s16[520,128]{1,0:T(8,128)(2,1)}, s16[520,128]{1,0:T(8,128)(2,1)S(1)}, u32[]{:S(2)}) copy-start(s16[520,128]{1,0:T(8,128)(2,1)S(1)} %collective-permute-done.25.refs_15_) | copy-start | bytes 399364
  148.5 26.8 %collective-permute-start.12 = (s16[520,128]{1,0:T(8,128)(2,1)}, s16[520,128]{1,0:T(8,128)(2,1)S(1)}, u32[]{:S(2)}, u32[]{:S(2)}) collective-permute-start(s16[520,128]{1,0:T(8,128)(2,1)} %get-tuple-element.55), channel_id=1, source_target_pairs={{0,24},{4,28},{8,16},{12,20},{16,8},{20,12},{24,0},{28,4},{1,25},{... | collective-permute-start | bytes 399368 | tf_op jit(solution)/shard_map/ppermute | solution.py:435
  156.9 15.8 %copy-start.7 = (s16[520,128]{1,0:T(8,128)(2,1)}, s16[520,128]{1,0:T(8,128)(2,1)S(1)}, u32[]{:S(2)}) copy-start(s16[520,128]{1,0:T(8,128)(2,1)S(1)} %collective-permute-done.26.refs_16_) | copy-start | bytes 399364
  156.9 18.4 %collective-permute-start.13 = (s16[520,128]{1,0:T(8,128)(2,1)}, s16[520,128]{1,0:T(8,128)(2,1)}, u32[]{:S(2)}, u32[]{:S(2)}) collective-permute-start(s16[520,128]{1,0:T(8,128)(2,1)} %get-tuple-element.56), channel_id=1, source_target_pairs={{0,28},{4,24},{8,20},{12,16},{16,12},{20,8},{24,4},{28,0},{1,29},{... | collective-permute-start | bytes 399368 | tf_op jit(solution)/shard_map/ppermute | solution.py:435
  158.2 14.6 %copy-start.8 = (s16[520,128]{1,0:T(8,128)(2,1)}, s16[520,128]{1,0:T(8,128)(2,1)S(1)}, u32[]{:S(2)}) copy-start(s16[520,128]{1,0:T(8,128)(2,1)S(1)} %collective-permute-done.27.refs_17_) | copy-start | bytes 399364
  158.2 17.2 %collective-permute-start.7 = (s16[520,128]{1,0:T(8,128)(2,1)}, s16[520,128]{1,0:T(8,128)(2,1)}, u32[]{:S(2)}, u32[]{:S(2)}) collective-permute-start(s16[520,128]{1,0:T(8,128)(2,1)} %get-tuple-element.50), channel_id=1, source_target_pairs={{0,4},{4,0},{8,12},{12,8},{16,20},{20,16},{24,28},{28,24},{1,5},{5... | collective-permute-start | bytes 399368 | tf_op jit(solution)/shard_map/ppermute | solution.py:435
  164.8 7.9 %copy-start.12 = (s16[520,128]{1,0:T(8,128)(2,1)}, s16[520,128]{1,0:T(8,128)(2,1)S(1)}, u32[]{:S(2)}) copy-start(s16[520,128]{1,0:T(8,128)(2,1)S(1)} %collective-permute-done.10.refs_6_) | copy-start | bytes 399364
  164.8 10.5 %collective-permute-start.8 = (s16[520,128]{1,0:T(8,128)(2,1)}, s16[520,128]{1,0:T(8,128)(2,1)}, u32[]{:S(2)}, u32[]{:S(2)}) collective-permute-start(s16[520,128]{1,0:T(8,128)(2,1)} %get-tuple-element.51), channel_id=1, source_target_pairs={{0,8},{4,12},{8,0},{12,4},{16,24},{20,28},{24,16},{28,20},{1,9},{5... | collective-permute-start | bytes 399368 | tf_op jit(solution)/shard_map/ppermute | solution.py:435
  167.2 5.6 %copy-start.16 = (s16[520,128]{1,0:T(8,128)(2,1)}, s16[520,128]{1,0:T(8,128)(2,1)S(1)}, u32[]{:S(2)}) copy-start(s16[520,128]{1,0:T(8,128)(2,1)S(1)} %collective-permute-done.11.refs_7_) | copy-start | bytes 399364
  167.2 8.2 %collective-permute-start.9 = (s16[520,128]{1,0:T(8,128)(2,1)}, s16[520,128]{1,0:T(8,128)(2,1)}, u32[]{:S(2)}, u32[]{:S(2)}) collective-permute-start(s16[520,128]{1,0:T(8,128)(2,1)} %get-tuple-element.52), channel_id=1, source_target_pairs={{0,12},{4,8},{8,4},{12,0},{16,28},{20,24},{24,20},{28,16},{1,13},{... | collective-permute-start | bytes 399368 | tf_op jit(solution)/shard_map/ppermute | solution.py:435
  175.3 0.7 copy-start.20
  190.2 13.7 %all-to-all-start.1 = ((f32[32,8,128]{2,1,0:T(8,128)}), f32[32,8,128]{2,1,0:T(8,128)S(1)}, u32[]{:S(2)}, u32[]{:S(2)}) async-start(f32[32,8,128]{2,1,0:T(8,128)} %broadcast_in_dim.62), calls=%async_computation.1 | async-start | bytes 262144 | tf_op jit(solution)/shard_map/all_to_all | solution.py:593
  203.9 0.6 copy-start
Sparse Core Ops, SparseCore 0:
  36.3 21.5 all-gather.4

commit v2 on v1

--- a/solution.py
+++ b/solution.py
@@ -15,6 +15,7 @@
 TILE = 64
 SUB = 16
 LANES = 128
+WINDOW = 5
 F32 = jnp.float32
 BF16 = jnp.bfloat16
 I16 = jnp.int16
@@ -145,11 +146,38 @@
                 out[2 * rows:, :] = marks[chunk, slab].astype(jnp.int32).astype(I16)
 
 
-def columns_kernel(slabs, chunk, length, me_ref, corr_ref, *rest):
+def pack_copies(slabs, me, source_ref, prints_ref, packed, semaphore, act):
+    for hop in range(slabs):
+        share = packed[hop].shape[0] - 1
+
+        def one(at, carry, hop=hop, share=share):
+            source = source_ref[(me ^ hop) * share + at]
+
+            @pl.when(source >= 0)
+            def _():
+                act(pltpu.make_async_copy(prints_ref.at[source], packed[hop].at[at], semaphore))
+
+            return carry
+
+        lax.fori_loop(0, share, one, 0)
+
+
+def columns_kernel(slabs, chunk, length, packs, me_ref, corr_ref, *rest):
+    me = me_ref[0]
+    if packs:
+        (source_ref, prints_ref, code_ref), rest = rest[:3], rest[3:]
+        packed, semaphore = rest[-6 - slabs:-6], rest[-6]
+        rest = rest[:-6 - slabs] + rest[-5:]
+        for hop in range(slabs):
+            share = packed[hop].shape[0] - 1
+            packed[hop][:share] = jnp.zeros_like(packed[hop][:share])
+            packed[hop][share] = code_ref[me ^ hop]
+        pack_copies(
+            slabs, me, source_ref, prints_ref, packed, semaphore, lambda copy: copy.start()
+        )
     ins, rest = rest[:slabs], rest[slabs:]
     back_lead, back_trail, lead, trail, turn_ref = rest[:5]
     outs, (stack, scale, field, high, low) = rest[5:5 + slabs], rest[5 + slabs:]
-    me = me_ref[0]
     short = length // RADIX
     rows = stack.shape[1] // 2
     width = stack.shape[2]
@@ -243,6 +271,10 @@
     for hop in range(slabs):
         outs[hop][:2 * rows, :] = stack[me ^ hop]
         outs[hop][2 * rows:, :] = scale[me ^ hop].astype(jnp.int32).astype(I16)
+    if packs:
+        pack_copies(
+            slabs, me, source_ref, prints_ref, packed, semaphore, lambda copy: copy.wait()
+        )
 
 
 def finish_kernel(slabs, chunks, me_ref, gain_ref, *rest):
@@ -318,37 +350,23 @@
         values = dot(blocks[...], prints_ref[...])
         each = count // 2 * bands
         chosen = lax.broadcasted_iota(jnp.int32, (each, 1), 0) == index_ref[...]
+        tiles = index_ref.shape[1] // LANES
         for part in range(2):
-            value_ref[part:part + 1, :] = jnp.sum(
+            line = jnp.sum(
                 jnp.where(chosen, values[part * each:(part + 1) * each, :], 0.0), axis=0, keepdims=True
             )
-
-
-def pack_kernel(source_ref, prints_ref, out_ref, semaphore):
-    out_ref[...] = jnp.zeros_like(out_ref)
-    count = out_ref.shape[0]
-
-    def begin(at, carry):
-        @pl.when(source_ref[at] >= 0)
-        def _():
-            pltpu.make_async_copy(
-                prints_ref.at[source_ref[at]], out_ref.at[at], semaphore
-            ).start()
-        return carry
-
-    def end(at, carry):
-        @pl.when(source_ref[at] >= 0)
-        def _():
-            pltpu.make_async_copy(
-                prints_ref.at[source_ref[at]], out_ref.at[at], semaphore
-            ).wait()
-        return carry
-
-    lax.fori_loop(0, count, begin, 0)
-    lax.fori_loop(0, count, end, 0)
-
-
-def small_kernel(slabs, lanes_q, each, total, row_ref, all_ref, pick_ref, sketch_ref, factor_ref, basis_ref, own):
+            for at in range(tiles):
+                value_ref[0, part * tiles + at:part * tiles + at + 1, :] = (
+                    line[:, at * LANES:(at + 1) * LANES]
+                )
+        for copy in range(1, value_ref.shape[0]):
+            value_ref[copy] = value_ref[0]
+
+
+def small_kernel(
+    slabs, lanes_q, each, total, row_ref, lane_ref, all_ref, pick_ref, sketch_ref, factor_ref, basis_ref,
+    own, found,
+):
     probes = lanes_q * each
     tiles = all_ref.shape[1] // each
     gram = {}
@@ -385,7 +403,7 @@
     for slab in range(slabs):
         for one in range(probes):
             own[one:one + 1, slab * LANES:(slab + 1) * LANES] = all_ref[
-                slab * lanes_q + one // each, pl.ds((one % each) * tiles + row_ref[0], 1), :
+                slab * lanes_q + one // each, pl.ds((one % each) * tiles + row_ref[slab], 1), :
             ]
     value = own[...]
     first = value.astype(BF16)
@@ -393,14 +411,18 @@
     second = rest.astype(BF16)
     third = (rest - second.astype(F32)).astype(BF16)
     sketch = dot(first, pick_ref[...]) + dot(second, pick_ref[...]) + dot(third, pick_ref[...])
-    sketch_ref[...] = sketch
+    found[0] = sketch
     solved = []
     for at in range(probes):
         value = sketch[at:at + 1, :]
         for back in range(at):
             value = value - lower[at, back] * solved[back]
         solved.append(value * inverse[at])
-        basis_ref[at:at + 1, :] = solved[at]
+        found[1, at:at + 1, :] = solved[at]
+    for part in range(each):
+        place = pl.ds(lane_ref[0] * each + part, 1)
+        sketch_ref[part:part + 1, :] = found[0, place, :]
+        basis_ref[part:part + 1, :] = found[1, place, :]
 
 
 def vmem():
@@ -426,13 +448,17 @@
     return jnp.sum(root * root * root * (weight_y[:, None] * weight_x[None, :]))
 
 
-def exchange(blocks):
+def exchange(blocks, sent):
     slabs = len(blocks)
     order = sorted(range(1, slabs), key=lambda hop: (-(hop * 2 // slabs), -(hop * 4 // slabs % 2)))
     arrived = [blocks[0]] + [None] * (slabs - 1)
     for hop in order:
         pairs = [(source, source ^ hop) for source in range(slabs)]
-        arrived[hop] = lax.ppermute(blocks[hop], "grid", pairs)
+        block = blocks[hop]
+        if len(sent) >= WINDOW:
+            block, _ = lax.optimization_barrier((block, sent[-WINDOW]))
+        arrived[hop] = lax.ppermute(block, "grid", pairs)
+        sent.append(arrived[hop])
     return arrived
 
 
@@ -484,62 +510,51 @@
         name="rows_forward",
     )(me_list, flat, lead, trail, turn_x)
 
+    history = []
     arrived = []
     for chunk in range(chunks):
-        arrived.append(exchange(sent[chunk * slabs:(chunk + 1) * slabs]))
+        arrived.append(exchange(sent[chunk * slabs:(chunk + 1) * slabs], history))
 
     read_count, band_rows, tile_cols = footprints.shape
     band_count = rows // band_rows
     tile_count = width // tile_cols
     capacity = 2 * read_count // slabs
     share = capacity // lanes_q
-    target = reading_slab[:, 0]
+    slots = slabs * capacity
+    target, _ = lax.optimization_barrier((reading_slab[:, 0], history[slabs // 2]))
     reading = jnp.arange(read_count, dtype=jnp.int32)
     onehot = (target[:, None] == jnp.arange(slabs, dtype=jnp.int32)[None, :]).astype(F32)
     before = (reading[:, None] > reading[None, :]).astype(F32)
     slot = jnp.sum(jnp.dot(before, onehot) * onehot, axis=1).astype(jnp.int32)
     place = target * capacity + slot
+    blocks = band_count * tile_count
     code = reading_tile * band_count + reading_band
     wanted = (
         jnp.arange(slabs, dtype=jnp.int32)[:, None] * capacity
         + lane_at * share
         + jnp.arange(share, dtype=jnp.int32)[None, :]
     ).reshape(-1)
-    source = jnp.max(
-        jnp.where(wanted[:, None] == place[None, :], reading[None, :], -1), axis=1
+    found = jnp.max(
+        jnp.where(wanted[:, None] == place[None, :], (reading * blocks + code)[None, :], -1), axis=1
     )
-    packed = pl.pallas_call(
-        pack_kernel,
-        in_specs=[smem(), pl.BlockSpec(memory_space=pl.ANY)],
-        out_specs=vmem(),
-        out_shape=jax.ShapeDtypeStruct((slabs * share, band_rows, tile_cols), BF16),
-        scratch_shapes=[pltpu.SemaphoreType.DMA],
-        compiler_params=params(),
-        name="pack_prints",
-    )(source, footprints)
-    shared = lax.all_to_all(
-        packed.reshape(slabs, share, band_rows, tile_cols), "grid", split_axis=0, concat_axis=0, tiled=True
-    )
-    prints = lax.all_gather(shared, "probe", axis=0, tiled=False)
-    slots = slabs * capacity
-    prints = prints.transpose(3, 4, 1, 0, 2).reshape(band_rows * tile_cols, slots)
-    listed = lax.all_gather(jnp.stack([place, code]), "grid", axis=0, tiled=False)
-    here = me * capacity + jnp.arange(capacity, dtype=jnp.int32)
-    index = jnp.max(
-        jnp.where(here[None, :, None] == listed[:, 0, None, :], listed[:, 1, None, :], 0), axis=2
-    ).reshape(1, slots)
-
-    gain = lax.rsqrt(filter_power(corr_lengths, height, width) / (height * width)) / (height * width)
-
-    returned = []
+    source = jnp.where(found < 0, -1, found // blocks)
+    codes = jnp.where(found < 0, 0, found % blocks).astype(BF16).reshape(slabs, 1, share)
+    codes = jnp.pad(codes, ((0, 0), (0, band_rows - 1), (0, tile_cols - share)))
+
+    halfway = []
     group = 256 // cut if cut % LANES == 0 else 1
+    parcel = jax.ShapeDtypeStruct((share + 1, band_rows, tile_cols), BF16)
     for chunk in range(chunks):
+        packs = chunk == 0
         results = pl.pallas_call(
-            lambda *refs, chunk=chunk: columns_kernel(slabs, chunk, height, *refs),
-            in_specs=[smem(), smem()] + [vmem()] * (slabs + 5),
-            out_specs=[vmem()] * slabs,
-            out_shape=[payload] * slabs,
-            scratch_shapes=[
+            lambda *refs, chunk=chunk, packs=packs: columns_kernel(slabs, chunk, height, packs, *refs),
+            in_specs=[smem(), smem()]
+            + ([smem(), pl.BlockSpec(memory_space=pl.ANY), vmem()] if packs else [])
+            + [vmem()] * (slabs + 5),
+            out_specs=[vmem()] * (2 * slabs if packs else slabs),
+            out_shape=[payload] * slabs + ([parcel] * slabs if packs else []),
+            scratch_shapes=([pltpu.SemaphoreType.DMA] if packs else [])
+            + [
                 pltpu.VMEM((slabs, 2 * rows, cut), I16),
                 pltpu.VMEM((slabs, RADIX, cut), F32),
                 pltpu.VMEM((2, height, cut), F32),
@@ -548,9 +563,33 @@
             ],
             compiler_params=params(),
             name="columns",
-        )(me_list, corr_lengths, *arrived[chunk], lead, trail, back_lead, back_trail, turn_y)
-        returned += exchange(results)
-
+        )(
+            me_list,
+            corr_lengths,
+            *([source, footprints, codes] if packs else []),
+            *arrived[chunk],
+            lead,
+            trail,
+            back_lead,
+            back_trail,
+            turn_y,
+        )
+        halfway.append(list(results[:slabs]))
+        if packs:
+            parcels = results[slabs:]
+
+    shared = jnp.stack(exchange(parcels, history))
+    gathered = lax.all_gather(shared, "probe", axis=0, tiled=False)
+    prints = gathered[:, :, :share].transpose(3, 4, 1, 0, 2).reshape(band_rows * tile_cols, slots)
+    index = gathered[:, :, share, 0, :share].transpose(1, 0, 2).reshape(1, slots).astype(jnp.int32)
+
+    gain = lax.rsqrt(filter_power(corr_lengths, height, width) / (height * width)) / (height * width)
+
+    returned = []
+    for results in halfway:
+        returned += exchange(results, history)
+
+    group_count = slabs * lanes_q
     smoothed, values = pl.pallas_call(
         lambda *refs: finish_kernel(slabs, chunks, *refs),
         grid=(rows // tile,),
@@ -565,11 +604,11 @@
         ],
         out_specs=[
             pl.BlockSpec((tile * each * column_tiles, LANES), lambda step: (step, 0)),
-            whole((each, slots)),
+            whole((group_count, each * slots // LANES, LANES)),
         ],
         out_shape=[
             jax.ShapeDtypeStruct(flat.shape, F32),
-            jax.ShapeDtypeStruct((each, slots), F32),
+            jax.ShapeDtypeStruct((group_count, each * slots // LANES, LANES), F32),
         ],
         scratch_shapes=[
             pltpu.VMEM((chunks, slabs, 2 * rows, cut), I16),
@@ -586,31 +625,28 @@
         smoothed.reshape(rows, column_tiles, each, LANES).transpose(0, 2, 1, 3).reshape(rows, each, width)
     )
 
-    group_count = slabs * lanes_q
-    spread = jnp.broadcast_to(
-        values.reshape(1, each * slots // LANES, LANES), (group_count, each * slots // LANES, LANES)
-    )
-    everyone = lax.all_to_all(spread, ("grid", "probe"), split_axis=0, concat_axis=0, tiled=True)
-    offset = me * capacity
-    lane_of = target * LANES + offset % LANES + slot
+    everyone = lax.all_to_all(values, ("grid", "probe"), split_axis=0, concat_axis=0, tiled=True)
+    offset = (me ^ jnp.arange(slabs, dtype=jnp.int32)) * capacity
+    lane_of = target * LANES + (me ^ target) * capacity % LANES + slot
     pick = (jnp.arange(slabs * LANES, dtype=jnp.int32)[:, None] == lane_of[None, :]).astype(BF16)
     probe_count = each * lanes_q
-    full, factor, basis = pl.pallas_call(
+    sketch, factor, basis = pl.pallas_call(
         lambda *refs: small_kernel(slabs, lanes_q, each, read_count * slabs, *refs),
-        in_specs=[smem(), vmem(), vmem()],
+        in_specs=[smem(), smem(), vmem(), vmem()],
         out_specs=[vmem()] * 3,
         out_shape=[
-            jax.ShapeDtypeStruct((probe_count, read_count), F32),
+            jax.ShapeDtypeStruct((each, read_count), F32),
             jax.ShapeDtypeStruct((probe_count, probe_count), F32),
-            jax.ShapeDtypeStruct((probe_count, read_count), F32),
-        ],
-        scratch_shapes=[pltpu.VMEM((probe_count, slabs * LANES), F32)],
+            jax.ShapeDtypeStruct((each, read_count), F32),
+        ],
+        scratch_shapes=[
+            pltpu.VMEM((probe_count, slabs * LANES), F32),
+            pltpu.VMEM((2, probe_count, read_count), F32),
+        ],
         compiler_params=params(),
         name="factor_basis",
-    )((offset // LANES).reshape(1), everyone, pick)
-    sketch = lax.dynamic_slice_in_dim(full, lane_at * each, each, 0).T
-    basis = lax.dynamic_slice_in_dim(basis, lane_at * each, each, 0).T
-    return (smoothed, sketch, factor, basis)
+    )(offset // LANES, lane_at.reshape(1).astype(jnp.int32), everyone, pick)
+    return (smoothed, sketch.T, factor, basis.T)
 
 
 def solution(mesh):

time: 217 us -> 180 us (0.83)
  blocking collectives: 48.2 us -> 0 us
  starting transfers between devices: 55.8 us -> 73.4 us
  waiting for transfers between devices: 28.9 us -> 26.5 us
    all_gather x1 -> x0, blocking collectives: 26.2 us -> none  [local(): lax.all_gather(jnp.stack([place, code]), 'grid', axis=0, tiled=False)]
    all_to_all x1 -> x0, blocking collectives: 22.1 us -> none  [local(): lax.all_to_all(packed.reshape(slabs, share, band_rows, tile_cols), 'grid'...]
    ppermute x28 -> x35, starting transfers between devices: 50.2 us -> 68 us  [exchange(): arrived[hop] = lax.ppermute(block, 'grid', pairs)]
    transpose x3 -> x0, local copies, waits for them, and re-layouts: 4.73 us -> none  [the longest x1 2.17 us: local(): prints.transpose(3, 4, 1, 0, 2).reshape(band_rows * tile_cols, slots)]
    slice x1 -> x2, local copies, waits for them, and re-layouts: 0.01 us -> 2.81 us  [the longest x1 1.95 us: local(): gathered[:, :, :share].transpose(3, 4, 1, 0, 2)]
    ppermute x28 -> x35, waiting for transfers between devices: 21.7 us -> 19.9 us  [exchange(): arrived[hop] = lax.ppermute(block, 'grid', pairs)]
    pallas_call x3 -> x2, Pallas kernels: 22.2 us -> 20.7 us  [local(): pl.pallas_call(lambda *refs, chunk=chunk, packs=packs: columns_kernel(sla...]
  transfers between devices with their start and end apart: 30 -> 37, of which waited for: 8 -> 13; matrix products, arithmetic and copies ran while one was open for 5% -> 8% of each run, Pallas kernels for 13% -> 11%
where the time goes in v2:
time: 180 us
  starting transfers between devices  73.4 us (41%)
  Pallas kernels  46.4 us (26%)
  waiting for transfers between devices  26.5 us (15%)
  between operations  16.6 us (9%)
  local copies, waits for them, and re-layouts  11.7 us (6%)
  other arithmetic  5.31 us (3%)
    ppermute x35, starting transfers between devices, exchange(): arrived[hop] = lax.ppermute(block, 'grid', pairs)  68 us
    pallas_call x2, Pallas kernels, local(): pl.pallas_call(lambda *refs, chunk=chunk, packs=packs: columns_kernel(sla...  20.7 us
    ppermute x35, waiting for transfers between devices, exchange(): arrived[hop] = lax.ppermute(block, 'grid', pairs)  19.9 us
    pallas_call x1, Pallas kernels, local(): pl.pallas_call(lambda *refs: finish_kernel(slabs, chunks, *refs), grid=(r...  13.2 us
    pallas_call x1, Pallas kernels, local(): pl.pallas_call(lambda *refs: rows_kernel(slabs, chunks, *refs), grid=(row...  10.5 us
    all_to_all x1, waiting for transfers between devices, local(): lax.all_to_all(values, ('grid', 'probe'), split_axis=0, concat_axis=0, ti...  6.61 us
    all_to_all x1, starting transfers between devices, local(): lax.all_to_all(values, ('grid', 'probe'), split_axis=0, concat_axis=0, ti...  5.38 us
    unnamed x81, local copies, waits for them, and re-layouts  4.28 us
  transfers between devices with their start and end apart: 37, of which 13 were waited for; matrix products, arithmetic and copies ran while one was open for 8% of the time, Pallas kernels for 11%

profile of v2, /device:TPU:0, one launch (start us, length us, event | category | flops | bytes accessed | tf_op | source)
XLA Modules:
  0.0 180.1 jit_solution(1460292971944680717)
XLA Ops:
  7.2 10.5 %rows_forward.1 = (s16[520,128]{1,0:T(8,128)(2,1)}, s16[520,128]{1,0:T(8,128)(2,1)}, s16[520,128]{1,0:T(8,128)(2,1)}, s16[520,128]{1,0:T(8,128)(2,1)}, s16[520,1...) custom-call(s32[1]{0:T(128)} %bitcast.refs_0_, ...), custom_call_target="tpu_custom_call" | custom-call | tf_op jit(solution)/shard_map/rows_forward/pallas_call | solution.py:491
  17.8 3.1 %collective-permute-start = (s16[520,128]{1,0:T(8,128)(2,1)}, s16[520,128]{1,0:T(8,128)(2,1)S(1)}, u32[]{:S(2)}, u32[]{:S(2)}) collective-permute-start(s16[520,128]{1,0:T(8,128)(2,1)} %get-tuple-element.80), channel_id=1, source_target_pairs={{0,8},{4,12},{8,0},{12,4},{16,24},{20,28},{24,16},{28,20},{1,9},{5... | collective-permute-start | bytes 399368 | tf_op jit(solution)/shard_map/ppermute | solution.py:460
  20.9 3.4 %collective-permute-start.1 = (s16[520,128]{1,0:T(8,128)(2,1)}, s16[520,128]{1,0:T(8,128)(2,1)S(1)}, u32[]{:S(2)}, u32[]{:S(2)}) collective-permute-start(s16[520,128]{1,0:T(8,128)(2,1)} %get-tuple-element.84), channel_id=1, source_target_pairs={{0,28},{4,24},{8,20},{12,16},{16,12},{20,8},{24,4},{28,0},{1,29},{... | collective-permute-start | bytes 399368 | tf_op jit(solution)/shard_map/ppermute | solution.py:460
  24.3 1.3 collective-permute-start.3
  25.6 0.8 collective-permute-start.5
  26.4 2.1 %collective-permute-start.6 = (s16[520,128]{1,0:T(8,128)(2,1)}, s16[520,128]{1,0:T(8,128)(2,1)S(1)}, u32[]{:S(2)}, u32[]{:S(2)}) collective-permute-start(s16[520,128]{1,0:T(8,128)(2,1)} %get-tuple-element.90), channel_id=1, source_target_pairs={{0,20},{4,16},{8,28},{12,24},{16,4},{20,0},{24,12},{28,8},{1,21},{... | collective-permute-start | bytes 399368 | tf_op jit(solution)/shard_map/ppermute | solution.py:460
  28.7 0.2 fusion.2
  28.9 0.2 select_reduce_fusion
  29.2 2.7 %collective-permute-done.1.refs_12_ = s16[520,128]{1,0:T(8,128)(2,1)S(1)} collective-permute-done((s16[520,128]{1,0:T(8,128)(2,1)}, s16[520,128]{1,0:T(8,128)(2,1)S(1)}, u32[]{:S(2)}, u32[]{:S(2)}) %collective-permute-start.1) | collective-permute-done | bytes 133152 | tf_op jit(solution)/shard_map/ppermute | solution.py:460
  32.0 1.4 collective-permute-done.3.refs_11_
  33.3 10.5 %collective-permute-start.4 = (s16[520,128]{1,0:T(8,128)(2,1)}, s16[520,128]{1,0:T(8,128)(2,1)S(1)}, u32[]{:S(2)}, u32[]{:S(2)}) collective-permute-start(s16[520,128]{1,0:T(8,128)(2,1)} %get-tuple-element.88), channel_id=1, source_target_pairs={{0,12},{4,8},{8,4},{12,0},{16,28},{20,24},{24,20},{28,16},{1,13},{... | collective-permute-start | bytes 399368 | tf_op jit(solution)/shard_map/ppermute | solution.py:460
  43.8 1.0 collective-permute-done.5.refs_9_
  44.8 3.8 %collective-permute-start.7 = (s16[520,128]{1,0:T(8,128)(2,1)}, s16[520,128]{1,0:T(8,128)(2,1)S(1)}, u32[]{:S(2)}, u32[]{:S(2)}) collective-permute-start(s16[520,128]{1,0:T(8,128)(2,1)} %get-tuple-element.97), channel_id=1, source_target_pairs={{0,24},{4,28},{8,16},{12,20},{16,8},{20,12},{24,0},{28,4},{1,25},{... | collective-permute-start | bytes 399368 | tf_op jit(solution)/shard_map/ppermute | solution.py:460
  48.7 1.1 collective-permute-done.6.refs_10_
  49.8 2.6 %collective-permute-start.20 = (s16[520,128]{1,0:T(8,128)(2,1)}, s16[520,128]{1,0:T(8,128)(2,1)S(1)}, u32[]{:S(2)}, u32[]{:S(2)}) collective-permute-start(s16[520,128]{1,0:T(8,128)(2,1)} %get-tuple-element.122), channel_id=1, source_target_pairs={{0,28},{4,24},{8,20},{12,16},{16,12},{20,8},{24,4},{28,0},{1,29},{... | collective-permute-start | bytes 399368 | tf_op jit(solution)/shard_map/ppermute | solution.py:460
  52.4 4.6 %collective-permute-start.12 = (s16[520,128]{1,0:T(8,128)(2,1)}, s16[520,128]{1,0:T(8,128)(2,1)S(1)}, u32[]{:S(2)}, u32[]{:S(2)}) collective-permute-start(s16[520,128]{1,0:T(8,128)(2,1)} %get-tuple-element.106), channel_id=1, source_target_pairs={{0,20},{4,16},{8,28},{12,24},{16,4},{20,0},{24,12},{28,8},{1,21},{... | collective-permute-start | bytes 399368 | tf_op jit(solution)/shard_map/ppermute | solution.py:460
  57.0 0.5 fusion.12.refs_2_
  57.5 0.6 pad.4.refs_4_
  58.2 0.6 copy-done.7
  58.8 11.7 %columns.2 = (s16[520,128]{1,0:T(8,128)(2,1)}, s16[520,128]{1,0:T(8,128)(2,1)}, s16[520,128]{1,0:T(8,128)(2,1)}, s16[520,128]{1,0:T(8,128)(2,1)}, s16[520,128]{1...) custom-call(s32[1]{0:T(128)} %bitcast.refs_0_, ...), custom_call_target="tpu_custom_call" | custom-call | tf_op jit(solution)/shard_map/columns/pallas_call | solution.py:549
  70.7 3.5 %collective-permute-start.13 = (bf16[17,16,128]{2,1,0:T(8,128)(2,1)}, bf16[17,16,128]{2,1,0:T(8,128)(2,1)S(1)}, u32[]{:S(2)}, u32[]{:S(2)}) collective-permute-start(bf16[17,16,128]{2,1,0:T(8,128)(2,1)} %get-tuple-element.107), channel_id=1, source_target_pairs={{0,28},{4,24},{8,20},{12,16},{16,12},{20,8},{24,4},{28,0},{1,29},{... | collective-permute-start | bytes 208904 | tf_op jit(solution)/shard_map/ppermute | solution.py:460
  74.3 1.9 %collective-permute-start.16 = (s16[520,128]{1,0:T(8,128)(2,1)S(1)}, s16[520,128]{1,0:T(8,128)(2,1)S(1)}, u32[]{:S(2)}, u32[]{:S(2)}) collective-permute-start(s16[520,128]{1,0:T(8,128)(2,1)S(1)} %copy-done.34), channel_id=1, source_target_pairs={{0,8},{4,12},{8,0},{12,4},{16,24},{20,28},{24,16},{28,20},{1,9},{5... | collective-permute-start | bytes 399368 | tf_op jit(solution)/shard_map/ppermute | solution.py:460
  76.3 1.6 collective-permute-start.21
  77.9 0.3 collective-permute-start.25
  78.2 0.7 collective-permute-done.13
  78.9 0.8 collective-permute-start.14
  79.6 0.9 bitcast_dynamic-update-slice_fusion.7
  80.5 3.8 %collective-permute-done.25 = bf16[17,16,128]{2,1,0:T(8,128)(2,1)S(1)} collective-permute-done((bf16[17,16,128]{2,1,0:T(8,128)(2,1)}, bf16[17,16,128]{2,1,0:T(8,128)(2,1)S(1)}, u32[]{:S(2)}, u32[]{:S(2)}) %collective-permute-start.25) | collective-permute-done | bytes 69664 | tf_op jit(solution)/shard_map/ppermute | solution.py:460
  84.3 3.9 %collective-permute-start.9 = (bf16[17,16,128]{2,1,0:T(8,128)(2,1)}, bf16[17,16,128]{2,1,0:T(8,128)(2,1)S(1)}, u32[]{:S(2)}, u32[]{:S(2)}) collective-permute-start(bf16[17,16,128]{2,1,0:T(8,128)(2,1)} %get-tuple-element.99), channel_id=1, source_target_pairs={{0,20},{4,16},{8,28},{12,24},{16,4},{20,0},{24,12},{28,8},{1,21},{... | collective-permute-start | bytes 208904 | tf_op jit(solution)/shard_map/ppermute | solution.py:460
  88.2 1.9 %collective-permute-start.22 = (bf16[17,16,128]{2,1,0:T(8,128)(2,1)}, bf16[17,16,128]{2,1,0:T(8,128)(2,1)S(1)}, u32[]{:S(2)}, u32[]{:S(2)}) collective-permute-start(bf16[17,16,128]{2,1,0:T(8,128)(2,1)} %get-tuple-element.124), channel_id=1, source_target_pairs={{0,8},{4,12},{8,0},{12,4},{16,24},{20,28},{24,16},{28,20},{1,9},{5... | collective-permute-start | bytes 208904 | tf_op jit(solution)/shard_map/ppermute | solution.py:460
  90.2 2.6 %collective-permute-done.22 = bf16[17,16,128]{2,1,0:T(8,128)(2,1)S(1)} collective-permute-done((bf16[17,16,128]{2,1,0:T(8,128)(2,1)}, bf16[17,16,128]{2,1,0:T(8,128)(2,1)S(1)}, u32[]{:S(2)}, u32[]{:S(2)}) %collective-permute-start.22) | collective-permute-done | bytes 69664 | tf_op jit(solution)/shard_map/ppermute | solution.py:460
  92.8 1.3 collective-permute-done.17
  94.2 0.8 copy-done
  95.1 1.6 collective-permute-start.27
  96.6 2.4 %collective-permute-start.10 = (s16[520,128]{1,0:T(8,128)(2,1)}, s16[520,128]{1,0:T(8,128)(2,1)S(1)}, u32[]{:S(2)}, u32[]{:S(2)}) collective-permute-start(s16[520,128]{1,0:T(8,128)(2,1)} %get-tuple-element.100), channel_id=1, source_target_pairs={{0,28},{4,24},{8,20},{12,16},{16,12},{20,8},{24,4},{28,0},{1,29},{... | collective-permute-start | bytes 399368 | tf_op jit(solution)/shard_map/ppermute | solution.py:460
  99.0 2.4 %collective-permute-start.18 = (s16[520,128]{1,0:T(8,128)(2,1)}, s16[520,128]{1,0:T(8,128)(2,1)S(1)}, u32[]{:S(2)}, u32[]{:S(2)}) collective-permute-start(s16[520,128]{1,0:T(8,128)(2,1)} %get-tuple-element.116), channel_id=1, source_target_pairs={{0,24},{4,28},{8,16},{12,20},{16,8},{20,12},{24,0},{28,4},{1,25},{... | collective-permute-start | bytes 399368 | tf_op jit(solution)/shard_map/ppermute | solution.py:460
  101.4 0.6 fusion.13
  103.4 9.0 %columns.3 = (s16[520,128]{1,0:T(8,128)(2,1)}, s16[520,128]{1,0:T(8,128)(2,1)}, s16[520,128]{1,0:T(8,128)(2,1)}, s16[520,128]{1,0:T(8,128)(2,1)}, s16[520,128]{1...) custom-call(s32[1]{0:T(128)} %bitcast.refs_0_, f32[2]{0:T(128)} %refs_1_.3, ...), custom_call_target="tpu_custom_call" | custom-call | tf_op jit(solution)/shard_map/columns/pallas_call | solution.py:549
  112.3 2.0 %collective-permute-start.15 = (s16[520,128]{1,0:T(8,128)(2,1)S(1)}, s16[520,128]{1,0:T(8,128)(2,1)S(1)}, u32[]{:S(2)}, u32[]{:S(2)}) collective-permute-start(s16[520,128]{1,0:T(8,128)(2,1)S(1)} %copy-done.32), channel_id=1, source_target_pairs={{0,8},{4,12},{8,0},{12,4},{16,24},{20,28},{24,16},{28,20},{1,9},{5... | collective-permute-start | bytes 399368 | tf_op jit(solution)/shard_map/ppermute | solution.py:460
  114.4 2.4 %collective-permute-start.28 = (s16[520,128]{1,0:T(8,128)(2,1)}, s16[520,128]{1,0:T(8,128)(2,1)S(1)}, u32[]{:S(2)}, u32[]{:S(2)}) collective-permute-start(s16[520,128]{1,0:T(8,128)(2,1)} %get-tuple-element.138), channel_id=1, source_target_pairs={{0,28},{4,24},{8,20},{12,16},{16,12},{20,8},{24,4},{28,0},{1,29},{... | collective-permute-start | bytes 399368 | tf_op jit(solution)/shard_map/ppermute | solution.py:460
  116.7 1.6 collective-permute-start.11
  118.3 2.6 %collective-permute-start.19 = (s16[520,128]{1,0:T(8,128)(2,1)S(1)}, s16[520,128]{1,0:T(8,128)(2,1)S(1)}, u32[]{:S(2)}, u32[]{:S(2)}) collective-permute-start(s16[520,128]{1,0:T(8,128)(2,1)S(1)} %copy-done.30), channel_id=1, source_target_pairs={{0,12},{4,8},{8,4},{12,0},{16,28},{20,24},{24,20},{28,16},{1,13},{... | collective-permute-start | bytes 399368 | tf_op jit(solution)/shard_map/ppermute | solution.py:460
  120.9 4.3 %collective-permute-done.23.refs_6_ = s16[520,128]{1,0:T(8,128)(2,1)S(1)} collective-permute-done((s16[520,128]{1,0:T(8,128)(2,1)}, s16[520,128]{1,0:T(8,128)(2,1)S(1)}, u32[]{:S(2)}, u32[]{:S(2)}) %collective-permute-start.23) | collective-permute-done | bytes 133152 | tf_op jit(solution)/shard_map/ppermute | solution.py:460
  125.2 2.9 %fusion.1 = f32[]{:T(128)} fusion(f32[1025]{0:T(1024)S(1)} %fusion.5, f32[1025]{0:T(1024)S(1)} %get-tuple-element.160, f32[1025]{0:T(1024)S(1)} %get-tuple-element.161), kind=kLoop, calls=%fused_computation.2 | loop fusion | flops 6303749 | bytes 12304 | tf_op jit(solution)/shard_map/reduce_sum | solution.py:448
  128.8 0.9 collective-permute-start.29
  129.7 0.3 collective-permute-start.33
  130.0 3.3 %collective-permute-start.30 = (s16[520,128]{1,0:T(8,128)(2,1)}, s16[520,128]{1,0:T(8,128)(2,1)}, u32[]{:S(2)}, u32[]{:S(2)}) collective-permute-start(s16[520,128]{1,0:T(8,128)(2,1)} %get-tuple-element.141), channel_id=1, source_target_pairs={{0,8},{4,12},{8,0},{12,4},{16,24},{20,28},{24,16},{28,20},{1,9},{5... | collective-permute-start | bytes 399368 | tf_op jit(solution)/shard_map/ppermute | solution.py:460
  133.4 1.4 collective-permute-start.32
  134.8 0.8 collective-permute-start.34
  135.6 2.0 %slice.16 = bf16[4,8,16,16,128]{4,3,2,1,0:T(8,128)(2,1)S(1)} slice(bf16[4,8,17,16,128]{4,3,2,1,0:T(8,128)(2,1)} %bitcast.56), slice={[0:4], [0:8], [0:16], [0:16], [0:128]} | slice | bytes 4194304 | tf_op jit(solution)/shard_map/slice | solution.py:583
  137.5 0.9 slice.17
  138.4 0.6 copy.47
  139.1 0.5 copy.54
  139.6 2.6 %copy.45.refs_21_ = bf16[2048,512]{1,0:T(8,128)(2,1)} copy(bf16[2048,512]{0,1:T(8,128)(2,1)S(1)} %bitcast.54) | data formatting | bytes 4194304 | tf_op jit(solution)/shard_map/reshape | solution.py:583
  142.2 0.7 reshape.178.refs_22_
  142.9 0.3 collective-permute-done.32.refs_13_
  143.2 0.5 collective-permute-done.34.refs_15_
  143.7 13.2 %rows_back.1 = (f32[8192,128]{1,0:T(8,128)}, f32[32,8,128]{2,1,0:T(8,128)}) custom-call(s32[1]{0:T(128)} %bitcast.refs_0_, f32[1]{0:T(128)} %bitcast.3.refs_1_, s16[520,128]{1,0:T(8,128)(2,1)} %get-tuple-element.91.refs_2_, s16[520,128]{1,0:T(8,128)(2,1)} %copy-done.22, s16[520,128]{1,0:T(8,128)(2,1)} %copy-done.20, s16[520,128]{1,0:T(8,128)(2,1)} %copy-done.23, ...), custom_call_target="tpu_custom_call" | custom-call | tf_op jit(solution)/shard_map/rows_back/pallas_call | solution.py:593
  156.9 5.4 %all-to-all-start = ((f32[32,8,128]{2,1,0:T(8,128)}), f32[32,8,128]{2,1,0:T(8,128)S(1)}, u32[]{:S(2)}, u32[]{:S(2)}) async-start(f32[32,8,128]{2,1,0:T(8,128)} %get-tuple-element.152), calls=%async_computation | async-start | bytes 262144 | tf_op jit(solution)/shard_map/all_to_all | solution.py:628
  162.3 0.6 and_select_fusion.2.refs_0_
  162.9 1.0 fusion.3.refs_3_
  163.9 6.6 %all-to-all-done.refs_2_ = f32[32,8,128]{2,1,0:T(8,128)S(1)} async-done(((f32[32,8,128]{2,1,0:T(8,128)}), f32[32,8,128]{2,1,0:T(8,128)S(1)}, u32[]{:S(2)}, u32[]{:S(2)}) %all-to-all-start) | async-done | bytes 131104 | tf_op jit(solution)/shard_map/all_to_all | solution.py:628
  170.5 0.7 copy-done.1
  171.2 2.1 %factor_basis.1 = (f32[2,256]{1,0:T(2,128)}, f32[8,8]{1,0:T(8,128)}, f32[2,256]{1,0:T(2,128)}) custom-call(s32[8]{0:T(128)} %and_select_fusion.2.refs_0_, s32[1]{0:T(128)} %bitcast.26.refs_1_, f32[32,8,128]{2,1,0:T(8,128)} %copy-done.1, bf16[1024,256]{1,0:T(8,128)(2,1)} %fusion.3.refs_3_), custom_call_target="tpu_custom_call" | custom-call | tf_op jit(solution)/shard_map/factor_basis/pallas_call | solution.py:633
  (119 shorter events, 1.0 us)
Async XLA Ops:
  7.2 21.5 %copy-start.27 = (s32[256,1]{0,1:T(1,128)S(1)}, s32[256,1]{0,1:T(1,128)}, u32[]{:S(2)}) copy-start(s32[256,1]{0,1:T(1,128)} %param.15) | copy-start | bytes 3076
  7.2 21.7 %copy-start.28 = (s32[256]{0:T(256)S(1)}, s32[256]{0:T(256)}, u32[]{:S(2)}) copy-start(s32[256]{0:T(256)} %param.16) | copy-start | bytes 3076
  7.2 21.7 %copy-start.29 = (s32[256]{0:T(256)S(1)}, s32[256]{0:T(256)}, u32[]{:S(2)}) copy-start(s32[256]{0:T(256)} %param.17) | copy-start | bytes 3076
  7.2 128.4 %all-gather.3.cloned.1.call-start = ((), (), s32[]{:S(2)}) async-start(), calls=%async_computation.1 | async-start | bytes 2785280 | tf_op jit(solution)/shard_map/all_gather | solution.py:582
  17.7 56.5 %copy-start.35 = (s16[520,128]{1,0:T(8,128)(2,1)S(1)}, s16[520,128]{1,0:T(8,128)(2,1)}, u32[]{:S(2)}) copy-start(s16[520,128]{1,0:T(8,128)(2,1)} %get-tuple-element.98) | copy-start | bytes 399364
  17.7 56.6 %copy-start.34 = (s16[520,128]{1,0:T(8,128)(2,1)S(1)}, s16[520,128]{1,0:T(8,128)(2,1)}, u32[]{:S(2)}) copy-start(s16[520,128]{1,0:T(8,128)(2,1)} %get-tuple-element.114) | copy-start | bytes 399364
  17.7 58.6 %copy-start.33 = (s16[520,128]{1,0:T(8,128)(2,1)S(1)}, s16[520,128]{1,0:T(8,128)(2,1)}, u32[]{:S(2)}) copy-start(s16[520,128]{1,0:T(8,128)(2,1)} %get-tuple-element.123) | copy-start | bytes 399364
  17.7 83.7 %copy-start.26 = (f32[2]{0:T(128)S(1)}, f32[2]{0:T(128)}, u32[]{:S(2)}) copy-start(f32[2]{0:T(128)} %refs_1_.3) | copy-start | bytes 28
  17.8 10.9 %collective-permute-start = (s16[520,128]{1,0:T(8,128)(2,1)}, s16[520,128]{1,0:T(8,128)(2,1)S(1)}, u32[]{:S(2)}, u32[]{:S(2)}) collective-permute-start(s16[520,128]{1,0:T(8,128)(2,1)} %get-tuple-element.80), channel_id=1, source_target_pairs={{0,8},{4,12},{8,0},{12,4},{16,24},{20,28},{24,16},{28,20},{1,9},{5... | collective-permute-start | bytes 399368 | tf_op jit(solution)/shard_map/ppermute | solution.py:460
  20.9 11.0 %collective-permute-start.1 = (s16[520,128]{1,0:T(8,128)(2,1)}, s16[520,128]{1,0:T(8,128)(2,1)S(1)}, u32[]{:S(2)}, u32[]{:S(2)}) collective-permute-start(s16[520,128]{1,0:T(8,128)(2,1)} %get-tuple-element.84), channel_id=1, source_target_pairs={{0,28},{4,24},{8,20},{12,16},{16,12},{20,8},{24,4},{28,0},{1,29},{... | collective-permute-start | bytes 399368 | tf_op jit(solution)/shard_map/ppermute | solution.py:460
  24.3 9.1 %collective-permute-start.3 = (s16[520,128]{1,0:T(8,128)(2,1)}, s16[520,128]{1,0:T(8,128)(2,1)S(1)}, u32[]{:S(2)}, u32[]{:S(2)}) collective-permute-start(s16[520,128]{1,0:T(8,128)(2,1)} %get-tuple-element.87), channel_id=1, source_target_pairs={{0,24},{4,28},{8,16},{12,20},{16,8},{20,12},{24,0},{28,4},{1,25},{... | collective-permute-start | bytes 399368 | tf_op jit(solution)/shard_map/ppermute | solution.py:460
  25.6 19.2 %collective-permute-start.5 = (s16[520,128]{1,0:T(8,128)(2,1)}, s16[520,128]{1,0:T(8,128)(2,1)S(1)}, u32[]{:S(2)}, u32[]{:S(2)}) collective-permute-start(s16[520,128]{1,0:T(8,128)(2,1)} %get-tuple-element.89), channel_id=1, source_target_pairs={{0,16},{4,20},{8,24},{12,28},{16,0},{20,4},{24,8},{28,12},{1,17},{... | collective-permute-start | bytes 399368 | tf_op jit(solution)/shard_map/ppermute | solution.py:460
  26.4 23.3 %collective-permute-start.6 = (s16[520,128]{1,0:T(8,128)(2,1)}, s16[520,128]{1,0:T(8,128)(2,1)S(1)}, u32[]{:S(2)}, u32[]{:S(2)}) collective-permute-start(s16[520,128]{1,0:T(8,128)(2,1)} %get-tuple-element.90), channel_id=1, source_target_pairs={{0,20},{4,16},{8,28},{12,24},{16,4},{20,0},{24,12},{28,8},{1,21},{... | collective-permute-start | bytes 399368 | tf_op jit(solution)/shard_map/ppermute | solution.py:460
  28.7 29.4 %copy-start.2 = (s16[520,128]{1,0:T(8,128)(2,1)}, s16[520,128]{1,0:T(8,128)(2,1)S(1)}, u32[]{:S(2)}) copy-start(s16[520,128]{1,0:T(8,128)(2,1)S(1)} %collective-permute-done.refs_7_) | copy-start | bytes 399364
  31.9 26.3 %copy-start.3 = (s16[520,128]{1,0:T(8,128)(2,1)}, s16[520,128]{1,0:T(8,128)(2,1)S(1)}, u32[]{:S(2)}) copy-start(s16[520,128]{1,0:T(8,128)(2,1)S(1)} %collective-permute-done.1.refs_12_) | copy-start | bytes 399364
  31.9 26.3 %collective-permute-start.2 = (s16[520,128]{1,0:T(8,128)(2,1)}, s16[520,128]{1,0:T(8,128)(2,1)S(1)}, u32[]{:S(2)}, u32[]{:S(2)}) collective-permute-start(s16[520,128]{1,0:T(8,128)(2,1)} %get-tuple-element.85), channel_id=1, source_target_pairs={{0,4},{4,0},{8,12},{12,8},{16,20},{20,16},{24,28},{28,24},{1,5},{5... | collective-permute-start | bytes 399368 | tf_op jit(solution)/shard_map/ppermute | solution.py:460
  33.3 24.8 %copy-start.4 = (s16[520,128]{1,0:T(8,128)(2,1)}, s16[520,128]{1,0:T(8,128)(2,1)S(1)}, u32[]{:S(2)}) copy-start(s16[520,128]{1,0:T(8,128)(2,1)S(1)} %collective-permute-done.3.refs_11_) | copy-start | bytes 399364
  33.3 19.0 %collective-permute-start.4 = (s16[520,128]{1,0:T(8,128)(2,1)}, s16[520,128]{1,0:T(8,128)(2,1)S(1)}, u32[]{:S(2)}, u32[]{:S(2)}) collective-permute-start(s16[520,128]{1,0:T(8,128)(2,1)} %get-tuple-element.88), channel_id=1, source_target_pairs={{0,12},{4,8},{8,4},{12,0},{16,28},{20,24},{24,20},{28,16},{1,13},{... | collective-permute-start | bytes 399368 | tf_op jit(solution)/shard_map/ppermute | solution.py:460
  44.8 13.3 %copy-start.5 = (s16[520,128]{1,0:T(8,128)(2,1)}, s16[520,128]{1,0:T(8,128)(2,1)S(1)}, u32[]{:S(2)}) copy-start(s16[520,128]{1,0:T(8,128)(2,1)S(1)} %collective-permute-done.5.refs_9_) | copy-start | bytes 399364
  44.8 29.4 %collective-permute-start.7 = (s16[520,128]{1,0:T(8,128)(2,1)}, s16[520,128]{1,0:T(8,128)(2,1)S(1)}, u32[]{:S(2)}, u32[]{:S(2)}) collective-permute-start(s16[520,128]{1,0:T(8,128)(2,1)} %get-tuple-element.97), channel_id=1, source_target_pairs={{0,24},{4,28},{8,16},{12,20},{16,8},{20,12},{24,0},{28,4},{1,25},{... | collective-permute-start | bytes 399368 | tf_op jit(solution)/shard_map/ppermute | solution.py:460
  49.8 26.5 %collective-permute-start.20 = (s16[520,128]{1,0:T(8,128)(2,1)}, s16[520,128]{1,0:T(8,128)(2,1)S(1)}, u32[]{:S(2)}, u32[]{:S(2)}) collective-permute-start(s16[520,128]{1,0:T(8,128)(2,1)} %get-tuple-element.122), channel_id=1, source_target_pairs={{0,28},{4,24},{8,20},{12,16},{16,12},{20,8},{24,4},{28,0},{1,29},{... | collective-permute-start | bytes 399368 | tf_op jit(solution)/shard_map/ppermute | solution.py:460
  52.4 25.5 %collective-permute-start.24 = (s16[520,128]{1,0:T(8,128)(2,1)}, s16[520,128]{1,0:T(8,128)(2,1)S(1)}, u32[]{:S(2)}, u32[]{:S(2)}) collective-permute-start(s16[520,128]{1,0:T(8,128)(2,1)} %get-tuple-element.130), channel_id=1, source_target_pairs={{0,16},{4,20},{8,24},{12,28},{16,0},{20,4},{24,8},{28,12},{1,17},{... | collective-permute-start | bytes 399368 | tf_op jit(solution)/shard_map/ppermute | solution.py:460
  52.4 18.3 %collective-permute-start.12 = (s16[520,128]{1,0:T(8,128)(2,1)}, s16[520,128]{1,0:T(8,128)(2,1)S(1)}, u32[]{:S(2)}, u32[]{:S(2)}) collective-permute-start(s16[520,128]{1,0:T(8,128)(2,1)} %get-tuple-element.106), channel_id=1, source_target_pairs={{0,20},{4,16},{8,28},{12,24},{16,4},{20,0},{24,12},{28,8},{1,21},{... | collective-permute-start | bytes 399368 | tf_op jit(solution)/shard_map/ppermute | solution.py:460
  70.5 41.8 %copy-start.32 = (s16[520,128]{1,0:T(8,128)(2,1)S(1)}, s16[520,128]{1,0:T(8,128)(2,1)}, u32[]{:S(2)}) copy-start(s16[520,128]{1,0:T(8,128)(2,1)} %get-tuple-element.109) | copy-start | bytes 399364
  70.5 46.2 %copy-start.31 = (s16[520,128]{1,0:T(8,128)(2,1)S(1)}, s16[520,128]{1,0:T(8,128)(2,1)}, u32[]{:S(2)}) copy-start(s16[520,128]{1,0:T(8,128)(2,1)} %get-tuple-element.101) | copy-start | bytes 399364
  70.5 47.8 %copy-start.30 = (s16[520,128]{1,0:T(8,128)(2,1)S(1)}, s16[520,128]{1,0:T(8,128)(2,1)}, u32[]{:S(2)}) copy-start(s16[520,128]{1,0:T(8,128)(2,1)} %get-tuple-element.117) | copy-start | bytes 399364
  70.7 32.6 %copy-start.12 = (s16[520,128]{1,0:T(8,128)(2,1)}, s16[520,128]{1,0:T(8,128)(2,1)S(1)}, u32[]{:S(2)}) copy-start(s16[520,128]{1,0:T(8,128)(2,1)S(1)} %collective-permute-done.12.refs_7_) | copy-start | bytes 399364
  70.7 8.2 %collective-permute-start.13 = (bf16[17,16,128]{2,1,0:T(8,128)(2,1)}, bf16[17,16,128]{2,1,0:T(8,128)(2,1)S(1)}, u32[]{:S(2)}, u32[]{:S(2)}) collective-permute-start(bf16[17,16,128]{2,1,0:T(8,128)(2,1)} %get-tuple-element.107), channel_id=1, source_target_pairs={{0,28},{4,24},{8,20},{12,16},{16,12},{20,8},{24,4},{28,0},{1,29},{... | collective-permute-start | bytes 208904 | tf_op jit(solution)/shard_map/ppermute | solution.py:460
  74.2 29.1 %copy-start.9 = (s16[520,128]{1,0:T(8,128)(2,1)}, s16[520,128]{1,0:T(8,128)(2,1)S(1)}, u32[]{:S(2)}) copy-start(s16[520,128]{1,0:T(8,128)(2,1)S(1)} %collective-permute-done.7.refs_8_) | copy-start | bytes 399364
  74.2 10.0 %collective-permute-start.8 = (s16[520,128]{1,0:T(8,128)(2,1)S(1)}, s16[520,128]{1,0:T(8,128)(2,1)S(1)}, u32[]{:S(2)}, u32[]{:S(2)}) collective-permute-start(s16[520,128]{1,0:T(8,128)(2,1)S(1)} %copy-done.35), channel_id=1, source_target_pairs={{0,12},{4,8},{8,4},{12,0},{16,28},{20,24},{24,20},{28,16},{1,13},{... | collective-permute-start | bytes 399368 | tf_op jit(solution)/shard_map/ppermute | solution.py:460
  74.3 13.8 %collective-permute-start.16 = (s16[520,128]{1,0:T(8,128)(2,1)S(1)}, s16[520,128]{1,0:T(8,128)(2,1)S(1)}, u32[]{:S(2)}, u32[]{:S(2)}) collective-permute-start(s16[520,128]{1,0:T(8,128)(2,1)S(1)} %copy-done.34), channel_id=1, source_target_pairs={{0,8},{4,12},{8,0},{12,4},{16,24},{20,28},{24,16},{28,20},{1,9},{5... | collective-permute-start | bytes 399368 | tf_op jit(solution)/shard_map/ppermute | solution.py:460
  76.3 27.0 %copy-start.10 = (s16[520,128]{1,0:T(8,128)(2,1)}, s16[520,128]{1,0:T(8,128)(2,1)S(1)}, u32[]{:S(2)}) copy-start(s16[520,128]{1,0:T(8,128)(2,1)S(1)} %collective-permute-done.20.refs_9_) | copy-start | bytes 399364
  76.3 11.9 %collective-permute-start.21 = (s16[520,128]{1,0:T(8,128)(2,1)S(1)}, s16[520,128]{1,0:T(8,128)(2,1)S(1)}, u32[]{:S(2)}, u32[]{:S(2)}) collective-permute-start(s16[520,128]{1,0:T(8,128)(2,1)S(1)} %copy-done.33), channel_id=1, source_target_pairs={{0,4},{4,0},{8,12},{12,8},{16,20},{20,16},{24,28},{28,24},{1,5},{5... | collective-permute-start | bytes 399368 | tf_op jit(solution)/shard_map/ppermute | solution.py:460
  77.9 25.5 %copy-start.11 = (s16[520,128]{1,0:T(8,128)(2,1)}, s16[520,128]{1,0:T(8,128)(2,1)S(1)}, u32[]{:S(2)}) copy-start(s16[520,128]{1,0:T(8,128)(2,1)S(1)} %collective-permute-done.24.refs_6_) | copy-start | bytes 399364
  77.9 6.4 %collective-permute-start.25 = (bf16[17,16,128]{2,1,0:T(8,128)(2,1)}, bf16[17,16,128]{2,1,0:T(8,128)(2,1)S(1)}, u32[]{:S(2)}, u32[]{:S(2)}) collective-permute-start(bf16[17,16,128]{2,1,0:T(8,128)(2,1)} %get-tuple-element.131), channel_id=1, source_target_pairs={{0,24},{4,28},{8,16},{12,20},{16,8},{20,12},{24,0},{28,4},{1,25},{... | collective-permute-start | bytes 208904 | tf_op jit(solution)/shard_map/ppermute | solution.py:460
  78.9 11.3 %collective-permute-start.14 = (bf16[17,16,128]{2,1,0:T(8,128)(2,1)}, bf16[17,16,128]{2,1,0:T(8,128)(2,1)S(1)}, u32[]{:S(2)}, u32[]{:S(2)}) collective-permute-start(bf16[17,16,128]{2,1,0:T(8,128)(2,1)} %get-tuple-element.108), channel_id=1, source_target_pairs={{0,4},{4,0},{8,12},{12,8},{16,20},{20,16},{24,28},{28,24},{1,5},{5... | collective-permute-start | bytes 208904 | tf_op jit(solution)/shard_map/ppermute | solution.py:460
  84.3 8.5 %collective-permute-start.26 = (bf16[17,16,128]{2,1,0:T(8,128)(2,1)}, bf16[17,16,128]{2,1,0:T(8,128)(2,1)S(1)}, u32[]{:S(2)}, u32[]{:S(2)}) collective-permute-start(bf16[17,16,128]{2,1,0:T(8,128)(2,1)} %get-tuple-element.132), channel_id=1, source_target_pairs={{0,12},{4,8},{8,4},{12,0},{16,28},{20,24},{24,20},{28,16},{1,13},{... | collective-permute-start | bytes 208904 | tf_op jit(solution)/shard_map/ppermute | solution.py:460
  84.3 19.1 %copy-start.17 = (s16[520,128]{1,0:T(8,128)(2,1)}, s16[520,128]{1,0:T(8,128)(2,1)S(1)}, u32[]{:S(2)}) copy-start(s16[520,128]{1,0:T(8,128)(2,1)S(1)} %collective-permute-done.8.refs_5_) | copy-start | bytes 399364
  84.3 9.8 %collective-permute-start.9 = (bf16[17,16,128]{2,1,0:T(8,128)(2,1)}, bf16[17,16,128]{2,1,0:T(8,128)(2,1)S(1)}, u32[]{:S(2)}, u32[]{:S(2)}) collective-permute-start(bf16[17,16,128]{2,1,0:T(8,128)(2,1)} %get-tuple-element.99), channel_id=1, source_target_pairs={{0,20},{4,16},{8,28},{12,24},{16,4},{20,0},{24,12},{28,8},{1,21},{... | collective-permute-start | bytes 208904 | tf_op jit(solution)/shard_map/ppermute | solution.py:460
  88.2 15.2 %copy-start.18 = (s16[520,128]{1,0:T(8,128)(2,1)}, s16[520,128]{1,0:T(8,128)(2,1)S(1)}, u32[]{:S(2)}) copy-start(s16[520,128]{1,0:T(8,128)(2,1)S(1)} %collective-permute-done.16.refs_4_) | copy-start | bytes 399364
  88.2 5.9 %collective-permute-start.17 = (bf16[17,16,128]{2,1,0:T(8,128)(2,1)}, bf16[17,16,128]{2,1,0:T(8,128)(2,1)S(1)}, u32[]{:S(2)}, u32[]{:S(2)}) collective-permute-start(bf16[17,16,128]{2,1,0:T(8,128)(2,1)} %get-tuple-element.115), channel_id=1, source_target_pairs={{0,16},{4,20},{8,24},{12,28},{16,0},{20,4},{24,8},{28,12},{1,17},{... | collective-permute-start | bytes 208904 | tf_op jit(solution)/shard_map/ppermute | solution.py:460
  88.2 15.2 %copy-start.19 = (s16[520,128]{1,0:T(8,128)(2,1)}, s16[520,128]{1,0:T(8,128)(2,1)S(1)}, u32[]{:S(2)}) copy-start(s16[520,128]{1,0:T(8,128)(2,1)S(1)} %collective-permute-done.21.refs_3_) | copy-start | bytes 399364
  88.2 4.6 %collective-permute-start.22 = (bf16[17,16,128]{2,1,0:T(8,128)(2,1)}, bf16[17,16,128]{2,1,0:T(8,128)(2,1)S(1)}, u32[]{:S(2)}, u32[]{:S(2)}) collective-permute-start(bf16[17,16,128]{2,1,0:T(8,128)(2,1)} %get-tuple-element.124), channel_id=1, source_target_pairs={{0,8},{4,12},{8,0},{12,4},{16,24},{20,28},{24,16},{28,20},{1,9},{5... | collective-permute-start | bytes 208904 | tf_op jit(solution)/shard_map/ppermute | solution.py:460
  95.1 19.3 %collective-permute-start.27 = (s16[520,128]{1,0:T(8,128)(2,1)}, s16[520,128]{1,0:T(8,128)(2,1)S(1)}, u32[]{:S(2)}, u32[]{:S(2)}) collective-permute-start(s16[520,128]{1,0:T(8,128)(2,1)} %get-tuple-element.133), channel_id=1, source_target_pairs={{0,20},{4,16},{8,28},{12,24},{16,4},{20,0},{24,12},{28,8},{1,21},{... | collective-permute-start | bytes 399368 | tf_op jit(solution)/shard_map/ppermute | solution.py:460
  96.6 20.1 %collective-permute-start.10 = (s16[520,128]{1,0:T(8,128)(2,1)}, s16[520,128]{1,0:T(8,128)(2,1)S(1)}, u32[]{:S(2)}, u32[]{:S(2)}) collective-permute-start(s16[520,128]{1,0:T(8,128)(2,1)} %get-tuple-element.100), channel_id=1, source_target_pairs={{0,28},{4,24},{8,20},{12,16},{16,12},{20,8},{24,4},{28,0},{1,29},{... | collective-permute-start | bytes 399368 | tf_op jit(solution)/shard_map/ppermute | solution.py:460
  99.0 19.3 %collective-permute-start.18 = (s16[520,128]{1,0:T(8,128)(2,1)}, s16[520,128]{1,0:T(8,128)(2,1)S(1)}, u32[]{:S(2)}, u32[]{:S(2)}) collective-permute-start(s16[520,128]{1,0:T(8,128)(2,1)} %get-tuple-element.116), channel_id=1, source_target_pairs={{0,24},{4,28},{8,16},{12,20},{16,8},{20,12},{24,0},{28,4},{1,25},{... | collective-permute-start | bytes 399368 | tf_op jit(solution)/shard_map/ppermute | solution.py:460
  101.4 23.8 %collective-permute-start.23 = (s16[520,128]{1,0:T(8,128)(2,1)}, s16[520,128]{1,0:T(8,128)(2,1)S(1)}, u32[]{:S(2)}, u32[]{:S(2)}) collective-permute-start(s16[520,128]{1,0:T(8,128)(2,1)} %get-tuple-element.125), channel_id=1, source_target_pairs={{0,16},{4,20},{8,24},{12,28},{16,0},{20,4},{24,8},{28,12},{1,17},{... | collective-permute-start | bytes 399368 | tf_op jit(solution)/shard_map/ppermute | solution.py:460
  112.3 17.4 %collective-permute-start.15 = (s16[520,128]{1,0:T(8,128)(2,1)S(1)}, s16[520,128]{1,0:T(8,128)(2,1)S(1)}, u32[]{:S(2)}, u32[]{:S(2)}) collective-permute-start(s16[520,128]{1,0:T(8,128)(2,1)S(1)} %copy-done.32), channel_id=1, source_target_pairs={{0,8},{4,12},{8,0},{12,4},{16,24},{20,28},{24,16},{28,20},{1,9},{5... | collective-permute-start | bytes 399368 | tf_op jit(solution)/shard_map/ppermute | solution.py:460
  114.4 24.6 %copy-start.13 = (s16[520,128]{1,0:T(8,128)(2,1)}, s16[520,128]{1,0:T(8,128)(2,1)S(1)}, u32[]{:S(2)}) copy-start(s16[520,128]{1,0:T(8,128)(2,1)S(1)} %collective-permute-done.27.refs_7_) | copy-start | bytes 399364
  114.4 14.4 %collective-permute-start.28 = (s16[520,128]{1,0:T(8,128)(2,1)}, s16[520,128]{1,0:T(8,128)(2,1)S(1)}, u32[]{:S(2)}, u32[]{:S(2)}) collective-permute-start(s16[520,128]{1,0:T(8,128)(2,1)} %get-tuple-element.138), channel_id=1, source_target_pairs={{0,28},{4,24},{8,20},{12,16},{16,12},{20,8},{24,4},{28,0},{1,29},{... | collective-permute-start | bytes 399368 | tf_op jit(solution)/shard_map/ppermute | solution.py:460
  116.7 22.2 %copy-start.14 = (s16[520,128]{1,0:T(8,128)(2,1)}, s16[520,128]{1,0:T(8,128)(2,1)S(1)}, u32[]{:S(2)}) copy-start(s16[520,128]{1,0:T(8,128)(2,1)S(1)} %collective-permute-done.10.refs_9_) | copy-start | bytes 399364
  116.7 13.3 %collective-permute-start.11 = (s16[520,128]{1,0:T(8,128)(2,1)S(1)}, s16[520,128]{1,0:T(8,128)(2,1)S(1)}, u32[]{:S(2)}, u32[]{:S(2)}) collective-permute-start(s16[520,128]{1,0:T(8,128)(2,1)S(1)} %copy-done.31), channel_id=1, source_target_pairs={{0,4},{4,0},{8,12},{12,8},{16,20},{20,16},{24,28},{28,24},{1,5},{5... | collective-permute-start | bytes 399368 | tf_op jit(solution)/shard_map/ppermute | solution.py:460
  118.3 20.7 %copy-start.15 = (s16[520,128]{1,0:T(8,128)(2,1)}, s16[520,128]{1,0:T(8,128)(2,1)S(1)}, u32[]{:S(2)}) copy-start(s16[520,128]{1,0:T(8,128)(2,1)S(1)} %collective-permute-done.18.refs_8_) | copy-start | bytes 399364
  118.3 16.5 %collective-permute-start.19 = (s16[520,128]{1,0:T(8,128)(2,1)S(1)}, s16[520,128]{1,0:T(8,128)(2,1)S(1)}, u32[]{:S(2)}, u32[]{:S(2)}) collective-permute-start(s16[520,128]{1,0:T(8,128)(2,1)S(1)} %copy-done.30), channel_id=1, source_target_pairs={{0,12},{4,8},{8,4},{12,0},{16,28},{20,24},{24,20},{28,16},{1,13},{... | collective-permute-start | bytes 399368 | tf_op jit(solution)/shard_map/ppermute | solution.py:460
  125.2 13.8 %copy-start.16 = (s16[520,128]{1,0:T(8,128)(2,1)}, s16[520,128]{1,0:T(8,128)(2,1)S(1)}, u32[]{:S(2)}) copy-start(s16[520,128]{1,0:T(8,128)(2,1)S(1)} %collective-permute-done.23.refs_6_) | copy-start | bytes 399364
  125.2 8.2 %collective-permute-start.31 = (s16[520,128]{1,0:T(8,128)(2,1)}, s16[520,128]{1,0:T(8,128)(2,1)S(1)}, u32[]{:S(2)}, u32[]{:S(2)}) collective-permute-start(s16[520,128]{1,0:T(8,128)(2,1)} %get-tuple-element.144), channel_id=1, source_target_pairs={{0,24},{4,28},{8,16},{12,20},{16,8},{20,12},{24,0},{28,4},{1,25},{... | collective-permute-start | bytes 399368 | tf_op jit(solution)/shard_map/ppermute | solution.py:460
  128.8 10.2 %copy-start.21 = (s16[520,128]{1,0:T(8,128)(2,1)}, s16[520,128]{1,0:T(8,128)(2,1)S(1)}, u32[]{:S(2)}) copy-start(s16[520,128]{1,0:T(8,128)(2,1)S(1)} %collective-permute-done.28.refs_17_) | copy-start | bytes 399364
  128.8 14.1 %collective-permute-start.29 = (s16[520,128]{1,0:T(8,128)(2,1)}, s16[520,128]{1,0:T(8,128)(2,1)S(1)}, u32[]{:S(2)}, u32[]{:S(2)}) collective-permute-start(s16[520,128]{1,0:T(8,128)(2,1)} %get-tuple-element.139), channel_id=1, source_target_pairs={{0,4},{4,0},{8,12},{12,8},{16,20},{20,16},{24,28},{28,24},{1,5},{5... | collective-permute-start | bytes 399368 | tf_op jit(solution)/shard_map/ppermute | solution.py:460
  129.7 9.3 %copy-start.20 = (s16[520,128]{1,0:T(8,128)(2,1)}, s16[520,128]{1,0:T(8,128)(2,1)S(1)}, u32[]{:S(2)}) copy-start(s16[520,128]{1,0:T(8,128)(2,1)S(1)} %collective-permute-done.15.refs_4_) | copy-start | bytes 399364
  129.7 13.2 %collective-permute-start.33 = (s16[520,128]{1,0:T(8,128)(2,1)}, s16[520,128]{1,0:T(8,128)(2,1)}, u32[]{:S(2)}, u32[]{:S(2)}) collective-permute-start(s16[520,128]{1,0:T(8,128)(2,1)} %get-tuple-element.147), channel_id=1, source_target_pairs={{0,16},{4,20},{8,24},{12,28},{16,0},{20,4},{24,8},{28,12},{1,17},{... | collective-permute-start | bytes 399368 | tf_op jit(solution)/shard_map/ppermute | solution.py:460
  130.0 12.9 %collective-permute-start.30 = (s16[520,128]{1,0:T(8,128)(2,1)}, s16[520,128]{1,0:T(8,128)(2,1)}, u32[]{:S(2)}, u32[]{:S(2)}) collective-permute-start(s16[520,128]{1,0:T(8,128)(2,1)} %get-tuple-element.141), channel_id=1, source_target_pairs={{0,8},{4,12},{8,0},{12,4},{16,24},{20,28},{24,16},{28,20},{1,9},{5... | collective-permute-start | bytes 399368 | tf_op jit(solution)/shard_map/ppermute | solution.py:460
  133.4 9.8 %collective-permute-start.32 = (s16[520,128]{1,0:T(8,128)(2,1)}, s16[520,128]{1,0:T(8,128)(2,1)}, u32[]{:S(2)}, u32[]{:S(2)}) collective-permute-start(s16[520,128]{1,0:T(8,128)(2,1)} %get-tuple-element.145), channel_id=1, source_target_pairs={{0,12},{4,8},{8,4},{12,0},{16,28},{20,24},{24,20},{28,16},{1,13},{... | collective-permute-start | bytes 399368 | tf_op jit(solution)/shard_map/ppermute | solution.py:460
  134.8 8.9 %collective-permute-start.34 = (s16[520,128]{1,0:T(8,128)(2,1)}, s16[520,128]{1,0:T(8,128)(2,1)}, u32[]{:S(2)}, u32[]{:S(2)}) collective-permute-start(s16[520,128]{1,0:T(8,128)(2,1)} %get-tuple-element.149), channel_id=1, source_target_pairs={{0,20},{4,16},{8,28},{12,24},{16,4},{20,0},{24,12},{28,8},{1,21},{... | collective-permute-start | bytes 399368 | tf_op jit(solution)/shard_map/ppermute | solution.py:460
  156.9 13.6 %all-to-all-start = ((f32[32,8,128]{2,1,0:T(8,128)}), f32[32,8,128]{2,1,0:T(8,128)S(1)}, u32[]{:S(2)}, u32[]{:S(2)}) async-start(f32[32,8,128]{2,1,0:T(8,128)} %get-tuple-element.152), calls=%async_computation | async-start | bytes 262144 | tf_op jit(solution)/shard_map/all_to_all | solution.py:628
  (9 other events, 36.0 us)
Sparse Core Ops, SparseCore 0:
  95.2 21.8 all-gather.2

commit v3 on v2

--- a/solution.py
+++ b/solution.py
@@ -89,6 +89,25 @@
 
 def scales(exponent):
     return jnp.exp2(exponent.astype(jnp.int32).astype(F32) * (1.0 / STEPS)) * (1.0 / TOP)
+
+
+def pack_kernel(source_ref, prints_ref, code_ref, packed, semaphore):
+    slabs, share = packed.shape[0], packed.shape[1] - 1
+
+    def begin(at, carry):
+        for slab in range(slabs):
+            pltpu.make_async_copy(
+                prints_ref.at[source_ref[slab * share + at]], packed.at[slab, at], semaphore
+            ).start()
+        return carry
+
+    lax.fori_loop(0, share, begin, 0)
+    codes = jnp.broadcast_to(code_ref[...], packed.shape[2:]).astype(BF16)
+    for slab in range(slabs):
+        packed[slab, share] = codes
+    pltpu.make_async_copy(
+        packed.at[:, pl.ds(0, share)], packed.at[:, pl.ds(0, share)], semaphore
+    ).wait()
 
 
 def rows_kernel(slabs, chunks, me_ref, x_ref, lead_ref, trail_ref, turn_ref, *rest):
@@ -146,35 +165,8 @@
                 out[2 * rows:, :] = marks[chunk, slab].astype(jnp.int32).astype(I16)
 
 
-def pack_copies(slabs, me, source_ref, prints_ref, packed, semaphore, act):
-    for hop in range(slabs):
-        share = packed[hop].shape[0] - 1
-
-        def one(at, carry, hop=hop, share=share):
-            source = source_ref[(me ^ hop) * share + at]
-
-            @pl.when(source >= 0)
-            def _():
-                act(pltpu.make_async_copy(prints_ref.at[source], packed[hop].at[at], semaphore))
-
-            return carry
-
-        lax.fori_loop(0, share, one, 0)
-
-
-def columns_kernel(slabs, chunk, length, packs, me_ref, corr_ref, *rest):
+def columns_kernel(slabs, chunk, length, me_ref, corr_ref, *rest):
     me = me_ref[0]
-    if packs:
-        (source_ref, prints_ref, code_ref), rest = rest[:3], rest[3:]
-        packed, semaphore = rest[-6 - slabs:-6], rest[-6]
-        rest = rest[:-6 - slabs] + rest[-5:]
-        for hop in range(slabs):
-            share = packed[hop].shape[0] - 1
-            packed[hop][:share] = jnp.zeros_like(packed[hop][:share])
-            packed[hop][share] = code_ref[me ^ hop]
-        pack_copies(
-            slabs, me, source_ref, prints_ref, packed, semaphore, lambda copy: copy.start()
-        )
     ins, rest = rest[:slabs], rest[slabs:]
     back_lead, back_trail, lead, trail, turn_ref = rest[:5]
     outs, (stack, scale, field, high, low) = rest[5:5 + slabs], rest[5 + slabs:]
@@ -271,10 +263,6 @@
     for hop in range(slabs):
         outs[hop][:2 * rows, :] = stack[me ^ hop]
         outs[hop][2 * rows:, :] = scale[me ^ hop].astype(jnp.int32).astype(I16)
-    if packs:
-        pack_copies(
-            slabs, me, source_ref, prints_ref, packed, semaphore, lambda copy: copy.wait()
-        )
 
 
 def finish_kernel(slabs, chunks, me_ref, gain_ref, *rest):
@@ -448,16 +436,19 @@
     return jnp.sum(root * root * root * (weight_y[:, None] * weight_x[None, :]))
 
 
+def send(value, axis, hop, sent):
+    pairs = [(source, source ^ hop) for source in range(lax.axis_size(axis))]
+    if len(sent) >= WINDOW:
+        value, _ = lax.optimization_barrier((value, sent[-WINDOW]))
+    return lax.ppermute(value, axis, pairs)
+
+
 def exchange(blocks, sent):
     slabs = len(blocks)
-    order = sorted(range(1, slabs), key=lambda hop: (-(hop * 2 // slabs), -(hop * 4 // slabs % 2)))
-    arrived = [blocks[0]] + [None] * (slabs - 1)
-    for hop in order:
-        pairs = [(source, source ^ hop) for source in range(slabs)]
-        block = blocks[hop]
-        if len(sent) >= WINDOW:
-            block, _ = lax.optimization_barrier((block, sent[-WINDOW]))
-        arrived[hop] = lax.ppermute(block, "grid", pairs)
+    far, near = range(slabs - 1, slabs // 2 - 1, -1), range(slabs // 2 - 1, 0, -1)
+    arrived = list(blocks)
+    for hop in [hop for pair in zip(far, near) for hop in pair] + [far[-1]]:
+        arrived[hop] = send(blocks[hop], "grid", hop, sent)
         sent.append(arrived[hop])
     return arrived
 
@@ -477,51 +468,13 @@
     turn_x = jnp.asarray(twiddles(width))
     turn_y = jnp.asarray(twiddles(height).T.copy())
     me_list = me.reshape(1).astype(jnp.int32)
-    column_tiles = width // LANES
-    flat = (
-        probes.reshape(rows, each, column_tiles, LANES)
-        .transpose(0, 2, 1, 3)
-        .reshape(rows * each * column_tiles, LANES)
-    )
-    payload = jax.ShapeDtypeStruct((2 * rows + RADIX, cut), I16)
-
-    def whole(shape):
-        return pl.BlockSpec(shape, lambda step: (0,) * len(shape))
-
-    sent = pl.pallas_call(
-        lambda *refs: rows_kernel(slabs, chunks, *refs),
-        grid=(rows // tile,),
-        in_specs=[
-            smem(),
-            pl.BlockSpec((tile * each * column_tiles, LANES), lambda step: (step, 0)),
-            whole(lead.shape),
-            whole(trail.shape),
-            whole(turn_x.shape),
-        ],
-        out_specs=[whole(payload.shape)] * (chunks * slabs),
-        out_shape=[payload] * (chunks * slabs),
-        scratch_shapes=[
-            pltpu.VMEM((chunks, slabs, 2 * rows, cut), I16),
-            pltpu.VMEM((chunks, slabs, RADIX, cut), F32),
-            pltpu.VMEM((RADIX * tile, 2 * short), BF16),
-            pltpu.VMEM((RADIX * tile, 2 * short), BF16),
-        ],
-        compiler_params=params(),
-        name="rows_forward",
-    )(me_list, flat, lead, trail, turn_x)
-
-    history = []
-    arrived = []
-    for chunk in range(chunks):
-        arrived.append(exchange(sent[chunk * slabs:(chunk + 1) * slabs], history))
-
     read_count, band_rows, tile_cols = footprints.shape
     band_count = rows // band_rows
     tile_count = width // tile_cols
     capacity = 2 * read_count // slabs
     share = capacity // lanes_q
     slots = slabs * capacity
-    target, _ = lax.optimization_barrier((reading_slab[:, 0], history[slabs // 2]))
+    target = reading_slab[:, 0]
     reading = jnp.arange(read_count, dtype=jnp.int32)
     onehot = (target[:, None] == jnp.arange(slabs, dtype=jnp.int32)[None, :]).astype(F32)
     before = (reading[:, None] > reading[None, :]).astype(F32)
@@ -537,24 +490,70 @@
     found = jnp.max(
         jnp.where(wanted[:, None] == place[None, :], (reading * blocks + code)[None, :], -1), axis=1
     )
-    source = jnp.where(found < 0, -1, found // blocks)
-    codes = jnp.where(found < 0, 0, found % blocks).astype(BF16).reshape(slabs, 1, share)
-    codes = jnp.pad(codes, ((0, 0), (0, band_rows - 1), (0, tile_cols - share)))
+    source = jnp.maximum(found, 0) // blocks
+    codes = jnp.where(found < 0, -1, found % blocks).astype(F32).reshape(1, slabs * share)
+
+    packed = pl.pallas_call(
+        pack_kernel,
+        in_specs=[smem(), pl.BlockSpec(memory_space=pl.ANY), vmem()],
+        out_specs=vmem(),
+        out_shape=jax.ShapeDtypeStruct((slabs, share + 1, band_rows, tile_cols), BF16),
+        scratch_shapes=[pltpu.SemaphoreType.DMA],
+        compiler_params=params(),
+        name="pack_prints",
+    )(source, footprints, codes)
+    gathered = lax.all_to_all(packed, "grid", split_axis=0, concat_axis=0, tiled=True)
+    me_list, _ = lax.optimization_barrier((me_list, packed))
+    column_tiles = width // LANES
+    flat = (
+        probes.reshape(rows, each, column_tiles, LANES)
+        .transpose(0, 2, 1, 3)
+        .reshape(rows * each * column_tiles, LANES)
+    )
+    payload = jax.ShapeDtypeStruct((2 * rows + RADIX, cut), I16)
+
+    def whole(shape):
+        return pl.BlockSpec(shape, lambda step: (0,) * len(shape))
+
+    sent = pl.pallas_call(
+        lambda *refs: rows_kernel(slabs, chunks, *refs),
+        grid=(rows // tile,),
+        in_specs=[
+            smem(),
+            pl.BlockSpec((tile * each * column_tiles, LANES), lambda step: (step, 0)),
+            whole(lead.shape),
+            whole(trail.shape),
+            whole(turn_x.shape),
+        ],
+        out_specs=[whole(payload.shape)] * (chunks * slabs),
+        out_shape=[payload] * (chunks * slabs),
+        scratch_shapes=[
+            pltpu.VMEM((chunks, slabs, 2 * rows, cut), I16),
+            pltpu.VMEM((chunks, slabs, RADIX, cut), F32),
+            pltpu.VMEM((RADIX * tile, 2 * short), BF16),
+            pltpu.VMEM((RADIX * tile, 2 * short), BF16),
+        ],
+        compiler_params=params(),
+        name="rows_forward",
+    )(me_list, flat, lead, trail, turn_x)
+
+    gathered, _ = lax.optimization_barrier((gathered, sent[0]))
+    gathered = lax.all_gather(gathered, "probe", axis=0, tiled=False)
+    history = []
+    arrived = []
+    for chunk in range(chunks):
+        arrived.append(exchange(sent[chunk * slabs:(chunk + 1) * slabs], history))
 
     halfway = []
     group = 256 // cut if cut % LANES == 0 else 1
-    parcel = jax.ShapeDtypeStruct((share + 1, band_rows, tile_cols), BF16)
     for chunk in range(chunks):
-        packs = chunk == 0
         results = pl.pallas_call(
-            lambda *refs, chunk=chunk, packs=packs: columns_kernel(slabs, chunk, height, packs, *refs),
+            lambda *refs, chunk=chunk: columns_kernel(slabs, chunk, height, *refs),
             in_specs=[smem(), smem()]
-            + ([smem(), pl.BlockSpec(memory_space=pl.ANY), vmem()] if packs else [])
             + [vmem()] * (slabs + 5),
-            out_specs=[vmem()] * (2 * slabs if packs else slabs),
-            out_shape=[payload] * slabs + ([parcel] * slabs if packs else []),
-            scratch_shapes=([pltpu.SemaphoreType.DMA] if packs else [])
-            + [
+            out_specs=[vmem()] * slabs,
+            out_shape=[payload] * slabs,
+            scratch_shapes=[
                 pltpu.VMEM((slabs, 2 * rows, cut), I16),
                 pltpu.VMEM((slabs, RADIX, cut), F32),
                 pltpu.VMEM((2, height, cut), F32),
@@ -566,7 +565,6 @@
         )(
             me_list,
             corr_lengths,
-            *([source, footprints, codes] if packs else []),
             *arrived[chunk],
             lead,
             trail,
@@ -574,20 +572,17 @@
             back_trail,
             turn_y,
         )
-        halfway.append(list(results[:slabs]))
-        if packs:
-            parcels = results[slabs:]
-
-    shared = jnp.stack(exchange(parcels, history))
-    gathered = lax.all_gather(shared, "probe", axis=0, tiled=False)
-    prints = gathered[:, :, :share].transpose(3, 4, 1, 0, 2).reshape(band_rows * tile_cols, slots)
-    index = gathered[:, :, share, 0, :share].transpose(1, 0, 2).reshape(1, slots).astype(jnp.int32)
+        halfway.append(list(results))
 
     gain = lax.rsqrt(filter_power(corr_lengths, height, width) / (height * width)) / (height * width)
 
     returned = []
     for results in halfway:
         returned += exchange(results, history)
+
+    prints = gathered[:, :, :share].transpose(3, 4, 1, 0, 2).reshape(band_rows * tile_cols, slots)
+    index = lax.dynamic_slice_in_dim(gathered[:, :, share, 0], me * share, share, 2)
+    index = index.transpose(1, 0, 2).reshape(1, slots).astype(jnp.int32)
 
     group_count = slabs * lanes_q
     smoothed, values = pl.pallas_call(
@@ -626,8 +621,8 @@
     )
 
     everyone = lax.all_to_all(values, ("grid", "probe"), split_axis=0, concat_axis=0, tiled=True)
-    offset = (me ^ jnp.arange(slabs, dtype=jnp.int32)) * capacity
-    lane_of = target * LANES + (me ^ target) * capacity % LANES + slot
+    offset = jnp.full((slabs,), me * capacity, jnp.int32)
+    lane_of = target * LANES + me * capacity % LANES + slot
     pick = (jnp.arange(slabs * LANES, dtype=jnp.int32)[:, None] == lane_of[None, :]).astype(BF16)
     probe_count = each * lanes_q
     sketch, factor, basis = pl.pallas_call(

time: 180 us -> 173 us (0.961)
  starting transfers between devices: 73.4 us -> 56 us
  waiting for transfers between devices: 26.5 us -> 37.6 us
  local copies, waits for them, and re-layouts: 11.7 us -> 9.45 us
    ppermute x35 -> x28, starting transfers between devices: 68 us -> 39.8 us  [send(): return lax.ppermute(value, axis, pairs)]
    all_to_all x0 -> x1, starting transfers between devices: none -> 7.29 us  [local(): lax.all_to_all(packed, 'grid', split_axis=0, concat_axis=0, tiled=True)]
    all_to_all x0 -> x1, waiting for transfers between devices: none -> 5.53 us  [local(): lax.all_to_all(packed, 'grid', split_axis=0, concat_axis=0, tiled=True)]
    ppermute x35 -> x28, waiting for transfers between devices: 19.9 us -> 24.8 us  [send(): return lax.ppermute(value, axis, pairs)]
    all_to_all x1, starting transfers between devices: 5.38 us -> 8.83 us  [local(): lax.all_to_all(values, ('grid', 'probe'), split_axis=0, concat_axis=0, ti...]
    unnamed x81 -> x56, local copies, waits for them, and re-layouts: 4.28 us -> 2.12 us
    pallas_call x2 -> x3, Pallas kernels: 20.7 us -> 20.7 us  [the longest x2 17.9 us: local(): pl.pallas_call(lambda *refs, chunk=chunk: columns_kernel(slabs, chunk, he...]
  transfers between devices with their start and end apart: 37 -> 31, of which waited for: 13 -> 11; matrix products, arithmetic and copies ran while one was open for 8% -> 7% of each run, Pallas kernels for 11% -> 16%
where the time goes in v3:
time: 173 us
  starting transfers between devices  56 us (32%)
  Pallas kernels  46.3 us (27%)
  waiting for transfers between devices  37.6 us (22%)
  between operations  16.4 us (9%)
  local copies, waits for them, and re-layouts  9.45 us (5%)
  other arithmetic  5.91 us (3%)
    ppermute x28, starting transfers between devices, send(): return lax.ppermute(value, axis, pairs)  39.8 us
    ppermute x28, waiting for transfers between devices, send(): return lax.ppermute(value, axis, pairs)  24.8 us
    pallas_call x2, Pallas kernels, local(): pl.pallas_call(lambda *refs, chunk=chunk: columns_kernel(slabs, chunk, he...  17.9 us
    pallas_call x1, Pallas kernels, local(): pl.pallas_call(lambda *refs: finish_kernel(slabs, chunks, *refs), grid=(r...  13 us
    pallas_call x1, Pallas kernels, local(): pl.pallas_call(lambda *refs: rows_kernel(slabs, chunks, *refs), grid=(row...  10.5 us
    all_to_all x1, starting transfers between devices, local(): lax.all_to_all(values, ('grid', 'probe'), split_axis=0, concat_axis=0, ti...  8.83 us
    all_to_all x1, starting transfers between devices, local(): lax.all_to_all(packed, 'grid', split_axis=0, concat_axis=0, tiled=True)  7.29 us
    all_to_all x1, waiting for transfers between devices, local(): lax.all_to_all(values, ('grid', 'probe'), split_axis=0, concat_axis=0, ti...  7.19 us
  transfers between devices with their start and end apart: 31, of which 11 were waited for; matrix products, arithmetic and copies ran while one was open for 7% of the time, Pallas kernels for 16%

profile of v3, /device:TPU:0, one launch (start us, length us, event | category | flops | bytes accessed | tf_op | source)
XLA Modules:
  0.0 172.6 jit_solution(8234229084634765313)
XLA Ops:
  7.2 0.9 fusion.2
  8.1 0.1 iota_add_fusion
  8.2 0.1 add.113
  8.3 0.7 add_add_fusion
  9.0 0.2 select_reduce_fusion
  9.2 0.5 and_select_fusion.1.source_ref
  9.7 0.5 fusion.8.code_ref
  10.2 2.8 %pack_prints.1 = bf16[8,17,16,128]{3,2,1,0:T(8,128)(2,1)} custom-call(s32[128]{0:T(128)} %and_select_fusion.1.source_ref, bf16[256,16,128]{2,1,0:T(8,128)(2,1)} %prints_ref.1, f32[1,128]{1,0:T(1,128)} %fusion.8.code_ref), custom_call_target="tpu_custom_call" | custom-call | tf_op jit(solution)/shard_map/pack_prints/pallas_call | solution.py:496
  13.1 7.3 %all-to-all-start = ((bf16[8,17,16,128]{3,2,1,0:T(8,128)(2,1)}), bf16[8,17,16,128]{3,2,1,0:T(8,128)(2,1)S(1)}, u32[]{:S(2)}, u32[]{:S(2)}) async-start(bf16[8,17,16,128]{3,2,1,0:T(8,128)(2,1)} %pack_prints.1), calls=%async_computation | async-start | bytes 1114112 | tf_op jit(solution)/shard_map/all_to_all | solution.py:505
  20.4 0.0 all-gather.3.cloned.1.call-start
  20.4 10.5 %rows_forward.1 = (s16[520,128]{1,0:T(8,128)(2,1)}, s16[520,128]{1,0:T(8,128)(2,1)}, s16[520,128]{1,0:T(8,128)(2,1)}, s16[520,128]{1,0:T(8,128)(2,1)}, s16[520,1...) custom-call(s32[1]{0:T(128)} %bitcast.refs_0_, ...), custom_call_target="tpu_custom_call" | custom-call | tf_op jit(solution)/shard_map/rows_forward/pallas_call | solution.py:518
  30.9 5.5 %all-to-all-done = bf16[8,17,16,128]{3,2,1,0:T(8,128)(2,1)S(1)} async-done(((bf16[8,17,16,128]{3,2,1,0:T(8,128)(2,1)}), bf16[8,17,16,128]{3,2,1,0:T(8,128)(2,1)S(1)}, u32[]{:S(2)}, u32[]{:S(2)}) %all-to-all-start) | async-done | bytes 557088 | tf_op jit(solution)/shard_map/all_to_all | solution.py:505
  36.5 0.8 copy-done
  37.3 2.4 %collective-permute-start = (s16[520,128]{1,0:T(8,128)(2,1)}, s16[520,128]{1,0:T(8,128)(2,1)S(1)}, u32[]{:S(2)}, u32[]{:S(2)}) collective-permute-start(s16[520,128]{1,0:T(8,128)(2,1)} %get-tuple-element.69), channel_id=1, source_target_pairs={{0,28},{4,24},{8,20},{12,16},{16,12},{20,8},{24,4},{28,0},{1,29},{... | collective-permute-start | bytes 399368 | tf_op jit(solution)/shard_map/ppermute | solution.py:443
  39.7 2.3 %collective-permute-start.6 = (s16[520,128]{1,0:T(8,128)(2,1)}, s16[520,128]{1,0:T(8,128)(2,1)S(1)}, u32[]{:S(2)}, u32[]{:S(2)}) collective-permute-start(s16[520,128]{1,0:T(8,128)(2,1)} %get-tuple-element.76), channel_id=1, source_target_pairs={{0,24},{4,28},{8,16},{12,20},{16,8},{20,12},{24,0},{28,4},{1,25},{... | collective-permute-start | bytes 399368 | tf_op jit(solution)/shard_map/ppermute | solution.py:443
  42.1 2.1 %collective-permute-start.2 = (s16[520,128]{1,0:T(8,128)(2,1)}, s16[520,128]{1,0:T(8,128)(2,1)S(1)}, u32[]{:S(2)}, u32[]{:S(2)}) collective-permute-start(s16[520,128]{1,0:T(8,128)(2,1)} %get-tuple-element.71), channel_id=1, source_target_pairs={{0,8},{4,12},{8,0},{12,4},{16,24},{20,28},{24,16},{28,20},{1,9},{5... | collective-permute-start | bytes 399368 | tf_op jit(solution)/shard_map/ppermute | solution.py:443
  44.1 0.9 collective-permute-start.5
  45.0 1.9 %collective-permute-done.refs_9_ = s16[520,128]{1,0:T(8,128)(2,1)S(1)} collective-permute-done((s16[520,128]{1,0:T(8,128)(2,1)}, s16[520,128]{1,0:T(8,128)(2,1)S(1)}, u32[]{:S(2)}, u32[]{:S(2)}) %collective-permute-start) | collective-permute-done | bytes 133152 | tf_op jit(solution)/shard_map/ppermute | solution.py:443
  46.9 1.3 collective-permute-start.1
  48.2 1.3 collective-permute-done.6.refs_8_
  49.5 1.5 collective-permute-start.10
  51.0 2.7 %collective-permute-done.3.refs_5_ = s16[520,128]{1,0:T(8,128)(2,1)S(1)} collective-permute-done((s16[520,128]{1,0:T(8,128)(2,1)}, s16[520,128]{1,0:T(8,128)(2,1)S(1)}, u32[]{:S(2)}, u32[]{:S(2)}) %collective-permute-start.3) | collective-permute-done | bytes 133152 | tf_op jit(solution)/shard_map/ppermute | solution.py:443
  53.7 0.6 collective-permute-start.4
  54.3 3.4 %collective-permute-done.2.refs_4_ = s16[520,128]{1,0:T(8,128)(2,1)S(1)} collective-permute-done((s16[520,128]{1,0:T(8,128)(2,1)}, s16[520,128]{1,0:T(8,128)(2,1)S(1)}, u32[]{:S(2)}, u32[]{:S(2)}) %collective-permute-start.2) | collective-permute-done | bytes 133152 | tf_op jit(solution)/shard_map/ppermute | solution.py:443
  57.7 0.1 collective-permute-start.16
  57.7 3.7 %collective-permute-done.5.refs_7_ = s16[520,128]{1,0:T(8,128)(2,1)S(1)} collective-permute-done((s16[520,128]{1,0:T(8,128)(2,1)}, s16[520,128]{1,0:T(8,128)(2,1)S(1)}, u32[]{:S(2)}, u32[]{:S(2)}) %collective-permute-start.5) | collective-permute-done | bytes 133152 | tf_op jit(solution)/shard_map/ppermute | solution.py:443
  61.4 4.4 %collective-permute-start.7 = (s16[520,128]{1,0:T(8,128)(2,1)}, s16[520,128]{1,0:T(8,128)(2,1)S(1)}, u32[]{:S(2)}, u32[]{:S(2)}) collective-permute-start(s16[520,128]{1,0:T(8,128)(2,1)} %get-tuple-element.81), channel_id=1, source_target_pairs={{0,24},{4,28},{8,16},{12,20},{16,8},{20,12},{24,0},{28,4},{1,25},{... | collective-permute-start | bytes 399368 | tf_op jit(solution)/shard_map/ppermute | solution.py:443
  65.9 0.1 collective-permute-start.11
  65.9 5.7 %collective-permute-done.4.refs_6_ = s16[520,128]{1,0:T(8,128)(2,1)S(1)} collective-permute-done((s16[520,128]{1,0:T(8,128)(2,1)}, s16[520,128]{1,0:T(8,128)(2,1)S(1)}, u32[]{:S(2)}, u32[]{:S(2)}) %collective-permute-start.4) | collective-permute-done | bytes 133152 | tf_op jit(solution)/shard_map/ppermute | solution.py:443
  71.6 0.3 collective-permute-start.19
  71.9 2.3 %collective-permute-start.17 = (s16[520,128]{1,0:T(8,128)(2,1)}, s16[520,128]{1,0:T(8,128)(2,1)S(1)}, u32[]{:S(2)}, u32[]{:S(2)}) collective-permute-start(s16[520,128]{1,0:T(8,128)(2,1)} %get-tuple-element.100), channel_id=1, source_target_pairs={{0,16},{4,20},{8,24},{12,28},{16,0},{20,4},{24,8},{28,12},{1,17},{... | collective-permute-start | bytes 399368 | tf_op jit(solution)/shard_map/ppermute | solution.py:443
  74.3 9.0 %columns.2 = (s16[520,128]{1,0:T(8,128)(2,1)}, s16[520,128]{1,0:T(8,128)(2,1)}, s16[520,128]{1,0:T(8,128)(2,1)}, s16[520,128]{1,0:T(8,128)(2,1)}, s16[520,128]{1...) custom-call(s32[1]{0:T(128)} %bitcast.refs_0_, f32[2]{0:T(128)} %refs_1_.3, ...), custom_call_target="tpu_custom_call" | custom-call | tf_op jit(solution)/shard_map/columns/pallas_call | solution.py:550
  83.2 2.9 %collective-permute-start.8 = (s16[520,128]{1,0:T(8,128)(2,1)}, s16[520,128]{1,0:T(8,128)(2,1)S(1)}, u32[]{:S(2)}, u32[]{:S(2)}) collective-permute-start(s16[520,128]{1,0:T(8,128)(2,1)} %get-tuple-element.82), channel_id=1, source_target_pairs={{0,28},{4,24},{8,20},{12,16},{16,12},{20,8},{24,4},{28,0},{1,29},{... | collective-permute-start | bytes 399368 | tf_op jit(solution)/shard_map/ppermute | solution.py:443
  86.2 3.2 %collective-permute-start.12 = (s16[520,128]{1,0:T(8,128)(2,1)}, s16[520,128]{1,0:T(8,128)(2,1)S(1)}, u32[]{:S(2)}, u32[]{:S(2)}) collective-permute-start(s16[520,128]{1,0:T(8,128)(2,1)} %get-tuple-element.89), channel_id=1, source_target_pairs={{0,8},{4,12},{8,0},{12,4},{16,24},{20,28},{24,16},{28,20},{1,9},{5... | collective-permute-start | bytes 399368 | tf_op jit(solution)/shard_map/ppermute | solution.py:443
  89.4 0.7 collective-permute-start.20
  90.1 0.6 fusion.9
  92.0 0.9 collective-permute-start.18
  92.9 1.8 %collective-permute-start.9 = (s16[520,128]{1,0:T(8,128)(2,1)}, s16[520,128]{1,0:T(8,128)(2,1)S(1)}, u32[]{:S(2)}, u32[]{:S(2)}) collective-permute-start(s16[520,128]{1,0:T(8,128)(2,1)} %get-tuple-element.83), channel_id=1, source_target_pairs={{0,4},{4,0},{8,12},{12,8},{16,20},{20,16},{24,28},{28,24},{1,5},{5... | collective-permute-start | bytes 399368 | tf_op jit(solution)/shard_map/ppermute | solution.py:443
  94.7 9.0 %columns.3 = (s16[520,128]{1,0:T(8,128)(2,1)}, s16[520,128]{1,0:T(8,128)(2,1)}, s16[520,128]{1,0:T(8,128)(2,1)}, s16[520,128]{1,0:T(8,128)(2,1)}, s16[520,128]{1...) custom-call(s32[1]{0:T(128)} %bitcast.refs_0_, f32[2]{0:T(128)} %refs_1_.3, ...), custom_call_target="tpu_custom_call" | custom-call | tf_op jit(solution)/shard_map/columns/pallas_call | solution.py:550
  103.7 1.8 %collective-permute-start.15 = (s16[520,128]{1,0:T(8,128)(2,1)}, s16[520,128]{1,0:T(8,128)(2,1)S(1)}, u32[]{:S(2)}, u32[]{:S(2)}) collective-permute-start(s16[520,128]{1,0:T(8,128)(2,1)} %get-tuple-element.95), channel_id=1, source_target_pairs={{0,16},{4,20},{8,24},{12,28},{16,0},{20,4},{24,8},{28,12},{1,17},{... | collective-permute-start | bytes 399368 | tf_op jit(solution)/shard_map/ppermute | solution.py:443
  105.6 1.5 collective-permute-start.24
  107.0 2.0 %collective-permute-start.21 = (s16[520,128]{1,0:T(8,128)(2,1)}, s16[520,128]{1,0:T(8,128)(2,1)S(1)}, u32[]{:S(2)}, u32[]{:S(2)}) collective-permute-start(s16[520,128]{1,0:T(8,128)(2,1)} %get-tuple-element.110), channel_id=1, source_target_pairs={{0,28},{4,24},{8,20},{12,16},{16,12},{20,8},{24,4},{28,0},{1,29},{... | collective-permute-start | bytes 399368 | tf_op jit(solution)/shard_map/ppermute | solution.py:443
  109.1 2.8 %fusion.1 = f32[]{:T(128)} fusion(f32[1025]{0:T(1024)S(1)} %fusion.5, f32[1025]{0:T(1024)S(1)} %get-tuple-element.133, f32[1025]{0:T(1024)S(1)} %get-tuple-element.134), kind=kLoop, calls=%fused_computation.2 | loop fusion | flops 6303749 | bytes 12304 | tf_op jit(solution)/shard_map/reduce_sum | solution.py:436
  112.6 2.3 %collective-permute-start.27 = (s16[520,128]{1,0:T(8,128)(2,1)}, s16[520,128]{1,0:T(8,128)(2,1)S(1)}, u32[]{:S(2)}, u32[]{:S(2)}) collective-permute-start(s16[520,128]{1,0:T(8,128)(2,1)} %get-tuple-element.121), channel_id=1, source_target_pairs={{0,24},{4,28},{8,16},{12,20},{16,8},{20,12},{24,0},{28,4},{1,25},{... | collective-permute-start | bytes 399368 | tf_op jit(solution)/shard_map/ppermute | solution.py:443
  115.0 1.7 %collective-permute-done.15.refs_6_ = s16[520,128]{1,0:T(8,128)(2,1)S(1)} collective-permute-done((s16[520,128]{1,0:T(8,128)(2,1)}, s16[520,128]{1,0:T(8,128)(2,1)S(1)}, u32[]{:S(2)}, u32[]{:S(2)}) %collective-permute-start.15) | collective-permute-done | bytes 133152 | tf_op jit(solution)/shard_map/ppermute | solution.py:443
  116.7 1.0 collective-permute-start.26
  117.7 2.0 %collective-permute-start.25 = (s16[520,128]{1,0:T(8,128)(2,1)}, s16[520,128]{1,0:T(8,128)(2,1)}, u32[]{:S(2)}, u32[]{:S(2)}) collective-permute-start(s16[520,128]{1,0:T(8,128)(2,1)} %get-tuple-element.117), channel_id=1, source_target_pairs={{0,16},{4,20},{8,24},{12,28},{16,0},{20,4},{24,8},{28,12},{1,17},{... | collective-permute-start | bytes 399368 | tf_op jit(solution)/shard_map/ppermute | solution.py:443
  119.7 1.4 collective-permute-start.22
  121.1 2.0 %slice.16 = bf16[4,8,16,16,128]{4,3,2,1,0:T(8,128)(2,1)S(1)} slice(bf16[4,8,17,16,128]{4,3,2,1,0:T(8,128)(2,1)} %bitcast.39), slice={[0:4], [0:8], [0:16], [0:16], [0:128]} | slice | bytes 4194304 | tf_op jit(solution)/shard_map/slice | solution.py:583
  123.1 0.9 slice.17
  123.9 0.6 copy.35
  124.6 0.5 copy.43
  125.2 2.6 %copy.33.refs_21_ = bf16[2048,512]{1,0:T(8,128)(2,1)} copy(bf16[2048,512]{0,1:T(8,128)(2,1)S(1)} %bitcast.37) | data formatting | bytes 4194304 | tf_op jit(solution)/shard_map/reshape | solution.py:583
  127.7 0.1 constant_dynamic-slice_fusion
  127.8 0.7 reshape.177.refs_22_
  128.5 3.4 %collective-permute-done.26.refs_15_ = s16[520,128]{1,0:T(8,128)(2,1)} collective-permute-done((s16[520,128]{1,0:T(8,128)(2,1)}, s16[520,128]{1,0:T(8,128)(2,1)}, u32[]{:S(2)}, u32[]{:S(2)}) %collective-permute-start.26) | collective-permute-done | bytes 133152 | tf_op jit(solution)/shard_map/ppermute | solution.py:443
  131.9 1.1 collective-permute-done.25.refs_14_
  133.0 13.0 %rows_back.1 = (f32[8192,128]{1,0:T(8,128)}, f32[32,8,128]{2,1,0:T(8,128)}) custom-call(s32[1]{0:T(128)} %bitcast.refs_0_, f32[1]{0:T(128)} %bitcast.5.refs_1_, s16[520,128]{1,0:T(8,128)(2,1)} %get-tuple-element.77.refs_2_, s16[520,128]{1,0:T(8,128)(2,1)} %copy-done.7, s16[520,128]{1,0:T(8,128)(2,1)} %copy-done.4, s16[520,128]{1,0:T(8,128)(2,1)} %copy-done.3, ...), custom_call_target="tpu_custom_call" | custom-call | tf_op jit(solution)/shard_map/rows_back/pallas_call | solution.py:588
  146.0 8.8 %all-to-all-start.1 = ((f32[32,8,128]{2,1,0:T(8,128)}), f32[32,8,128]{2,1,0:T(8,128)S(1)}, u32[]{:S(2)}, u32[]{:S(2)}) async-start(f32[32,8,128]{2,1,0:T(8,128)} %get-tuple-element.124), calls=%async_computation.1 | async-start | bytes 262144 | tf_op jit(solution)/shard_map/all_to_all | solution.py:623
  154.9 1.0 fusion.3.refs_3_
  155.9 7.2 %all-to-all-done.1.refs_2_ = f32[32,8,128]{2,1,0:T(8,128)S(1)} async-done(((f32[32,8,128]{2,1,0:T(8,128)}), f32[32,8,128]{2,1,0:T(8,128)S(1)}, u32[]{:S(2)}, u32[]{:S(2)}) %all-to-all-start.1) | async-done | bytes 131104 | tf_op jit(solution)/shard_map/all_to_all | solution.py:623
  163.1 0.5 broadcast_in_dim.44.refs_0_
  163.6 0.1 copy-done.1
  163.7 2.1 %factor_basis.1 = (f32[2,256]{1,0:T(2,128)}, f32[8,8]{1,0:T(8,128)}, f32[2,256]{1,0:T(2,128)}) custom-call(s32[8]{0:T(128)} %broadcast_in_dim.44.refs_0_, s32[1]{0:T(128)} %bitcast.16.refs_1_, f32[32,8,128]{2,1,0:T(8,128)} %copy-done.1, bf16[1024,256]{1,0:T(8,128)(2,1)} %fusion.3.refs_3_), custom_call_target="tpu_custom_call" | custom-call | tf_op jit(solution)/shard_map/factor_basis/pallas_call | solution.py:628
  (81 shorter events, 0.2 us)
Async XLA Ops:
  13.1 23.4 %all-to-all-start = ((bf16[8,17,16,128]{3,2,1,0:T(8,128)(2,1)}), bf16[8,17,16,128]{3,2,1,0:T(8,128)(2,1)S(1)}, u32[]{:S(2)}, u32[]{:S(2)}) async-start(bf16[8,17,16,128]{3,2,1,0:T(8,128)(2,1)} %pack_prints.1), calls=%async_computation | async-start | bytes 1114112 | tf_op jit(solution)/shard_map/all_to_all | solution.py:505
  20.4 100.8 %all-gather.3.cloned.1.call-start = ((), (), s32[]{:S(2)}) async-start(), calls=%async_computation.2 | async-start | bytes 2785280 | tf_op jit(solution)/shard_map/all_gather | solution.py:541
  20.4 69.7 %copy-start.26 = (f32[2]{0:T(128)S(1)}, f32[2]{0:T(128)}, u32[]{:S(2)}) copy-start(f32[2]{0:T(128)} %refs_1_.3) | copy-start | bytes 28
  36.5 0.8 copy-start
  37.3 9.6 %collective-permute-start = (s16[520,128]{1,0:T(8,128)(2,1)}, s16[520,128]{1,0:T(8,128)(2,1)S(1)}, u32[]{:S(2)}, u32[]{:S(2)}) collective-permute-start(s16[520,128]{1,0:T(8,128)(2,1)} %get-tuple-element.69), channel_id=1, source_target_pairs={{0,28},{4,24},{8,20},{12,16},{16,12},{20,8},{24,4},{28,0},{1,29},{... | collective-permute-start | bytes 399368 | tf_op jit(solution)/shard_map/ppermute | solution.py:443
  39.7 9.8 %collective-permute-start.6 = (s16[520,128]{1,0:T(8,128)(2,1)}, s16[520,128]{1,0:T(8,128)(2,1)S(1)}, u32[]{:S(2)}, u32[]{:S(2)}) collective-permute-start(s16[520,128]{1,0:T(8,128)(2,1)} %get-tuple-element.76), channel_id=1, source_target_pairs={{0,24},{4,28},{8,16},{12,20},{16,8},{20,12},{24,0},{28,4},{1,25},{... | collective-permute-start | bytes 399368 | tf_op jit(solution)/shard_map/ppermute | solution.py:443
  42.0 11.6 %collective-permute-start.3 = (s16[520,128]{1,0:T(8,128)(2,1)}, s16[520,128]{1,0:T(8,128)(2,1)S(1)}, u32[]{:S(2)}, u32[]{:S(2)}) collective-permute-start(s16[520,128]{1,0:T(8,128)(2,1)} %get-tuple-element.72), channel_id=1, source_target_pairs={{0,12},{4,8},{8,4},{12,0},{16,28},{20,24},{24,20},{28,16},{1,13},{... | collective-permute-start | bytes 399368 | tf_op jit(solution)/shard_map/ppermute | solution.py:443
  42.1 15.6 %collective-permute-start.2 = (s16[520,128]{1,0:T(8,128)(2,1)}, s16[520,128]{1,0:T(8,128)(2,1)S(1)}, u32[]{:S(2)}, u32[]{:S(2)}) collective-permute-start(s16[520,128]{1,0:T(8,128)(2,1)} %get-tuple-element.71), channel_id=1, source_target_pairs={{0,8},{4,12},{8,0},{12,4},{16,24},{20,28},{24,16},{28,20},{1,9},{5... | collective-permute-start | bytes 399368 | tf_op jit(solution)/shard_map/ppermute | solution.py:443
  44.1 17.3 %collective-permute-start.5 = (s16[520,128]{1,0:T(8,128)(2,1)}, s16[520,128]{1,0:T(8,128)(2,1)S(1)}, u32[]{:S(2)}, u32[]{:S(2)}) collective-permute-start(s16[520,128]{1,0:T(8,128)(2,1)} %get-tuple-element.75), channel_id=1, source_target_pairs={{0,20},{4,16},{8,28},{12,24},{16,4},{20,0},{24,12},{28,8},{1,21},{... | collective-permute-start | bytes 399368 | tf_op jit(solution)/shard_map/ppermute | solution.py:443
  46.9 27.3 %copy-start.17 = (s16[520,128]{1,0:T(8,128)(2,1)}, s16[520,128]{1,0:T(8,128)(2,1)S(1)}, u32[]{:S(2)}) copy-start(s16[520,128]{1,0:T(8,128)(2,1)S(1)} %collective-permute-done.refs_9_) | copy-start | bytes 399364
  46.9 18.9 %collective-permute-start.1 = (s16[520,128]{1,0:T(8,128)(2,1)}, s16[520,128]{1,0:T(8,128)(2,1)S(1)}, u32[]{:S(2)}, u32[]{:S(2)}) collective-permute-start(s16[520,128]{1,0:T(8,128)(2,1)} %get-tuple-element.70), channel_id=1, source_target_pairs={{0,4},{4,0},{8,12},{12,8},{16,20},{20,16},{24,28},{28,24},{1,5},{5... | collective-permute-start | bytes 399368 | tf_op jit(solution)/shard_map/ppermute | solution.py:443
  49.5 24.7 %copy-start.19 = (s16[520,128]{1,0:T(8,128)(2,1)}, s16[520,128]{1,0:T(8,128)(2,1)S(1)}, u32[]{:S(2)}) copy-start(s16[520,128]{1,0:T(8,128)(2,1)S(1)} %collective-permute-done.6.refs_8_) | copy-start | bytes 399364
  49.5 16.3 %collective-permute-start.10 = (s16[520,128]{1,0:T(8,128)(2,1)}, s16[520,128]{1,0:T(8,128)(2,1)S(1)}, u32[]{:S(2)}, u32[]{:S(2)}) collective-permute-start(s16[520,128]{1,0:T(8,128)(2,1)} %get-tuple-element.87), channel_id=1, source_target_pairs={{0,28},{4,24},{8,20},{12,16},{16,12},{20,8},{24,4},{28,0},{1,29},{... | collective-permute-start | bytes 399368 | tf_op jit(solution)/shard_map/ppermute | solution.py:443
  53.7 20.5 %copy-start.20 = (s16[520,128]{1,0:T(8,128)(2,1)}, s16[520,128]{1,0:T(8,128)(2,1)S(1)}, u32[]{:S(2)}) copy-start(s16[520,128]{1,0:T(8,128)(2,1)S(1)} %collective-permute-done.3.refs_5_) | copy-start | bytes 399364
  53.7 17.9 %collective-permute-start.4 = (s16[520,128]{1,0:T(8,128)(2,1)}, s16[520,128]{1,0:T(8,128)(2,1)S(1)}, u32[]{:S(2)}, u32[]{:S(2)}) collective-permute-start(s16[520,128]{1,0:T(8,128)(2,1)} %get-tuple-element.74), channel_id=1, source_target_pairs={{0,16},{4,20},{8,24},{12,28},{16,0},{20,4},{24,8},{28,12},{1,17},{... | collective-permute-start | bytes 399368 | tf_op jit(solution)/shard_map/ppermute | solution.py:443
  57.7 16.5 %copy-start.22 = (s16[520,128]{1,0:T(8,128)(2,1)}, s16[520,128]{1,0:T(8,128)(2,1)S(1)}, u32[]{:S(2)}) copy-start(s16[520,128]{1,0:T(8,128)(2,1)S(1)} %collective-permute-done.2.refs_4_) | copy-start | bytes 399364
  57.7 14.2 %collective-permute-start.16 = (s16[520,128]{1,0:T(8,128)(2,1)}, s16[520,128]{1,0:T(8,128)(2,1)S(1)}, u32[]{:S(2)}, u32[]{:S(2)}) collective-permute-start(s16[520,128]{1,0:T(8,128)(2,1)} %get-tuple-element.99), channel_id=1, source_target_pairs={{0,12},{4,8},{8,4},{12,0},{16,28},{20,24},{24,20},{28,16},{1,13},{... | collective-permute-start | bytes 399368 | tf_op jit(solution)/shard_map/ppermute | solution.py:443
  61.4 12.8 %copy-start.23 = (s16[520,128]{1,0:T(8,128)(2,1)}, s16[520,128]{1,0:T(8,128)(2,1)S(1)}, u32[]{:S(2)}) copy-start(s16[520,128]{1,0:T(8,128)(2,1)S(1)} %collective-permute-done.5.refs_7_) | copy-start | bytes 399364
  61.4 21.8 %collective-permute-start.7 = (s16[520,128]{1,0:T(8,128)(2,1)}, s16[520,128]{1,0:T(8,128)(2,1)S(1)}, u32[]{:S(2)}, u32[]{:S(2)}) collective-permute-start(s16[520,128]{1,0:T(8,128)(2,1)} %get-tuple-element.81), channel_id=1, source_target_pairs={{0,24},{4,28},{8,16},{12,20},{16,8},{20,12},{24,0},{28,4},{1,25},{... | collective-permute-start | bytes 399368 | tf_op jit(solution)/shard_map/ppermute | solution.py:443
  65.8 8.4 %copy-start.24 = (s16[520,128]{1,0:T(8,128)(2,1)}, s16[520,128]{1,0:T(8,128)(2,1)S(1)}, u32[]{:S(2)}) copy-start(s16[520,128]{1,0:T(8,128)(2,1)S(1)} %collective-permute-done.1.refs_3_) | copy-start | bytes 399364
  65.8 20.3 %collective-permute-start.13 = (s16[520,128]{1,0:T(8,128)(2,1)}, s16[520,128]{1,0:T(8,128)(2,1)S(1)}, u32[]{:S(2)}, u32[]{:S(2)}) collective-permute-start(s16[520,128]{1,0:T(8,128)(2,1)} %get-tuple-element.92), channel_id=1, source_target_pairs={{0,8},{4,12},{8,0},{12,4},{16,24},{20,28},{24,16},{28,20},{1,9},{5... | collective-permute-start | bytes 399368 | tf_op jit(solution)/shard_map/ppermute | solution.py:443
  65.8 28.8 %copy-start.8 = (s16[520,128]{1,0:T(8,128)(2,1)}, s16[520,128]{1,0:T(8,128)(2,1)S(1)}, u32[]{:S(2)}) copy-start(s16[520,128]{1,0:T(8,128)(2,1)S(1)} %collective-permute-done.10.refs_9_) | copy-start | bytes 399364
  65.9 20.3 %collective-permute-start.11 = (s16[520,128]{1,0:T(8,128)(2,1)}, s16[520,128]{1,0:T(8,128)(2,1)S(1)}, u32[]{:S(2)}, u32[]{:S(2)}) collective-permute-start(s16[520,128]{1,0:T(8,128)(2,1)} %get-tuple-element.88), channel_id=1, source_target_pairs={{0,4},{4,0},{8,12},{12,8},{16,20},{20,16},{24,28},{28,24},{1,5},{5... | collective-permute-start | bytes 399368 | tf_op jit(solution)/shard_map/ppermute | solution.py:443
  71.6 2.7 %copy-start.25 = (s16[520,128]{1,0:T(8,128)(2,1)}, s16[520,128]{1,0:T(8,128)(2,1)S(1)}, u32[]{:S(2)}) copy-start(s16[520,128]{1,0:T(8,128)(2,1)S(1)} %collective-permute-done.4.refs_6_) | copy-start | bytes 399364
  71.6 17.8 %collective-permute-start.19 = (s16[520,128]{1,0:T(8,128)(2,1)}, s16[520,128]{1,0:T(8,128)(2,1)S(1)}, u32[]{:S(2)}, u32[]{:S(2)}) collective-permute-start(s16[520,128]{1,0:T(8,128)(2,1)} %get-tuple-element.104), channel_id=1, source_target_pairs={{0,20},{4,16},{8,28},{12,24},{16,4},{20,0},{24,12},{28,8},{1,21},{... | collective-permute-start | bytes 399368 | tf_op jit(solution)/shard_map/ppermute | solution.py:443
  71.9 22.8 %copy-start.9 = (s16[520,128]{1,0:T(8,128)(2,1)}, s16[520,128]{1,0:T(8,128)(2,1)S(1)}, u32[]{:S(2)}) copy-start(s16[520,128]{1,0:T(8,128)(2,1)S(1)} %collective-permute-done.16.refs_5_) | copy-start | bytes 399364
  71.9 20.1 %collective-permute-start.17 = (s16[520,128]{1,0:T(8,128)(2,1)}, s16[520,128]{1,0:T(8,128)(2,1)S(1)}, u32[]{:S(2)}, u32[]{:S(2)}) collective-permute-start(s16[520,128]{1,0:T(8,128)(2,1)} %get-tuple-element.100), channel_id=1, source_target_pairs={{0,16},{4,20},{8,24},{12,28},{16,0},{20,4},{24,8},{28,12},{1,17},{... | collective-permute-start | bytes 399368 | tf_op jit(solution)/shard_map/ppermute | solution.py:443
  83.2 11.4 %copy-start.11 = (s16[520,128]{1,0:T(8,128)(2,1)}, s16[520,128]{1,0:T(8,128)(2,1)S(1)}, u32[]{:S(2)}) copy-start(s16[520,128]{1,0:T(8,128)(2,1)S(1)} %collective-permute-done.7.refs_8_) | copy-start | bytes 399364
  83.2 9.7 %collective-permute-start.8 = (s16[520,128]{1,0:T(8,128)(2,1)}, s16[520,128]{1,0:T(8,128)(2,1)S(1)}, u32[]{:S(2)}, u32[]{:S(2)}) collective-permute-start(s16[520,128]{1,0:T(8,128)(2,1)} %get-tuple-element.82), channel_id=1, source_target_pairs={{0,28},{4,24},{8,20},{12,16},{16,12},{20,8},{24,4},{28,0},{1,29},{... | collective-permute-start | bytes 399368 | tf_op jit(solution)/shard_map/ppermute | solution.py:443
  86.2 8.5 %copy-start.13 = (s16[520,128]{1,0:T(8,128)(2,1)}, s16[520,128]{1,0:T(8,128)(2,1)S(1)}, u32[]{:S(2)}) copy-start(s16[520,128]{1,0:T(8,128)(2,1)S(1)} %collective-permute-done.13.refs_4_) | copy-start | bytes 399364
  86.2 17.5 %collective-permute-start.14 = (s16[520,128]{1,0:T(8,128)(2,1)}, s16[520,128]{1,0:T(8,128)(2,1)S(1)}, u32[]{:S(2)}, u32[]{:S(2)}) collective-permute-start(s16[520,128]{1,0:T(8,128)(2,1)} %get-tuple-element.93), channel_id=1, source_target_pairs={{0,12},{4,8},{8,4},{12,0},{16,28},{20,24},{24,20},{28,16},{1,13},{... | collective-permute-start | bytes 399368 | tf_op jit(solution)/shard_map/ppermute | solution.py:443
  86.2 8.5 %copy-start.15 = (s16[520,128]{1,0:T(8,128)(2,1)}, s16[520,128]{1,0:T(8,128)(2,1)S(1)}, u32[]{:S(2)}) copy-start(s16[520,128]{1,0:T(8,128)(2,1)S(1)} %collective-permute-done.11.refs_3_) | copy-start | bytes 399364
  86.2 19.4 %collective-permute-start.12 = (s16[520,128]{1,0:T(8,128)(2,1)}, s16[520,128]{1,0:T(8,128)(2,1)S(1)}, u32[]{:S(2)}, u32[]{:S(2)}) collective-permute-start(s16[520,128]{1,0:T(8,128)(2,1)} %get-tuple-element.89), channel_id=1, source_target_pairs={{0,8},{4,12},{8,0},{12,4},{16,24},{20,28},{24,16},{28,20},{1,9},{5... | collective-permute-start | bytes 399368 | tf_op jit(solution)/shard_map/ppermute | solution.py:443
  89.4 5.3 %copy-start.16 = (s16[520,128]{1,0:T(8,128)(2,1)}, s16[520,128]{1,0:T(8,128)(2,1)S(1)}, u32[]{:S(2)}) copy-start(s16[520,128]{1,0:T(8,128)(2,1)S(1)} %collective-permute-done.19.refs_7_) | copy-start | bytes 399364
  89.4 17.7 %collective-permute-start.20 = (s16[520,128]{1,0:T(8,128)(2,1)}, s16[520,128]{1,0:T(8,128)(2,1)S(1)}, u32[]{:S(2)}, u32[]{:S(2)}) collective-permute-start(s16[520,128]{1,0:T(8,128)(2,1)} %get-tuple-element.105), channel_id=1, source_target_pairs={{0,24},{4,28},{8,16},{12,20},{16,8},{20,12},{24,0},{28,4},{1,25},{... | collective-permute-start | bytes 399368 | tf_op jit(solution)/shard_map/ppermute | solution.py:443
  92.0 2.7 %copy-start.18 = (s16[520,128]{1,0:T(8,128)(2,1)}, s16[520,128]{1,0:T(8,128)(2,1)S(1)}, u32[]{:S(2)}) copy-start(s16[520,128]{1,0:T(8,128)(2,1)S(1)} %collective-permute-done.17.refs_6_) | copy-start | bytes 399364
  92.0 20.6 %collective-permute-start.18 = (s16[520,128]{1,0:T(8,128)(2,1)}, s16[520,128]{1,0:T(8,128)(2,1)S(1)}, u32[]{:S(2)}, u32[]{:S(2)}) collective-permute-start(s16[520,128]{1,0:T(8,128)(2,1)} %get-tuple-element.101), channel_id=1, source_target_pairs={{0,20},{4,16},{8,28},{12,24},{16,4},{20,0},{24,12},{28,8},{1,21},{... | collective-permute-start | bytes 399368 | tf_op jit(solution)/shard_map/ppermute | solution.py:443
  92.9 30.2 %copy-start.2 = (s16[520,128]{1,0:T(8,128)(2,1)}, s16[520,128]{1,0:T(8,128)(2,1)S(1)}, u32[]{:S(2)}) copy-start(s16[520,128]{1,0:T(8,128)(2,1)S(1)} %collective-permute-done.8.refs_9_) | copy-start | bytes 399364
  92.9 22.1 %collective-permute-start.9 = (s16[520,128]{1,0:T(8,128)(2,1)}, s16[520,128]{1,0:T(8,128)(2,1)S(1)}, u32[]{:S(2)}, u32[]{:S(2)}) collective-permute-start(s16[520,128]{1,0:T(8,128)(2,1)} %get-tuple-element.83), channel_id=1, source_target_pairs={{0,4},{4,0},{8,12},{12,8},{16,20},{20,16},{24,28},{28,24},{1,5},{5... | collective-permute-start | bytes 399368 | tf_op jit(solution)/shard_map/ppermute | solution.py:443
  103.7 20.8 %copy-start.3 = (s16[520,128]{1,0:T(8,128)(2,1)}, s16[520,128]{1,0:T(8,128)(2,1)S(1)}, u32[]{:S(2)}) copy-start(s16[520,128]{1,0:T(8,128)(2,1)S(1)} %collective-permute-done.14.refs_5_) | copy-start | bytes 399364
  103.7 13.0 %collective-permute-start.15 = (s16[520,128]{1,0:T(8,128)(2,1)}, s16[520,128]{1,0:T(8,128)(2,1)S(1)}, u32[]{:S(2)}, u32[]{:S(2)}) collective-permute-start(s16[520,128]{1,0:T(8,128)(2,1)} %get-tuple-element.95), channel_id=1, source_target_pairs={{0,16},{4,20},{8,24},{12,28},{16,0},{20,4},{24,8},{28,12},{1,17},{... | collective-permute-start | bytes 399368 | tf_op jit(solution)/shard_map/ppermute | solution.py:443
  105.6 19.0 %copy-start.4 = (s16[520,128]{1,0:T(8,128)(2,1)}, s16[520,128]{1,0:T(8,128)(2,1)S(1)}, u32[]{:S(2)}) copy-start(s16[520,128]{1,0:T(8,128)(2,1)S(1)} %collective-permute-done.12.refs_4_) | copy-start | bytes 399364
  105.6 12.1 %collective-permute-start.24 = (s16[520,128]{1,0:T(8,128)(2,1)}, s16[520,128]{1,0:T(8,128)(2,1)S(1)}, u32[]{:S(2)}, u32[]{:S(2)}) collective-permute-start(s16[520,128]{1,0:T(8,128)(2,1)} %get-tuple-element.115), channel_id=1, source_target_pairs={{0,12},{4,8},{8,4},{12,0},{16,28},{20,24},{24,20},{28,16},{1,13},{... | collective-permute-start | bytes 399368 | tf_op jit(solution)/shard_map/ppermute | solution.py:443
  107.0 17.5 %copy-start.5 = (s16[520,128]{1,0:T(8,128)(2,1)}, s16[520,128]{1,0:T(8,128)(2,1)S(1)}, u32[]{:S(2)}) copy-start(s16[520,128]{1,0:T(8,128)(2,1)S(1)} %collective-permute-done.20.refs_8_) | copy-start | bytes 399364
  107.0 12.6 %collective-permute-start.21 = (s16[520,128]{1,0:T(8,128)(2,1)}, s16[520,128]{1,0:T(8,128)(2,1)S(1)}, u32[]{:S(2)}, u32[]{:S(2)}) collective-permute-start(s16[520,128]{1,0:T(8,128)(2,1)} %get-tuple-element.110), channel_id=1, source_target_pairs={{0,28},{4,24},{8,20},{12,16},{16,12},{20,8},{24,4},{28,0},{1,29},{... | collective-permute-start | bytes 399368 | tf_op jit(solution)/shard_map/ppermute | solution.py:443
  112.6 11.9 %copy-start.6 = (s16[520,128]{1,0:T(8,128)(2,1)}, s16[520,128]{1,0:T(8,128)(2,1)S(1)}, u32[]{:S(2)}) copy-start(s16[520,128]{1,0:T(8,128)(2,1)S(1)} %collective-permute-done.18.refs_7_) | copy-start | bytes 399364
  112.6 15.9 %collective-permute-start.27 = (s16[520,128]{1,0:T(8,128)(2,1)}, s16[520,128]{1,0:T(8,128)(2,1)S(1)}, u32[]{:S(2)}, u32[]{:S(2)}) collective-permute-start(s16[520,128]{1,0:T(8,128)(2,1)} %get-tuple-element.121), channel_id=1, source_target_pairs={{0,24},{4,28},{8,16},{12,20},{16,8},{20,12},{24,0},{28,4},{1,25},{... | collective-permute-start | bytes 399368 | tf_op jit(solution)/shard_map/ppermute | solution.py:443
  115.0 9.6 %copy-start.7 = (s16[520,128]{1,0:T(8,128)(2,1)}, s16[520,128]{1,0:T(8,128)(2,1)S(1)}, u32[]{:S(2)}) copy-start(s16[520,128]{1,0:T(8,128)(2,1)S(1)} %collective-permute-done.9.refs_3_) | copy-start | bytes 399364
  115.0 13.5 %collective-permute-start.23 = (s16[520,128]{1,0:T(8,128)(2,1)}, s16[520,128]{1,0:T(8,128)(2,1)}, u32[]{:S(2)}, u32[]{:S(2)}) collective-permute-start(s16[520,128]{1,0:T(8,128)(2,1)} %get-tuple-element.113), channel_id=1, source_target_pairs={{0,8},{4,12},{8,0},{12,4},{16,24},{20,28},{24,16},{28,20},{1,9},{5... | collective-permute-start | bytes 399368 | tf_op jit(solution)/shard_map/ppermute | solution.py:443
  116.7 7.9 %copy-start.10 = (s16[520,128]{1,0:T(8,128)(2,1)}, s16[520,128]{1,0:T(8,128)(2,1)S(1)}, u32[]{:S(2)}) copy-start(s16[520,128]{1,0:T(8,128)(2,1)S(1)} %collective-permute-done.15.refs_6_) | copy-start | bytes 399364
  116.7 15.2 %collective-permute-start.26 = (s16[520,128]{1,0:T(8,128)(2,1)}, s16[520,128]{1,0:T(8,128)(2,1)}, u32[]{:S(2)}, u32[]{:S(2)}) collective-permute-start(s16[520,128]{1,0:T(8,128)(2,1)} %get-tuple-element.119), channel_id=1, source_target_pairs={{0,20},{4,16},{8,28},{12,24},{16,4},{20,0},{24,12},{28,8},{1,21},{... | collective-permute-start | bytes 399368 | tf_op jit(solution)/shard_map/ppermute | solution.py:443
  117.7 6.9 %copy-start.12 = (s16[520,128]{1,0:T(8,128)(2,1)}, s16[520,128]{1,0:T(8,128)(2,1)S(1)}, u32[]{:S(2)}) copy-start(s16[520,128]{1,0:T(8,128)(2,1)S(1)} %collective-permute-done.24.refs_13_) | copy-start | bytes 399364
  117.7 15.3 %collective-permute-start.25 = (s16[520,128]{1,0:T(8,128)(2,1)}, s16[520,128]{1,0:T(8,128)(2,1)}, u32[]{:S(2)}, u32[]{:S(2)}) collective-permute-start(s16[520,128]{1,0:T(8,128)(2,1)} %get-tuple-element.117), channel_id=1, source_target_pairs={{0,16},{4,20},{8,24},{12,28},{16,0},{20,4},{24,8},{28,12},{1,17},{... | collective-permute-start | bytes 399368 | tf_op jit(solution)/shard_map/ppermute | solution.py:443
  119.7 4.9 %copy-start.14 = (s16[520,128]{1,0:T(8,128)(2,1)}, s16[520,128]{1,0:T(8,128)(2,1)S(1)}, u32[]{:S(2)}) copy-start(s16[520,128]{1,0:T(8,128)(2,1)S(1)} %collective-permute-done.21.refs_17_) | copy-start | bytes 399364
  119.7 13.3 %collective-permute-start.22 = (s16[520,128]{1,0:T(8,128)(2,1)}, s16[520,128]{1,0:T(8,128)(2,1)}, u32[]{:S(2)}, u32[]{:S(2)}) collective-permute-start(s16[520,128]{1,0:T(8,128)(2,1)} %get-tuple-element.111), channel_id=1, source_target_pairs={{0,4},{4,0},{8,12},{12,8},{16,20},{20,16},{24,28},{28,24},{1,5},{5... | collective-permute-start | bytes 399368 | tf_op jit(solution)/shard_map/ppermute | solution.py:443
  128.5 4.5 %copy-start.21 = (s16[520,128]{1,0:T(8,128)(2,1)}, s16[520,128]{1,0:T(8,128)(2,1)S(1)}, u32[]{:S(2)}) copy-start(s16[520,128]{1,0:T(8,128)(2,1)S(1)} %collective-permute-done.27.refs_16_) | copy-start | bytes 399364
  146.0 17.1 %all-to-all-start.1 = ((f32[32,8,128]{2,1,0:T(8,128)}), f32[32,8,128]{2,1,0:T(8,128)S(1)}, u32[]{:S(2)}, u32[]{:S(2)}) async-start(f32[32,8,128]{2,1,0:T(8,128)} %get-tuple-element.124), calls=%async_computation.1 | async-start | bytes 262144 | tf_op jit(solution)/shard_map/all_to_all | solution.py:623
  163.1 0.6 copy-start.1
Sparse Core Ops, SparseCore 0:
  37.4 24.8 all-gather.2

commit v4 on v3

--- a/solution.py
+++ b/solution.py
@@ -91,23 +91,39 @@
     return jnp.exp2(exponent.astype(jnp.int32).astype(F32) * (1.0 / STEPS)) * (1.0 / TOP)
 
 
-def pack_kernel(source_ref, prints_ref, code_ref, packed, semaphore):
-    slabs, share = packed.shape[0], packed.shape[1] - 1
-
-    def begin(at, carry):
-        for slab in range(slabs):
-            pltpu.make_async_copy(
-                prints_ref.at[source_ref[slab * share + at]], packed.at[slab, at], semaphore
-            ).start()
-        return carry
-
-    lax.fori_loop(0, share, begin, 0)
-    codes = jnp.broadcast_to(code_ref[...], packed.shape[2:]).astype(BF16)
+def pack_kernel(
+    slabs, capacity, bands, spot_ref, target_ref, band_ref, tile_ref, prints_ref, packed, place_ref, wide, flat, thin
+):
+    count, band_rows, _ = prints_ref.shape
+    share = packed.shape[1] - 1
+    sent = slabs * share
+    target = target_ref[...]
+    mine = (lax.broadcasted_iota(jnp.int32, (slabs, 1), 0) == target).astype(F32)
+    earlier = lax.broadcasted_iota(jnp.int32, (count, count), 0) < lax.broadcasted_iota(
+        jnp.int32, (count, count), 1
+    )
+    before = dot(mine.astype(BF16), earlier.astype(F32).astype(BF16))
+    slot = jnp.sum(before * mine, axis=0, keepdims=True).astype(jnp.int32)
+    place = target * capacity + slot
+    place_ref[...] = place
+    order = lax.broadcasted_iota(jnp.int32, (sent, 1), 0)
+    wanted = order // share * capacity + spot_ref[1] * share + order % share
+    pick = (place == wanted).astype(F32).astype(BF16)
+    code = (tile_ref[...] * bands + band_ref[...] + 1).astype(F32).astype(BF16)
+    code = lax.dot_general(
+        jnp.broadcast_to(code, (band_rows, count)), pick, (((1,), (1,)), ((), ())), preferred_element_type=F32
+    )
+    code = (code - 1.0).astype(BF16)
+    wide[...] = prints_ref[...].astype(F32).reshape(count * band_rows, LANES)
+    for row in range(band_rows):
+        flat[:, row * LANES:(row + 1) * LANES] = wide[pl.ds(row, count, stride=band_rows), :].astype(BF16)
+    picked = dot(pick, flat[...])
+    for row in range(band_rows):
+        thin[pl.ds(row, sent, stride=band_rows), :] = picked[:, row * LANES:(row + 1) * LANES]
     for slab in range(slabs):
-        packed[slab, share] = codes
-    pltpu.make_async_copy(
-        packed.at[:, pl.ds(0, share)], packed.at[:, pl.ds(0, share)], semaphore
-    ).wait()
+        lines = thin[slab * share * band_rows:(slab + 1) * share * band_rows, :]
+        packed[slab, :share] = lines.reshape(share, band_rows, LANES).astype(BF16)
+        packed[slab, share] = code
 
 
 def rows_kernel(slabs, chunks, me_ref, x_ref, lead_ref, trail_ref, turn_ref, *rest):
@@ -267,8 +283,8 @@
 
 def finish_kernel(slabs, chunks, me_ref, gain_ref, *rest):
     ins, rest = rest[:slabs * chunks], rest[slabs * chunks:]
-    lead_ref, trail_ref, turn_ref, prints_ref, index_ref, out_ref, value_ref = rest[:7]
-    stack, scale, high, low, field, blocks = rest[7:]
+    lead_ref, trail_ref, turn_ref, prints_hbm, index_ref, out_ref, value_ref = rest[:7]
+    stack, scale, high, low, field, blocks, prints_ref, semaphore = rest[7:]
     step, last = pl.program_id(0), pl.num_programs(0) - 1
     short = turn_ref.shape[1]
     halves, tile = short // LANES, high.shape[0] // RADIX
@@ -278,6 +294,7 @@
 
     @pl.when(step == 0)
     def _():
+        pltpu.make_async_copy(prints_hbm, prints_ref, semaphore).start()
         for chunk in range(chunks):
             for hop in range(slabs):
                 slab = me_ref[0] ^ hop
@@ -335,6 +352,7 @@
                 blocks[column * bands:(column + 1) * bands, row * LANES:(row + 1) * LANES] = (
                     piece.astype(BF16)
                 )
+        pltpu.make_async_copy(prints_hbm, prints_ref, semaphore).wait()
         values = dot(blocks[...], prints_ref[...])
         each = count // 2 * bands
         chosen = lax.broadcasted_iota(jnp.int32, (each, 1), 0) == index_ref[...]
@@ -352,7 +370,7 @@
 
 
 def small_kernel(
-    slabs, lanes_q, each, total, row_ref, lane_ref, all_ref, pick_ref, sketch_ref, factor_ref, basis_ref,
+    slabs, lanes_q, each, total, capacity, spot_ref, all_ref, pick_ref, sketch_ref, factor_ref, basis_ref,
     own, found,
 ):
     probes = lanes_q * each
@@ -391,7 +409,7 @@
     for slab in range(slabs):
         for one in range(probes):
             own[one:one + 1, slab * LANES:(slab + 1) * LANES] = all_ref[
-                slab * lanes_q + one // each, pl.ds((one % each) * tiles + row_ref[slab], 1), :
+                slab * lanes_q + one // each, pl.ds((one % each) * tiles + spot_ref[0] * capacity // LANES, 1), :
             ]
     value = own[...]
     first = value.astype(BF16)
@@ -408,7 +426,7 @@
         solved.append(value * inverse[at])
         found[1, at:at + 1, :] = solved[at]
     for part in range(each):
-        place = pl.ds(lane_ref[0] * each + part, 1)
+        place = pl.ds(spot_ref[1] * each + part, 1)
         sketch_ref[part:part + 1, :] = found[0, place, :]
         basis_ref[part:part + 1, :] = found[1, place, :]
 
@@ -467,41 +485,35 @@
     lead, trail, back_lead, back_trail = (jnp.asarray(part) for part in dft_blocks(short))
     turn_x = jnp.asarray(twiddles(width))
     turn_y = jnp.asarray(twiddles(height).T.copy())
-    me_list = me.reshape(1).astype(jnp.int32)
+    me_list = jnp.stack([me, lane_at]).astype(jnp.int32)
+    spot = me_list
     read_count, band_rows, tile_cols = footprints.shape
     band_count = rows // band_rows
-    tile_count = width // tile_cols
     capacity = 2 * read_count // slabs
     share = capacity // lanes_q
     slots = slabs * capacity
-    target = reading_slab[:, 0]
-    reading = jnp.arange(read_count, dtype=jnp.int32)
-    onehot = (target[:, None] == jnp.arange(slabs, dtype=jnp.int32)[None, :]).astype(F32)
-    before = (reading[:, None] > reading[None, :]).astype(F32)
-    slot = jnp.sum(jnp.dot(before, onehot) * onehot, axis=1).astype(jnp.int32)
-    place = target * capacity + slot
-    blocks = band_count * tile_count
-    code = reading_tile * band_count + reading_band
-    wanted = (
-        jnp.arange(slabs, dtype=jnp.int32)[:, None] * capacity
-        + lane_at * share
-        + jnp.arange(share, dtype=jnp.int32)[None, :]
-    ).reshape(-1)
-    found = jnp.max(
-        jnp.where(wanted[:, None] == place[None, :], (reading * blocks + code)[None, :], -1), axis=1
-    )
-    source = jnp.maximum(found, 0) // blocks
-    codes = jnp.where(found < 0, -1, found % blocks).astype(F32).reshape(1, slabs * share)
-
-    packed = pl.pallas_call(
-        pack_kernel,
-        in_specs=[smem(), pl.BlockSpec(memory_space=pl.ANY), vmem()],
-        out_specs=vmem(),
-        out_shape=jax.ShapeDtypeStruct((slabs, share + 1, band_rows, tile_cols), BF16),
-        scratch_shapes=[pltpu.SemaphoreType.DMA],
+    packed, place = pl.pallas_call(
+        lambda *refs: pack_kernel(slabs, capacity, band_count, *refs),
+        in_specs=[smem()] + [vmem()] * 4,
+        out_specs=[vmem()] * 2,
+        out_shape=[
+            jax.ShapeDtypeStruct((slabs, share + 1, band_rows, tile_cols), BF16),
+            jax.ShapeDtypeStruct((1, read_count), jnp.int32),
+        ],
+        scratch_shapes=[
+            pltpu.VMEM((read_count * band_rows, LANES), F32),
+            pltpu.VMEM((read_count, band_rows * LANES), BF16),
+            pltpu.VMEM((slabs * share * band_rows, LANES), F32),
+        ],
         compiler_params=params(),
         name="pack_prints",
-    )(source, footprints, codes)
+    )(
+        me_list,
+        reading_slab.reshape(1, read_count),
+        reading_band.reshape(1, read_count),
+        reading_tile.reshape(1, read_count),
+        footprints,
+    )
     gathered = lax.all_to_all(packed, "grid", split_axis=0, concat_axis=0, tiled=True)
     me_list, _ = lax.optimization_barrier((me_list, packed))
     column_tiles = width // LANES
@@ -594,7 +606,7 @@
             whole(lead.shape),
             whole(trail.shape),
             whole(turn_x.shape),
-            whole(prints.shape),
+            pl.BlockSpec(memory_space=pl.ANY),
             whole(index.shape),
         ],
         out_specs=[
@@ -612,6 +624,8 @@
             pltpu.VMEM((RADIX * tile, 2 * short), BF16),
             pltpu.VMEM((each * column_tiles, rows, LANES), F32),
             pltpu.VMEM((each * column_tiles * band_count, band_rows * tile_cols), BF16),
+            pltpu.VMEM(prints.shape, BF16),
+            pltpu.SemaphoreType.DMA,
         ],
         compiler_params=params(),
         name="rows_back",
@@ -621,13 +635,12 @@
     )
 
     everyone = lax.all_to_all(values, ("grid", "probe"), split_axis=0, concat_axis=0, tiled=True)
-    offset = jnp.full((slabs,), me * capacity, jnp.int32)
-    lane_of = target * LANES + me * capacity % LANES + slot
+    lane_of = place[0] // capacity * LANES + me * capacity % LANES + place[0] % capacity
     pick = (jnp.arange(slabs * LANES, dtype=jnp.int32)[:, None] == lane_of[None, :]).astype(BF16)
     probe_count = each * lanes_q
     sketch, factor, basis = pl.pallas_call(
-        lambda *refs: small_kernel(slabs, lanes_q, each, read_count * slabs, *refs),
-        in_specs=[smem(), smem(), vmem(), vmem()],
+        lambda *refs: small_kernel(slabs, lanes_q, each, read_count * slabs, capacity, *refs),
+        in_specs=[smem(), vmem(), vmem()],
         out_specs=[vmem()] * 3,
         out_shape=[
             jax.ShapeDtypeStruct((each, read_count), F32),
@@ -640,7 +653,7 @@
         ],
         compiler_params=params(),
         name="factor_basis",
-    )(offset // LANES, lane_at.reshape(1).astype(jnp.int32), everyone, pick)
+    )(spot, everyone, pick)
     return (smoothed, sketch.T, factor, basis.T)
 
 

time: 173 us -> 168 us (0.971)
  waiting for transfers between devices: 37.6 us -> 32.3 us
  starting transfers between devices: 56 us -> 57.9 us
    ppermute x28, starting transfers between devices: 39.8 us -> 44.4 us  [send(): return lax.ppermute(value, axis, pairs)]
    ppermute x28, waiting for transfers between devices: 24.8 us -> 20.5 us  [send(): return lax.ppermute(value, axis, pairs)]
    all_to_all x1, starting transfers between devices: 8.83 us -> 6.23 us  [local(): lax.all_to_all(values, ('grid', 'probe'), split_axis=0, concat_axis=0, ti...]
  transfers between devices with their start and end apart: 31 -> 31, of which waited for: 11 -> 11; matrix products, arithmetic and copies ran while one was open for 7% -> 7% of each run, Pallas kernels for 16% -> 17%
where the time goes in v4:
time: 168 us; the launch traced here: 167 us
  starting transfers between devices  57.9 us (34%)
  Pallas kernels  46.9 us (28%)
  waiting for transfers between devices  32.3 us (19%)
  between operations  16.3 us (10%)
  local copies, waits for them, and re-layouts  9.19 us (5%)
  other arithmetic  4.5 us (3%)
    ppermute x28, starting transfers between devices, send(): return lax.ppermute(value, axis, pairs)  44.4 us
    ppermute x28, waiting for transfers between devices, send(): return lax.ppermute(value, axis, pairs)  20.5 us
    pallas_call x2, Pallas kernels, local(): pl.pallas_call(lambda *refs, chunk=chunk: columns_kernel(slabs, chunk, he...  17.8 us
    pallas_call x1, Pallas kernels, local(): pl.pallas_call(lambda *refs: finish_kernel(slabs, chunks, *refs), grid=(r...  13 us
    pallas_call x1, Pallas kernels, local(): pl.pallas_call(lambda *refs: rows_kernel(slabs, chunks, *refs), grid=(row...  10.6 us
    all_to_all x1, starting transfers between devices, local(): lax.all_to_all(packed, 'grid', split_axis=0, concat_axis=0, tiled=True)  7.28 us
    all_to_all x1, waiting for transfers between devices, local(): lax.all_to_all(values, ('grid', 'probe'), split_axis=0, concat_axis=0, ti...  7.17 us
    all_to_all x1, starting transfers between devices, local(): lax.all_to_all(values, ('grid', 'probe'), split_axis=0, concat_axis=0, ti...  6.23 us
  transfers between devices with their start and end apart: 31, of which 11 were waited for; matrix products, arithmetic and copies ran while one was open for 7% of the time, Pallas kernels for 17%

profile of v4, /device:TPU:0, one launch (start us, length us, event | category | flops | bytes accessed | tf_op | source)
XLA Modules:
  0.0 167.2 jit_solution(9060166288087077977)
XLA Ops:
  7.2 0.6 pad_add_fusion.refs_0_
  7.8 3.4 %pack_prints.1 = (bf16[8,17,16,128]{3,2,1,0:T(8,128)(2,1)}, s32[1,256]{1,0:T(1,128)}) custom-call(s32[2]{0:T(128)} %pad_add_fusion.refs_0_, s32[1,256]{1,0:T(1,128)} %bitcast.43, s32[1,256]{1,0:T(1,128)} %bitcast.44, s32[1,256]{1,0:T(1,128)} %bitcast.45, bf16[256,16,128]{2,1,0:T(8,128)(2,1)} %refs_4_.2), custom_call_target="tpu_custom_call" | custom-call | tf_op jit(solution)/shard_map/pack_prints/pallas_call | solution.py:495
  11.2 7.3 %all-to-all-start = ((bf16[8,17,16,128]{3,2,1,0:T(8,128)(2,1)}), bf16[8,17,16,128]{3,2,1,0:T(8,128)(2,1)S(1)}, u32[]{:S(2)}, u32[]{:S(2)}) async-start(bf16[8,17,16,128]{3,2,1,0:T(8,128)(2,1)} %get-tuple-element.68), calls=%async_computation | async-start | bytes 1114112 | tf_op jit(solution)/shard_map/all_to_all | solution.py:517
  18.4 0.0 all-gather.3.cloned.1.call-start
  18.5 0.0 copy-start.26
  18.5 10.6 %rows_forward.1 = (s16[520,128]{1,0:T(8,128)(2,1)}, s16[520,128]{1,0:T(8,128)(2,1)}, s16[520,128]{1,0:T(8,128)(2,1)}, s16[520,128]{1,0:T(8,128)(2,1)}, s16[520,1...) custom-call(s32[2]{0:T(128)} %pad_add_fusion.refs_0_, ...), custom_call_target="tpu_custom_call" | custom-call | tf_op jit(solution)/shard_map/rows_forward/pallas_call | solution.py:530
  29.1 4.5 %all-to-all-done = bf16[8,17,16,128]{3,2,1,0:T(8,128)(2,1)S(1)} async-done(((bf16[8,17,16,128]{3,2,1,0:T(8,128)(2,1)}), bf16[8,17,16,128]{3,2,1,0:T(8,128)(2,1)S(1)}, u32[]{:S(2)}, u32[]{:S(2)}) %all-to-all-start) | async-done | bytes 557088 | tf_op jit(solution)/shard_map/all_to_all | solution.py:517
  33.6 0.8 copy-done
  34.4 0.0 all-gather.3.cloned.1.call-update
  34.5 2.4 %collective-permute-start = (s16[520,128]{1,0:T(8,128)(2,1)}, s16[520,128]{1,0:T(8,128)(2,1)S(1)}, u32[]{:S(2)}, u32[]{:S(2)}) collective-permute-start(s16[520,128]{1,0:T(8,128)(2,1)} %get-tuple-element.72), channel_id=1, source_target_pairs={{0,28},{4,24},{8,20},{12,16},{16,12},{20,8},{24,4},{28,0},{1,29},{... | collective-permute-start | bytes 399368 | tf_op jit(solution)/shard_map/ppermute | solution.py:461
  36.9 2.4 %collective-permute-start.6 = (s16[520,128]{1,0:T(8,128)(2,1)}, s16[520,128]{1,0:T(8,128)(2,1)S(1)}, u32[]{:S(2)}, u32[]{:S(2)}) collective-permute-start(s16[520,128]{1,0:T(8,128)(2,1)} %get-tuple-element.79), channel_id=1, source_target_pairs={{0,24},{4,28},{8,16},{12,20},{16,8},{20,12},{24,0},{28,4},{1,25},{... | collective-permute-start | bytes 399368 | tf_op jit(solution)/shard_map/ppermute | solution.py:461
  39.3 0.0 collective-permute-start.3
  39.3 2.0 %collective-permute-start.2 = (s16[520,128]{1,0:T(8,128)(2,1)}, s16[520,128]{1,0:T(8,128)(2,1)S(1)}, u32[]{:S(2)}, u32[]{:S(2)}) collective-permute-start(s16[520,128]{1,0:T(8,128)(2,1)} %get-tuple-element.74), channel_id=1, source_target_pairs={{0,8},{4,12},{8,0},{12,4},{16,24},{20,28},{24,16},{28,20},{1,9},{5... | collective-permute-start | bytes 399368 | tf_op jit(solution)/shard_map/ppermute | solution.py:461
  41.3 0.9 collective-permute-start.5
  42.2 1.6 collective-permute-done.refs_9_
  43.8 1.3 collective-permute-start.1
  45.1 1.4 collective-permute-done.6.refs_8_
  46.5 1.5 collective-permute-start.10
  47.9 1.7 %collective-permute-done.3.refs_5_ = s16[520,128]{1,0:T(8,128)(2,1)S(1)} collective-permute-done((s16[520,128]{1,0:T(8,128)(2,1)}, s16[520,128]{1,0:T(8,128)(2,1)S(1)}, u32[]{:S(2)}, u32[]{:S(2)}) %collective-permute-start.3) | collective-permute-done | bytes 133152 | tf_op jit(solution)/shard_map/ppermute | solution.py:461
  49.6 2.9 %collective-permute-start.4 = (s16[520,128]{1,0:T(8,128)(2,1)}, s16[520,128]{1,0:T(8,128)(2,1)S(1)}, u32[]{:S(2)}, u32[]{:S(2)}) collective-permute-start(s16[520,128]{1,0:T(8,128)(2,1)} %get-tuple-element.77), channel_id=1, source_target_pairs={{0,16},{4,20},{8,24},{12,28},{16,0},{20,4},{24,8},{28,12},{1,17},{... | collective-permute-start | bytes 399368 | tf_op jit(solution)/shard_map/ppermute | solution.py:461
  52.5 1.1 collective-permute-done.2.refs_4_
  53.6 1.0 collective-permute-start.16
  54.6 5.9 %collective-permute-done.5.refs_7_ = s16[520,128]{1,0:T(8,128)(2,1)S(1)} collective-permute-done((s16[520,128]{1,0:T(8,128)(2,1)}, s16[520,128]{1,0:T(8,128)(2,1)S(1)}, u32[]{:S(2)}, u32[]{:S(2)}) %collective-permute-start.5) | collective-permute-done | bytes 133152 | tf_op jit(solution)/shard_map/ppermute | solution.py:461
  60.5 3.6 %collective-permute-start.7 = (s16[520,128]{1,0:T(8,128)(2,1)}, s16[520,128]{1,0:T(8,128)(2,1)S(1)}, u32[]{:S(2)}, u32[]{:S(2)}) collective-permute-start(s16[520,128]{1,0:T(8,128)(2,1)} %get-tuple-element.84), channel_id=1, source_target_pairs={{0,24},{4,28},{8,16},{12,20},{16,8},{20,12},{24,0},{28,4},{1,25},{... | collective-permute-start | bytes 399368 | tf_op jit(solution)/shard_map/ppermute | solution.py:461
  64.1 0.0 collective-permute-done.1.refs_3_
  64.1 0.0 collective-permute-done.10.refs_9_
  64.1 0.1 collective-permute-start.11
  64.2 4.6 %collective-permute-done.4.refs_6_ = s16[520,128]{1,0:T(8,128)(2,1)S(1)} collective-permute-done((s16[520,128]{1,0:T(8,128)(2,1)}, s16[520,128]{1,0:T(8,128)(2,1)S(1)}, u32[]{:S(2)}, u32[]{:S(2)}) %collective-permute-start.4) | collective-permute-done | bytes 133152 | tf_op jit(solution)/shard_map/ppermute | solution.py:461
  68.8 0.5 collective-permute-start.19
  69.3 2.8 %collective-permute-start.17 = (s16[520,128]{1,0:T(8,128)(2,1)}, s16[520,128]{1,0:T(8,128)(2,1)S(1)}, u32[]{:S(2)}, u32[]{:S(2)}) collective-permute-start(s16[520,128]{1,0:T(8,128)(2,1)} %get-tuple-element.103), channel_id=1, source_target_pairs={{0,16},{4,20},{8,24},{12,28},{16,0},{20,4},{24,8},{28,12},{1,17},{... | collective-permute-start | bytes 399368 | tf_op jit(solution)/shard_map/ppermute | solution.py:461
  72.1 8.9 %columns.2 = (s16[520,128]{1,0:T(8,128)(2,1)}, s16[520,128]{1,0:T(8,128)(2,1)}, s16[520,128]{1,0:T(8,128)(2,1)}, s16[520,128]{1,0:T(8,128)(2,1)}, s16[520,128]{1...) custom-call(s32[2]{0:T(128)} %pad_add_fusion.refs_0_, f32[2]{0:T(128)} %refs_1_.3, ...), custom_call_target="tpu_custom_call" | custom-call | tf_op jit(solution)/shard_map/columns/pallas_call | solution.py:562
  81.1 1.6 collective-permute-start.8
  82.6 0.2 collective-permute-start.14
  82.8 0.0 collective-permute-done.11.refs_3_
  82.8 5.2 %collective-permute-start.12 = (s16[520,128]{1,0:T(8,128)(2,1)}, s16[520,128]{1,0:T(8,128)(2,1)S(1)}, u32[]{:S(2)}, u32[]{:S(2)}) collective-permute-start(s16[520,128]{1,0:T(8,128)(2,1)} %get-tuple-element.92), channel_id=1, source_target_pairs={{0,8},{4,12},{8,0},{12,4},{16,24},{20,28},{24,16},{28,20},{1,9},{5... | collective-permute-start | bytes 399368 | tf_op jit(solution)/shard_map/ppermute | solution.py:461
  88.0 0.6 fusion.6
  89.8 1.6 collective-permute-start.18
  91.4 1.5 collective-permute-start.9
  92.9 8.9 %columns.3 = (s16[520,128]{1,0:T(8,128)(2,1)}, s16[520,128]{1,0:T(8,128)(2,1)}, s16[520,128]{1,0:T(8,128)(2,1)}, s16[520,128]{1,0:T(8,128)(2,1)}, s16[520,128]{1...) custom-call(s32[2]{0:T(128)} %pad_add_fusion.refs_0_, f32[2]{0:T(128)} %refs_1_.3, ...), custom_call_target="tpu_custom_call" | custom-call | tf_op jit(solution)/shard_map/columns/pallas_call | solution.py:562
  101.9 1.5 collective-permute-start.15
  103.3 2.3 %collective-permute-start.24 = (s16[520,128]{1,0:T(8,128)(2,1)}, s16[520,128]{1,0:T(8,128)(2,1)S(1)}, u32[]{:S(2)}, u32[]{:S(2)}) collective-permute-start(s16[520,128]{1,0:T(8,128)(2,1)} %get-tuple-element.118), channel_id=1, source_target_pairs={{0,12},{4,8},{8,4},{12,0},{16,28},{20,24},{24,20},{28,16},{1,13},{... | collective-permute-start | bytes 399368 | tf_op jit(solution)/shard_map/ppermute | solution.py:461
  105.6 2.3 %collective-permute-start.21 = (s16[520,128]{1,0:T(8,128)(2,1)}, s16[520,128]{1,0:T(8,128)(2,1)S(1)}, u32[]{:S(2)}, u32[]{:S(2)}) collective-permute-start(s16[520,128]{1,0:T(8,128)(2,1)} %get-tuple-element.113), channel_id=1, source_target_pairs={{0,28},{4,24},{8,20},{12,16},{16,12},{20,8},{24,4},{28,0},{1,29},{... | collective-permute-start | bytes 399368 | tf_op jit(solution)/shard_map/ppermute | solution.py:461
  108.0 2.8 %fusion.1 = f32[]{:T(128)} fusion(f32[1025]{0:T(1024)S(1)} %fusion.4, f32[1025]{0:T(1024)S(1)} %get-tuple-element.134, f32[1025]{0:T(1024)S(1)} %get-tuple-element.135), kind=kLoop, calls=%fused_computation.2 | loop fusion | flops 6303749 | bytes 12304 | tf_op jit(solution)/shard_map/reduce_sum | solution.py:454
  111.6 1.7 %collective-permute-start.27 = (s16[520,128]{1,0:T(8,128)(2,1)}, s16[520,128]{1,0:T(8,128)(2,1)S(1)}, u32[]{:S(2)}, u32[]{:S(2)}) collective-permute-start(s16[520,128]{1,0:T(8,128)(2,1)} %get-tuple-element.124), channel_id=1, source_target_pairs={{0,24},{4,28},{8,16},{12,20},{16,8},{20,12},{24,0},{28,4},{1,25},{... | collective-permute-start | bytes 399368 | tf_op jit(solution)/shard_map/ppermute | solution.py:461
  113.3 3.1 %collective-permute-start.26 = (s16[520,128]{1,0:T(8,128)(2,1)}, s16[520,128]{1,0:T(8,128)(2,1)}, u32[]{:S(2)}, u32[]{:S(2)}) collective-permute-start(s16[520,128]{1,0:T(8,128)(2,1)} %get-tuple-element.122), channel_id=1, source_target_pairs={{0,20},{4,16},{8,28},{12,24},{16,4},{20,0},{24,12},{28,8},{1,21},{... | collective-permute-start | bytes 399368 | tf_op jit(solution)/shard_map/ppermute | solution.py:461
  116.4 0.6 collective-permute-start.25
  117.0 0.1 collective-permute-done.21.refs_17_
  117.2 1.6 collective-permute-start.22
  118.8 0.9 slice.17
  119.6 2.0 %slice.16 = bf16[4,8,16,16,128]{4,3,2,1,0:T(8,128)(2,1)S(1)} slice(bf16[4,8,17,16,128]{4,3,2,1,0:T(8,128)(2,1)} %bitcast.41), slice={[0:4], [0:8], [0:16], [0:16], [0:128]} | slice | bytes 4194304 | tf_op jit(solution)/shard_map/slice | solution.py:595
  121.6 0.1 constant_dynamic-slice_fusion
  121.7 0.7 reshape.96.refs_22_
  122.4 0.4 copy.35
  122.8 0.5 copy.43
  123.4 0.0 copy-start.27
  123.4 2.6 %copy.33.refs_21_ = bf16[2048,512]{1,0:T(8,128)(2,1)} copy(bf16[2048,512]{0,1:T(8,128)(2,1)S(1)} %bitcast.38) | data formatting | bytes 4194304 | tf_op jit(solution)/shard_map/reshape | solution.py:595
  126.0 2.4 %collective-permute-done.26.refs_15_ = s16[520,128]{1,0:T(8,128)(2,1)} collective-permute-done((s16[520,128]{1,0:T(8,128)(2,1)}, s16[520,128]{1,0:T(8,128)(2,1)}, u32[]{:S(2)}, u32[]{:S(2)}) %collective-permute-start.26) | collective-permute-done | bytes 133152 | tf_op jit(solution)/shard_map/ppermute | solution.py:461
  128.4 1.7 %collective-permute-done.25.refs_14_ = s16[520,128]{1,0:T(8,128)(2,1)} collective-permute-done((s16[520,128]{1,0:T(8,128)(2,1)}, s16[520,128]{1,0:T(8,128)(2,1)}, u32[]{:S(2)}, u32[]{:S(2)}) %collective-permute-start.25) | collective-permute-done | bytes 133152 | tf_op jit(solution)/shard_map/ppermute | solution.py:461
  130.1 13.0 %rows_back.1 = (f32[8192,128]{1,0:T(8,128)}, f32[32,8,128]{2,1,0:T(8,128)}) custom-call(s32[2]{0:T(128)} %pad_add_fusion.refs_0_, f32[1]{0:T(128)} %bitcast.7.refs_1_, s16[520,128]{1,0:T(8,128)(2,1)} %get-tuple-element.80.refs_2_, s16[520,128]{1,0:T(8,128)(2,1)} %copy-done.7, s16[520,128]{1,0:T(8,128)(2,1)} %copy-done.4, s16[520,128]{1,0:T(8,128)(2,1)} %copy-done.3, ...), custom_call_target="tpu_custom_call" | custom-call | tf_op jit(solution)/shard_map/rows_back/pallas_call | solution.py:600
  143.1 6.2 %all-to-all-start.1 = ((f32[32,8,128]{2,1,0:T(8,128)}), f32[32,8,128]{2,1,0:T(8,128)S(1)}, u32[]{:S(2)}, u32[]{:S(2)}) async-start(f32[32,8,128]{2,1,0:T(8,128)} %get-tuple-element.127), calls=%async_computation.1 | async-start | bytes 262144 | tf_op jit(solution)/shard_map/all_to_all | solution.py:637
  149.4 1.0 fusion.2.refs_2_
  150.4 7.2 %all-to-all-done.1.refs_1_ = f32[32,8,128]{2,1,0:T(8,128)S(1)} async-done(((f32[32,8,128]{2,1,0:T(8,128)}), f32[32,8,128]{2,1,0:T(8,128)S(1)}, u32[]{:S(2)}, u32[]{:S(2)}) %all-to-all-start.1) | async-done | bytes 131104 | tf_op jit(solution)/shard_map/all_to_all | solution.py:637
  157.6 0.7 copy-done.1
  158.2 2.1 %factor_basis.1 = (f32[2,256]{1,0:T(2,128)}, f32[8,8]{1,0:T(8,128)}, f32[2,256]{1,0:T(2,128)}) custom-call(s32[2]{0:T(128)} %pad_add_fusion.refs_0_, f32[32,8,128]{2,1,0:T(8,128)} %copy-done.1, bf16[1024,256]{1,0:T(8,128)(2,1)} %fusion.2.refs_2_), custom_call_target="tpu_custom_call" | custom-call | tf_op jit(solution)/shard_map/factor_basis/pallas_call | solution.py:641
  (76 shorter events, 0.2 us)
Async XLA Ops:
  11.2 22.5 %all-to-all-start = ((bf16[8,17,16,128]{3,2,1,0:T(8,128)(2,1)}), bf16[8,17,16,128]{3,2,1,0:T(8,128)(2,1)S(1)}, u32[]{:S(2)}, u32[]{:S(2)}) async-start(bf16[8,17,16,128]{3,2,1,0:T(8,128)(2,1)} %get-tuple-element.68), calls=%async_computation | async-start | bytes 1114112 | tf_op jit(solution)/shard_map/all_to_all | solution.py:517
  18.4 100.3 %all-gather.3.cloned.1.call-start = ((), (), s32[]{:S(2)}) async-start(), calls=%async_computation.2 | async-start | bytes 2785280 | tf_op jit(solution)/shard_map/all_gather | solution.py:553
  18.5 69.5 %copy-start.26 = (f32[2]{0:T(128)S(1)}, f32[2]{0:T(128)}, u32[]{:S(2)}) copy-start(f32[2]{0:T(128)} %refs_1_.3) | copy-start | bytes 28
  33.6 0.8 copy-start
  34.5 9.3 %collective-permute-start = (s16[520,128]{1,0:T(8,128)(2,1)}, s16[520,128]{1,0:T(8,128)(2,1)S(1)}, u32[]{:S(2)}, u32[]{:S(2)}) collective-permute-start(s16[520,128]{1,0:T(8,128)(2,1)} %get-tuple-element.72), channel_id=1, source_target_pairs={{0,28},{4,24},{8,20},{12,16},{16,12},{20,8},{24,4},{28,0},{1,29},{... | collective-permute-start | bytes 399368 | tf_op jit(solution)/shard_map/ppermute | solution.py:461
  36.9 9.6 %collective-permute-start.6 = (s16[520,128]{1,0:T(8,128)(2,1)}, s16[520,128]{1,0:T(8,128)(2,1)S(1)}, u32[]{:S(2)}, u32[]{:S(2)}) collective-permute-start(s16[520,128]{1,0:T(8,128)(2,1)} %get-tuple-element.79), channel_id=1, source_target_pairs={{0,24},{4,28},{8,16},{12,20},{16,8},{20,12},{24,0},{28,4},{1,25},{... | collective-permute-start | bytes 399368 | tf_op jit(solution)/shard_map/ppermute | solution.py:461
  39.3 10.4 %collective-permute-start.3 = (s16[520,128]{1,0:T(8,128)(2,1)}, s16[520,128]{1,0:T(8,128)(2,1)S(1)}, u32[]{:S(2)}, u32[]{:S(2)}) collective-permute-start(s16[520,128]{1,0:T(8,128)(2,1)} %get-tuple-element.75), channel_id=1, source_target_pairs={{0,12},{4,8},{8,4},{12,0},{16,28},{20,24},{24,20},{28,16},{1,13},{... | collective-permute-start | bytes 399368 | tf_op jit(solution)/shard_map/ppermute | solution.py:461
  39.3 14.4 %collective-permute-start.2 = (s16[520,128]{1,0:T(8,128)(2,1)}, s16[520,128]{1,0:T(8,128)(2,1)S(1)}, u32[]{:S(2)}, u32[]{:S(2)}) collective-permute-start(s16[520,128]{1,0:T(8,128)(2,1)} %get-tuple-element.74), channel_id=1, source_target_pairs={{0,8},{4,12},{8,0},{12,4},{16,24},{20,28},{24,16},{28,20},{1,9},{5... | collective-permute-start | bytes 399368 | tf_op jit(solution)/shard_map/ppermute | solution.py:461
  41.3 19.2 %collective-permute-start.5 = (s16[520,128]{1,0:T(8,128)(2,1)}, s16[520,128]{1,0:T(8,128)(2,1)S(1)}, u32[]{:S(2)}, u32[]{:S(2)}) collective-permute-start(s16[520,128]{1,0:T(8,128)(2,1)} %get-tuple-element.78), channel_id=1, source_target_pairs={{0,20},{4,16},{8,28},{12,24},{16,4},{20,0},{24,12},{28,8},{1,21},{... | collective-permute-start | bytes 399368 | tf_op jit(solution)/shard_map/ppermute | solution.py:461
  43.8 28.3 %copy-start.17 = (s16[520,128]{1,0:T(8,128)(2,1)}, s16[520,128]{1,0:T(8,128)(2,1)S(1)}, u32[]{:S(2)}) copy-start(s16[520,128]{1,0:T(8,128)(2,1)S(1)} %collective-permute-done.refs_9_) | copy-start | bytes 399364
  43.8 20.3 %collective-permute-start.1 = (s16[520,128]{1,0:T(8,128)(2,1)}, s16[520,128]{1,0:T(8,128)(2,1)S(1)}, u32[]{:S(2)}, u32[]{:S(2)}) collective-permute-start(s16[520,128]{1,0:T(8,128)(2,1)} %get-tuple-element.73), channel_id=1, source_target_pairs={{0,4},{4,0},{8,12},{12,8},{16,20},{20,16},{24,28},{28,24},{1,5},{5... | collective-permute-start | bytes 399368 | tf_op jit(solution)/shard_map/ppermute | solution.py:461
  46.5 25.6 %copy-start.19 = (s16[520,128]{1,0:T(8,128)(2,1)}, s16[520,128]{1,0:T(8,128)(2,1)S(1)}, u32[]{:S(2)}) copy-start(s16[520,128]{1,0:T(8,128)(2,1)S(1)} %collective-permute-done.6.refs_8_) | copy-start | bytes 399364
  46.5 17.6 %collective-permute-start.10 = (s16[520,128]{1,0:T(8,128)(2,1)}, s16[520,128]{1,0:T(8,128)(2,1)S(1)}, u32[]{:S(2)}, u32[]{:S(2)}) collective-permute-start(s16[520,128]{1,0:T(8,128)(2,1)} %get-tuple-element.90), channel_id=1, source_target_pairs={{0,28},{4,24},{8,20},{12,16},{16,12},{20,8},{24,4},{28,0},{1,29},{... | collective-permute-start | bytes 399368 | tf_op jit(solution)/shard_map/ppermute | solution.py:461
  49.6 22.5 %copy-start.20 = (s16[520,128]{1,0:T(8,128)(2,1)}, s16[520,128]{1,0:T(8,128)(2,1)S(1)}, u32[]{:S(2)}) copy-start(s16[520,128]{1,0:T(8,128)(2,1)S(1)} %collective-permute-done.3.refs_5_) | copy-start | bytes 399364
  49.6 19.1 %collective-permute-start.4 = (s16[520,128]{1,0:T(8,128)(2,1)}, s16[520,128]{1,0:T(8,128)(2,1)S(1)}, u32[]{:S(2)}, u32[]{:S(2)}) collective-permute-start(s16[520,128]{1,0:T(8,128)(2,1)} %get-tuple-element.77), channel_id=1, source_target_pairs={{0,16},{4,20},{8,24},{12,28},{16,0},{20,4},{24,8},{28,12},{1,17},{... | collective-permute-start | bytes 399368 | tf_op jit(solution)/shard_map/ppermute | solution.py:461
  53.6 18.5 %copy-start.22 = (s16[520,128]{1,0:T(8,128)(2,1)}, s16[520,128]{1,0:T(8,128)(2,1)S(1)}, u32[]{:S(2)}) copy-start(s16[520,128]{1,0:T(8,128)(2,1)S(1)} %collective-permute-done.2.refs_4_) | copy-start | bytes 399364
  53.6 15.7 %collective-permute-start.16 = (s16[520,128]{1,0:T(8,128)(2,1)}, s16[520,128]{1,0:T(8,128)(2,1)S(1)}, u32[]{:S(2)}, u32[]{:S(2)}) collective-permute-start(s16[520,128]{1,0:T(8,128)(2,1)} %get-tuple-element.102), channel_id=1, source_target_pairs={{0,12},{4,8},{8,4},{12,0},{16,28},{20,24},{24,20},{28,16},{1,13},{... | collective-permute-start | bytes 399368 | tf_op jit(solution)/shard_map/ppermute | solution.py:461
  60.5 11.6 %copy-start.23 = (s16[520,128]{1,0:T(8,128)(2,1)}, s16[520,128]{1,0:T(8,128)(2,1)S(1)}, u32[]{:S(2)}) copy-start(s16[520,128]{1,0:T(8,128)(2,1)S(1)} %collective-permute-done.5.refs_7_) | copy-start | bytes 399364
  60.5 20.5 %collective-permute-start.7 = (s16[520,128]{1,0:T(8,128)(2,1)}, s16[520,128]{1,0:T(8,128)(2,1)S(1)}, u32[]{:S(2)}, u32[]{:S(2)}) collective-permute-start(s16[520,128]{1,0:T(8,128)(2,1)} %get-tuple-element.84), channel_id=1, source_target_pairs={{0,24},{4,28},{8,16},{12,20},{16,8},{20,12},{24,0},{28,4},{1,25},{... | collective-permute-start | bytes 399368 | tf_op jit(solution)/shard_map/ppermute | solution.py:461
  64.1 8.0 %copy-start.24 = (s16[520,128]{1,0:T(8,128)(2,1)}, s16[520,128]{1,0:T(8,128)(2,1)S(1)}, u32[]{:S(2)}) copy-start(s16[520,128]{1,0:T(8,128)(2,1)S(1)} %collective-permute-done.1.refs_3_) | copy-start | bytes 399364
  64.1 18.5 %collective-permute-start.13 = (s16[520,128]{1,0:T(8,128)(2,1)}, s16[520,128]{1,0:T(8,128)(2,1)S(1)}, u32[]{:S(2)}, u32[]{:S(2)}) collective-permute-start(s16[520,128]{1,0:T(8,128)(2,1)} %get-tuple-element.95), channel_id=1, source_target_pairs={{0,8},{4,12},{8,0},{12,4},{16,24},{20,28},{24,16},{28,20},{1,9},{5... | collective-permute-start | bytes 399368 | tf_op jit(solution)/shard_map/ppermute | solution.py:461
  64.1 28.8 %copy-start.10 = (s16[520,128]{1,0:T(8,128)(2,1)}, s16[520,128]{1,0:T(8,128)(2,1)S(1)}, u32[]{:S(2)}) copy-start(s16[520,128]{1,0:T(8,128)(2,1)S(1)} %collective-permute-done.10.refs_9_) | copy-start | bytes 399364
  64.1 18.7 %collective-permute-start.11 = (s16[520,128]{1,0:T(8,128)(2,1)}, s16[520,128]{1,0:T(8,128)(2,1)S(1)}, u32[]{:S(2)}, u32[]{:S(2)}) collective-permute-start(s16[520,128]{1,0:T(8,128)(2,1)} %get-tuple-element.91), channel_id=1, source_target_pairs={{0,4},{4,0},{8,12},{12,8},{16,20},{20,16},{24,28},{28,24},{1,5},{5... | collective-permute-start | bytes 399368 | tf_op jit(solution)/shard_map/ppermute | solution.py:461
  68.8 3.4 %copy-start.25 = (s16[520,128]{1,0:T(8,128)(2,1)}, s16[520,128]{1,0:T(8,128)(2,1)S(1)}, u32[]{:S(2)}) copy-start(s16[520,128]{1,0:T(8,128)(2,1)S(1)} %collective-permute-done.4.refs_6_) | copy-start | bytes 399364
  68.8 19.2 %collective-permute-start.19 = (s16[520,128]{1,0:T(8,128)(2,1)}, s16[520,128]{1,0:T(8,128)(2,1)S(1)}, u32[]{:S(2)}, u32[]{:S(2)}) collective-permute-start(s16[520,128]{1,0:T(8,128)(2,1)} %get-tuple-element.107), channel_id=1, source_target_pairs={{0,20},{4,16},{8,28},{12,24},{16,4},{20,0},{24,12},{28,8},{1,21},{... | collective-permute-start | bytes 399368 | tf_op jit(solution)/shard_map/ppermute | solution.py:461
  69.3 23.6 %copy-start.12 = (s16[520,128]{1,0:T(8,128)(2,1)}, s16[520,128]{1,0:T(8,128)(2,1)S(1)}, u32[]{:S(2)}) copy-start(s16[520,128]{1,0:T(8,128)(2,1)S(1)} %collective-permute-done.16.refs_5_) | copy-start | bytes 399364
  69.3 20.5 %collective-permute-start.17 = (s16[520,128]{1,0:T(8,128)(2,1)}, s16[520,128]{1,0:T(8,128)(2,1)S(1)}, u32[]{:S(2)}, u32[]{:S(2)}) collective-permute-start(s16[520,128]{1,0:T(8,128)(2,1)} %get-tuple-element.103), channel_id=1, source_target_pairs={{0,16},{4,20},{8,24},{12,28},{16,0},{20,4},{24,8},{28,12},{1,17},{... | collective-permute-start | bytes 399368 | tf_op jit(solution)/shard_map/ppermute | solution.py:461
  81.1 11.9 %copy-start.13 = (s16[520,128]{1,0:T(8,128)(2,1)}, s16[520,128]{1,0:T(8,128)(2,1)S(1)}, u32[]{:S(2)}) copy-start(s16[520,128]{1,0:T(8,128)(2,1)S(1)} %collective-permute-done.7.refs_8_) | copy-start | bytes 399364
  81.1 10.4 %collective-permute-start.8 = (s16[520,128]{1,0:T(8,128)(2,1)}, s16[520,128]{1,0:T(8,128)(2,1)S(1)}, u32[]{:S(2)}, u32[]{:S(2)}) collective-permute-start(s16[520,128]{1,0:T(8,128)(2,1)} %get-tuple-element.85), channel_id=1, source_target_pairs={{0,28},{4,24},{8,20},{12,16},{16,12},{20,8},{24,4},{28,0},{1,29},{... | collective-permute-start | bytes 399368 | tf_op jit(solution)/shard_map/ppermute | solution.py:461
  82.6 10.3 %copy-start.14 = (s16[520,128]{1,0:T(8,128)(2,1)}, s16[520,128]{1,0:T(8,128)(2,1)S(1)}, u32[]{:S(2)}) copy-start(s16[520,128]{1,0:T(8,128)(2,1)S(1)} %collective-permute-done.13.refs_4_) | copy-start | bytes 399364
  82.6 19.2 %collective-permute-start.14 = (s16[520,128]{1,0:T(8,128)(2,1)}, s16[520,128]{1,0:T(8,128)(2,1)S(1)}, u32[]{:S(2)}, u32[]{:S(2)}) collective-permute-start(s16[520,128]{1,0:T(8,128)(2,1)} %get-tuple-element.96), channel_id=1, source_target_pairs={{0,12},{4,8},{8,4},{12,0},{16,28},{20,24},{24,20},{28,16},{1,13},{... | collective-permute-start | bytes 399368 | tf_op jit(solution)/shard_map/ppermute | solution.py:461
  82.8 10.1 %copy-start.15 = (s16[520,128]{1,0:T(8,128)(2,1)}, s16[520,128]{1,0:T(8,128)(2,1)S(1)}, u32[]{:S(2)}) copy-start(s16[520,128]{1,0:T(8,128)(2,1)S(1)} %collective-permute-done.11.refs_3_) | copy-start | bytes 399364
  82.8 20.5 %collective-permute-start.12 = (s16[520,128]{1,0:T(8,128)(2,1)}, s16[520,128]{1,0:T(8,128)(2,1)S(1)}, u32[]{:S(2)}, u32[]{:S(2)}) collective-permute-start(s16[520,128]{1,0:T(8,128)(2,1)} %get-tuple-element.92), channel_id=1, source_target_pairs={{0,8},{4,12},{8,0},{12,4},{16,24},{20,28},{24,16},{28,20},{1,9},{5... | collective-permute-start | bytes 399368 | tf_op jit(solution)/shard_map/ppermute | solution.py:461
  88.0 5.0 %copy-start.16 = (s16[520,128]{1,0:T(8,128)(2,1)}, s16[520,128]{1,0:T(8,128)(2,1)S(1)}, u32[]{:S(2)}) copy-start(s16[520,128]{1,0:T(8,128)(2,1)S(1)} %collective-permute-done.19.refs_7_) | copy-start | bytes 399364
  88.0 17.7 %collective-permute-start.20 = (s16[520,128]{1,0:T(8,128)(2,1)}, s16[520,128]{1,0:T(8,128)(2,1)S(1)}, u32[]{:S(2)}, u32[]{:S(2)}) collective-permute-start(s16[520,128]{1,0:T(8,128)(2,1)} %get-tuple-element.108), channel_id=1, source_target_pairs={{0,24},{4,28},{8,16},{12,20},{16,8},{20,12},{24,0},{28,4},{1,25},{... | collective-permute-start | bytes 399368 | tf_op jit(solution)/shard_map/ppermute | solution.py:461
  89.8 3.1 %copy-start.18 = (s16[520,128]{1,0:T(8,128)(2,1)}, s16[520,128]{1,0:T(8,128)(2,1)S(1)}, u32[]{:S(2)}) copy-start(s16[520,128]{1,0:T(8,128)(2,1)S(1)} %collective-permute-done.17.refs_6_) | copy-start | bytes 399364
  89.8 21.7 %collective-permute-start.18 = (s16[520,128]{1,0:T(8,128)(2,1)}, s16[520,128]{1,0:T(8,128)(2,1)S(1)}, u32[]{:S(2)}, u32[]{:S(2)}) collective-permute-start(s16[520,128]{1,0:T(8,128)(2,1)} %get-tuple-element.104), channel_id=1, source_target_pairs={{0,20},{4,16},{8,28},{12,24},{16,4},{20,0},{24,12},{28,8},{1,21},{... | collective-permute-start | bytes 399368 | tf_op jit(solution)/shard_map/ppermute | solution.py:461
  91.4 30.2 %copy-start.2 = (s16[520,128]{1,0:T(8,128)(2,1)}, s16[520,128]{1,0:T(8,128)(2,1)S(1)}, u32[]{:S(2)}) copy-start(s16[520,128]{1,0:T(8,128)(2,1)S(1)} %collective-permute-done.8.refs_9_) | copy-start | bytes 399364
  91.4 21.8 %collective-permute-start.9 = (s16[520,128]{1,0:T(8,128)(2,1)}, s16[520,128]{1,0:T(8,128)(2,1)S(1)}, u32[]{:S(2)}, u32[]{:S(2)}) collective-permute-start(s16[520,128]{1,0:T(8,128)(2,1)} %get-tuple-element.86), channel_id=1, source_target_pairs={{0,4},{4,0},{8,12},{12,8},{16,20},{20,16},{24,28},{28,24},{1,5},{5... | collective-permute-start | bytes 399368 | tf_op jit(solution)/shard_map/ppermute | solution.py:461
  101.9 20.9 %copy-start.3 = (s16[520,128]{1,0:T(8,128)(2,1)}, s16[520,128]{1,0:T(8,128)(2,1)S(1)}, u32[]{:S(2)}) copy-start(s16[520,128]{1,0:T(8,128)(2,1)S(1)} %collective-permute-done.14.refs_5_) | copy-start | bytes 399364
  101.9 11.4 %collective-permute-start.15 = (s16[520,128]{1,0:T(8,128)(2,1)}, s16[520,128]{1,0:T(8,128)(2,1)S(1)}, u32[]{:S(2)}, u32[]{:S(2)}) collective-permute-start(s16[520,128]{1,0:T(8,128)(2,1)} %get-tuple-element.98), channel_id=1, source_target_pairs={{0,16},{4,20},{8,24},{12,28},{16,0},{20,4},{24,8},{28,12},{1,17},{... | collective-permute-start | bytes 399368 | tf_op jit(solution)/shard_map/ppermute | solution.py:461
  103.3 19.4 %copy-start.4 = (s16[520,128]{1,0:T(8,128)(2,1)}, s16[520,128]{1,0:T(8,128)(2,1)S(1)}, u32[]{:S(2)}) copy-start(s16[520,128]{1,0:T(8,128)(2,1)S(1)} %collective-permute-done.12.refs_4_) | copy-start | bytes 399364
  103.3 13.1 %collective-permute-start.24 = (s16[520,128]{1,0:T(8,128)(2,1)}, s16[520,128]{1,0:T(8,128)(2,1)S(1)}, u32[]{:S(2)}, u32[]{:S(2)}) collective-permute-start(s16[520,128]{1,0:T(8,128)(2,1)} %get-tuple-element.118), channel_id=1, source_target_pairs={{0,12},{4,8},{8,4},{12,0},{16,28},{20,24},{24,20},{28,16},{1,13},{... | collective-permute-start | bytes 399368 | tf_op jit(solution)/shard_map/ppermute | solution.py:461
  105.6 17.1 %copy-start.5 = (s16[520,128]{1,0:T(8,128)(2,1)}, s16[520,128]{1,0:T(8,128)(2,1)S(1)}, u32[]{:S(2)}) copy-start(s16[520,128]{1,0:T(8,128)(2,1)S(1)} %collective-permute-done.20.refs_8_) | copy-start | bytes 399364
  105.6 11.5 %collective-permute-start.21 = (s16[520,128]{1,0:T(8,128)(2,1)}, s16[520,128]{1,0:T(8,128)(2,1)S(1)}, u32[]{:S(2)}, u32[]{:S(2)}) collective-permute-start(s16[520,128]{1,0:T(8,128)(2,1)} %get-tuple-element.113), channel_id=1, source_target_pairs={{0,28},{4,24},{8,20},{12,16},{16,12},{20,8},{24,4},{28,0},{1,29},{... | collective-permute-start | bytes 399368 | tf_op jit(solution)/shard_map/ppermute | solution.py:461
  111.5 11.2 %copy-start.6 = (s16[520,128]{1,0:T(8,128)(2,1)}, s16[520,128]{1,0:T(8,128)(2,1)S(1)}, u32[]{:S(2)}) copy-start(s16[520,128]{1,0:T(8,128)(2,1)S(1)} %collective-permute-done.18.refs_7_) | copy-start | bytes 399364
  111.6 14.4 %collective-permute-start.27 = (s16[520,128]{1,0:T(8,128)(2,1)}, s16[520,128]{1,0:T(8,128)(2,1)S(1)}, u32[]{:S(2)}, u32[]{:S(2)}) collective-permute-start(s16[520,128]{1,0:T(8,128)(2,1)} %get-tuple-element.124), channel_id=1, source_target_pairs={{0,24},{4,28},{8,16},{12,20},{16,8},{20,12},{24,0},{28,4},{1,25},{... | collective-permute-start | bytes 399368 | tf_op jit(solution)/shard_map/ppermute | solution.py:461
  113.3 9.5 %copy-start.7 = (s16[520,128]{1,0:T(8,128)(2,1)}, s16[520,128]{1,0:T(8,128)(2,1)S(1)}, u32[]{:S(2)}) copy-start(s16[520,128]{1,0:T(8,128)(2,1)S(1)} %collective-permute-done.9.refs_3_) | copy-start | bytes 399364
  113.3 12.7 %collective-permute-start.23 = (s16[520,128]{1,0:T(8,128)(2,1)}, s16[520,128]{1,0:T(8,128)(2,1)}, u32[]{:S(2)}, u32[]{:S(2)}) collective-permute-start(s16[520,128]{1,0:T(8,128)(2,1)} %get-tuple-element.116), channel_id=1, source_target_pairs={{0,8},{4,12},{8,0},{12,4},{16,24},{20,28},{24,16},{28,20},{1,9},{5... | collective-permute-start | bytes 399368 | tf_op jit(solution)/shard_map/ppermute | solution.py:461
  113.3 9.5 %copy-start.8 = (s16[520,128]{1,0:T(8,128)(2,1)}, s16[520,128]{1,0:T(8,128)(2,1)S(1)}, u32[]{:S(2)}) copy-start(s16[520,128]{1,0:T(8,128)(2,1)S(1)} %collective-permute-done.15.refs_6_) | copy-start | bytes 399364
  113.3 15.1 %collective-permute-start.26 = (s16[520,128]{1,0:T(8,128)(2,1)}, s16[520,128]{1,0:T(8,128)(2,1)}, u32[]{:S(2)}, u32[]{:S(2)}) collective-permute-start(s16[520,128]{1,0:T(8,128)(2,1)} %get-tuple-element.122), channel_id=1, source_target_pairs={{0,20},{4,16},{8,28},{12,24},{16,4},{20,0},{24,12},{28,8},{1,21},{... | collective-permute-start | bytes 399368 | tf_op jit(solution)/shard_map/ppermute | solution.py:461
  116.4 6.4 %copy-start.9 = (s16[520,128]{1,0:T(8,128)(2,1)}, s16[520,128]{1,0:T(8,128)(2,1)S(1)}, u32[]{:S(2)}) copy-start(s16[520,128]{1,0:T(8,128)(2,1)S(1)} %collective-permute-done.24.refs_13_) | copy-start | bytes 399364
  116.4 13.7 %collective-permute-start.25 = (s16[520,128]{1,0:T(8,128)(2,1)}, s16[520,128]{1,0:T(8,128)(2,1)}, u32[]{:S(2)}, u32[]{:S(2)}) collective-permute-start(s16[520,128]{1,0:T(8,128)(2,1)} %get-tuple-element.120), channel_id=1, source_target_pairs={{0,16},{4,20},{8,24},{12,28},{16,0},{20,4},{24,8},{28,12},{1,17},{... | collective-permute-start | bytes 399368 | tf_op jit(solution)/shard_map/ppermute | solution.py:461
  117.2 5.7 %copy-start.11 = (s16[520,128]{1,0:T(8,128)(2,1)}, s16[520,128]{1,0:T(8,128)(2,1)S(1)}, u32[]{:S(2)}) copy-start(s16[520,128]{1,0:T(8,128)(2,1)S(1)} %collective-permute-done.21.refs_17_) | copy-start | bytes 399364
  117.2 12.9 %collective-permute-start.22 = (s16[520,128]{1,0:T(8,128)(2,1)}, s16[520,128]{1,0:T(8,128)(2,1)}, u32[]{:S(2)}, u32[]{:S(2)}) collective-permute-start(s16[520,128]{1,0:T(8,128)(2,1)} %get-tuple-element.114), channel_id=1, source_target_pairs={{0,4},{4,0},{8,12},{12,8},{16,20},{20,16},{24,28},{28,24},{1,5},{5... | collective-permute-start | bytes 399368 | tf_op jit(solution)/shard_map/ppermute | solution.py:461
  123.4 26.0 %copy-start.27 = (s32[1,256]{1,0:T(1,128)S(1)}, s32[1,256]{1,0:T(1,128)}, u32[]{:S(2)}) copy-start(s32[1,256]{1,0:T(1,128)} %get-tuple-element.128) | copy-start | bytes 3076
  126.0 4.1 %copy-start.21 = (s16[520,128]{1,0:T(8,128)(2,1)}, s16[520,128]{1,0:T(8,128)(2,1)S(1)}, u32[]{:S(2)}) copy-start(s16[520,128]{1,0:T(8,128)(2,1)S(1)} %collective-permute-done.27.refs_16_) | copy-start | bytes 399364
  143.1 14.5 %all-to-all-start.1 = ((f32[32,8,128]{2,1,0:T(8,128)}), f32[32,8,128]{2,1,0:T(8,128)S(1)}, u32[]{:S(2)}, u32[]{:S(2)}) async-start(f32[32,8,128]{2,1,0:T(8,128)} %get-tuple-element.127), calls=%async_computation.1 | async-start | bytes 262144 | tf_op jit(solution)/shard_map/all_to_all | solution.py:637
  157.6 0.7 copy-start.1
Sparse Core Ops, SparseCore 0:
  34.6 22.3 all-gather.2

commit v5 on v4

--- a/solution.py
+++ b/solution.py
@@ -16,6 +16,7 @@
 SUB = 16
 LANES = 128
 WINDOW = 5
+PAD = 8
 F32 = jnp.float32
 BF16 = jnp.bfloat16
 I16 = jnp.int16
@@ -126,21 +127,36 @@
         packed[slab, share] = code
 
 
-def rows_kernel(slabs, chunks, me_ref, x_ref, lead_ref, trail_ref, turn_ref, *rest):
-    outs, (stack, marks, high, low) = rest[: slabs * chunks], rest[slabs * chunks:]
+def rows_kernel(slabs, chunks, me_ref, x_hbm, lead_ref, trail_ref, turn_ref, *rest):
+    outs, (stack, marks, high, low, x_ref, arrival) = rest[: slabs * chunks], rest[slabs * chunks:]
     step, last = pl.program_id(0), pl.num_programs(0) - 1
     short = turn_ref.shape[1]
     halves, tile = short // LANES, high.shape[0] // RADIX
     rows = (outs[0].shape[0] - RADIX) // 2
     width = outs[0].shape[1]
-    stride = 2 * RADIX * halves
+    lines = 2 * RADIX * halves
+    stride = lines + PAD
+
+    def fetch(at):
+        begin = pl.multiple_of(at * tile, SUB)
+        return pltpu.make_async_copy(
+            x_hbm.at[pl.ds(begin, tile)], x_ref.at[pl.ds(begin, tile), pl.ds(0, lines)], arrival.at[at]
+        )
+
+    @pl.when(step == 0)
+    def _():
+        for at in range(rows // tile):
+            fetch(at).start()
+
+    fetch(step).wait()
+    x_flat = x_ref.reshape(rows * stride, LANES)
     for start in range(0, tile, SUB):
         for half in range(halves):
             values = []
             for n1 in range(RADIX):
-                at = start * stride + (n1 * halves + half) * 2
+                at = (step * tile + start) * stride + (n1 * halves + half) * 2
                 values.append(
-                    tuple(x_ref[pl.ds(at + part, SUB, stride=stride), :] for part in range(2))
+                    tuple(x_flat[pl.ds(at + part, SUB, stride=stride), :] for part in range(2))
                 )
             mixed = dft8(values, -1)
             for k1 in range(RADIX):
@@ -283,14 +299,17 @@
 
 def finish_kernel(slabs, chunks, me_ref, gain_ref, *rest):
     ins, rest = rest[:slabs * chunks], rest[slabs * chunks:]
-    lead_ref, trail_ref, turn_ref, prints_hbm, index_ref, out_ref, value_ref = rest[:7]
-    stack, scale, high, low, field, blocks, prints_ref, semaphore = rest[7:]
+    lead_ref, trail_ref, turn_ref, prints_hbm, index_ref, out_hbm, value_ref = rest[:7]
+    stack, scale, high, low, field, blocks, prints_ref, semaphore, out_ref, departure = rest[7:]
     step, last = pl.program_id(0), pl.num_programs(0) - 1
     short = turn_ref.shape[1]
     halves, tile = short // LANES, high.shape[0] // RADIX
     rows = stack.shape[2] // 2
     width = stack.shape[3]
-    stride = 2 * RADIX * halves
+    lines = 2 * RADIX * halves
+    stride = lines + PAD
+    out_flat = out_ref.reshape(rows * stride, LANES)
+    band_rows = prints_ref.shape[0] // LANES
 
     @pl.when(step == 0)
     def _():
@@ -337,18 +356,26 @@
                 column = n1 * halves + half
                 for part in range(2):
                     value = done[n1][part] * gain
-                    out_ref[pl.ds(start * stride + column * 2 + part, SUB, stride=stride), :] = value
-                    place = pl.multiple_of(step * tile + start, SUB)
+                    at = (step * tile + start) * stride + column * 2 + part
+                    out_flat[pl.ds(at, SUB, stride=stride), :] = value
+                    place = pl.multiple_of((step * tile + start) // band_rows * (band_rows + PAD), PAD)
                     field[part * RADIX * halves + column, pl.ds(place, SUB), :] = value
+
+    def store(at):
+        begin = pl.multiple_of(at * tile, SUB)
+        return pltpu.make_async_copy(
+            out_ref.at[pl.ds(begin, tile), pl.ds(0, lines)], out_hbm.at[pl.ds(begin, tile)], departure.at[at]
+        )
+
+    store(step).start()
 
     @pl.when(step == last)
     def _():
-        band_rows = prints_ref.shape[0] // LANES
-        bands = field.shape[1] // band_rows
+        bands = rows // band_rows
         count = field.shape[0]
         for column in range(count):
             for row in range(band_rows):
-                piece = field[column, pl.ds(row, bands, stride=band_rows), :]
+                piece = field[column, pl.ds(row, bands, stride=band_rows + PAD), :]
                 blocks[column * bands:(column + 1) * bands, row * LANES:(row + 1) * LANES] = (
                     piece.astype(BF16)
                 )
@@ -367,6 +394,8 @@
                 )
         for copy in range(1, value_ref.shape[0]):
             value_ref[copy] = value_ref[0]
+        for at in range(rows // tile):
+            store(at).wait()
 
 
 def small_kernel(
@@ -517,10 +546,9 @@
     gathered = lax.all_to_all(packed, "grid", split_axis=0, concat_axis=0, tiled=True)
     me_list, _ = lax.optimization_barrier((me_list, packed))
     column_tiles = width // LANES
+    lines = each * column_tiles
     flat = (
-        probes.reshape(rows, each, column_tiles, LANES)
-        .transpose(0, 2, 1, 3)
-        .reshape(rows * each * column_tiles, LANES)
+        probes.reshape(rows, each, column_tiles, LANES).transpose(0, 2, 1, 3).reshape(rows, lines, LANES)
     )
     payload = jax.ShapeDtypeStruct((2 * rows + RADIX, cut), I16)
 
@@ -532,30 +560,32 @@
         grid=(rows // tile,),
         in_specs=[
             smem(),
-            pl.BlockSpec((tile * each * column_tiles, LANES), lambda step: (step, 0)),
-            whole(lead.shape),
-            whole(trail.shape),
-            whole(turn_x.shape),
-        ],
-        out_specs=[whole(payload.shape)] * (chunks * slabs),
+            pl.BlockSpec(memory_space=pl.ANY),
+            vmem(),
+            vmem(),
+            vmem(),
+        ],
+        out_specs=[vmem()] * (chunks * slabs),
         out_shape=[payload] * (chunks * slabs),
         scratch_shapes=[
             pltpu.VMEM((chunks, slabs, 2 * rows, cut), I16),
             pltpu.VMEM((chunks, slabs, RADIX, cut), F32),
             pltpu.VMEM((RADIX * tile, 2 * short), BF16),
             pltpu.VMEM((RADIX * tile, 2 * short), BF16),
+            pltpu.VMEM((rows, lines + PAD, LANES), F32),
+            pltpu.SemaphoreType.DMA((rows // tile,)),
         ],
         compiler_params=params(),
         name="rows_forward",
     )(me_list, flat, lead, trail, turn_x)
 
-    gathered, _ = lax.optimization_barrier((gathered, sent[0]))
-    gathered = lax.all_gather(gathered, "probe", axis=0, tiled=False)
     history = []
     arrived = []
     for chunk in range(chunks):
         arrived.append(exchange(sent[chunk * slabs:(chunk + 1) * slabs], history))
 
+    gathered, _ = lax.optimization_barrier((gathered, history[:3]))
+    gathered = lax.all_gather(gathered, "probe", axis=0, tiled=False)
     halfway = []
     group = 256 // cut if cut % LANES == 0 else 1
     for chunk in range(chunks):
@@ -601,16 +631,16 @@
         lambda *refs: finish_kernel(slabs, chunks, *refs),
         grid=(rows // tile,),
         in_specs=[smem(), smem()]
-        + [whole(payload.shape)] * (chunks * slabs)
+        + [vmem()] * (chunks * slabs)
         + [
-            whole(lead.shape),
-            whole(trail.shape),
-            whole(turn_x.shape),
+            vmem(),
+            vmem(),
+            vmem(),
             pl.BlockSpec(memory_space=pl.ANY),
-            whole(index.shape),
+            vmem(),
         ],
         out_specs=[
-            pl.BlockSpec((tile * each * column_tiles, LANES), lambda step: (step, 0)),
+            pl.BlockSpec(memory_space=pl.ANY),
             whole((group_count, each * slots // LANES, LANES)),
         ],
         out_shape=[
@@ -622,10 +652,12 @@
             pltpu.VMEM((chunks, slabs, RADIX, cut), F32),
             pltpu.VMEM((RADIX * tile, 2 * short), BF16),
             pltpu.VMEM((RADIX * tile, 2 * short), BF16),
-            pltpu.VMEM((each * column_tiles, rows, LANES), F32),
+            pltpu.VMEM((lines, band_count * (band_rows + PAD), LANES), F32),
             pltpu.VMEM((each * column_tiles * band_count, band_rows * tile_cols), BF16),
             pltpu.VMEM(prints.shape, BF16),
             pltpu.SemaphoreType.DMA,
+            pltpu.VMEM((rows, lines + PAD, LANES), F32),
+            pltpu.SemaphoreType.DMA((rows // tile,)),
         ],
         compiler_params=params(),
         name="rows_back",

time: 168 us -> 164 us (0.976)
  Pallas kernels: 46.9 us -> 43.5 us
    all_to_all x1, waiting for transfers between devices: 4.55 us -> 0.01 us  [local(): lax.all_to_all(packed, 'grid', split_axis=0, concat_axis=0, tiled=True)]
    ppermute x28, starting transfers between devices: 44.4 us -> 47.8 us  [send(): return lax.ppermute(value, axis, pairs)]
    ppermute x28, waiting for transfers between devices: 20.5 us -> 23.6 us  [send(): return lax.ppermute(value, axis, pairs)]
    pallas_call x1, Pallas kernels: 13 us -> 10.4 us  [local(): pl.pallas_call(lambda *refs: finish_kernel(slabs, chunks, *refs), grid=(r...]
    all_to_all x1, starting transfers between devices: 6.23 us -> 3.77 us  [local(): lax.all_to_all(values, ('grid', 'probe'), split_axis=0, concat_axis=0, ti...]
  transfers between devices with their start and end apart: 31 -> 31, of which waited for: 11 -> 9; matrix products, arithmetic and copies ran while one was open for 7% -> 7% of each run, Pallas kernels for 17% -> 17%
where the time goes in v5:
time: 164 us; the launch traced here: 163 us
  starting transfers between devices  58.8 us (36%)
  Pallas kernels  43.5 us (27%)
  waiting for transfers between devices  30.8 us (19%)
  between operations  16.3 us (10%)
  local copies, waits for them, and re-layouts  9.22 us (6%)
  other arithmetic  4.51 us (3%)
    ppermute x28, starting transfers between devices, send(): return lax.ppermute(value, axis, pairs)  47.8 us
    ppermute x28, waiting for transfers between devices, send(): return lax.ppermute(value, axis, pairs)  23.6 us
    pallas_call x2, Pallas kernels, local(): pl.pallas_call(lambda *refs, chunk=chunk: columns_kernel(slabs, chunk, he...  17.8 us
    pallas_call x1, Pallas kernels, local(): pl.pallas_call(lambda *refs: finish_kernel(slabs, chunks, *refs), grid=(r...  10.4 us
    pallas_call x1, Pallas kernels, local(): pl.pallas_call(lambda *refs: rows_kernel(slabs, chunks, *refs), grid=(row...  9.78 us
    all_to_all x1, starting transfers between devices, local(): lax.all_to_all(packed, 'grid', split_axis=0, concat_axis=0, tiled=True)  7.28 us
    all_to_all x1, waiting for transfers between devices, local(): lax.all_to_all(values, ('grid', 'probe'), split_axis=0, concat_axis=0, ti...  7.17 us
    all_to_all x1, starting transfers between devices, local(): lax.all_to_all(values, ('grid', 'probe'), split_axis=0, concat_axis=0, ti...  3.77 us
  transfers between devices with their start and end apart: 31, of which 9 were waited for; matrix products, arithmetic and copies ran while one was open for 7% of the time, Pallas kernels for 17%

profile of v5, /device:TPU:0, one launch (start us, length us, event | category | flops | bytes accessed | tf_op | source)
XLA Modules:
  0.0 163.2 jit_solution(7911074619851050174)
XLA Ops:
  7.2 0.6 pad_add_fusion.refs_0_
  7.8 3.4 %pack_prints.1 = (bf16[8,17,16,128]{3,2,1,0:T(8,128)(2,1)}, s32[1,256]{1,0:T(1,128)}) custom-call(s32[2]{0:T(128)} %pad_add_fusion.refs_0_, s32[1,256]{1,0:T(1,128)} %bitcast.43, s32[1,256]{1,0:T(1,128)} %bitcast.44, s32[1,256]{1,0:T(1,128)} %bitcast.45, bf16[256,16,128]{2,1,0:T(8,128)(2,1)} %refs_4_.2), custom_call_target="tpu_custom_call" | custom-call | tf_op jit(solution)/shard_map/pack_prints/pallas_call | solution.py:524
  11.2 7.3 %all-to-all-start = ((bf16[8,17,16,128]{3,2,1,0:T(8,128)(2,1)}), bf16[8,17,16,128]{3,2,1,0:T(8,128)(2,1)S(1)}, u32[]{:S(2)}, u32[]{:S(2)}) async-start(bf16[8,17,16,128]{3,2,1,0:T(8,128)(2,1)} %get-tuple-element.68), calls=%async_computation | async-start | bytes 1114112 | tf_op jit(solution)/shard_map/all_to_all | solution.py:546
  18.4 0.0 all-gather.3.cloned.1.call-start
  18.5 0.0 copy-start.26
  18.5 9.8 %rows_forward.1 = (s16[520,128]{1,0:T(8,128)(2,1)}, s16[520,128]{1,0:T(8,128)(2,1)}, s16[520,128]{1,0:T(8,128)(2,1)}, s16[520,128]{1,0:T(8,128)(2,1)}, s16[520,1...) custom-call(s32[2]{0:T(128)} %pad_add_fusion.refs_0_, ...), custom_call_target="tpu_custom_call" | custom-call | tf_op jit(solution)/shard_map/rows_forward/pallas_call | solution.py:558
  28.3 2.9 %collective-permute-start.3 = (s16[520,128]{1,0:T(8,128)(2,1)}, s16[520,128]{1,0:T(8,128)(2,1)S(1)}, u32[]{:S(2)}, u32[]{:S(2)}) collective-permute-start(s16[520,128]{1,0:T(8,128)(2,1)} %get-tuple-element.75), channel_id=1, source_target_pairs={{0,12},{4,8},{8,4},{12,0},{16,28},{20,24},{24,20},{28,16},{1,13},{... | collective-permute-start | bytes 399368 | tf_op jit(solution)/shard_map/ppermute | solution.py:490
  31.2 2.4 %collective-permute-start = (s16[520,128]{1,0:T(8,128)(2,1)}, s16[520,128]{1,0:T(8,128)(2,1)S(1)}, u32[]{:S(2)}, u32[]{:S(2)}) collective-permute-start(s16[520,128]{1,0:T(8,128)(2,1)} %get-tuple-element.72), channel_id=1, source_target_pairs={{0,28},{4,24},{8,20},{12,16},{16,12},{20,8},{24,4},{28,0},{1,29},{... | collective-permute-start | bytes 399368 | tf_op jit(solution)/shard_map/ppermute | solution.py:490
  33.6 1.5 collective-permute-start.6
  35.1 1.0 collective-permute-done.3.refs_5_
  36.1 4.7 %collective-permute-done.refs_9_ = s16[520,128]{1,0:T(8,128)(2,1)S(1)} collective-permute-done((s16[520,128]{1,0:T(8,128)(2,1)}, s16[520,128]{1,0:T(8,128)(2,1)S(1)}, u32[]{:S(2)}, u32[]{:S(2)}) %collective-permute-start) | collective-permute-done | bytes 133152 | tf_op jit(solution)/shard_map/ppermute | solution.py:490
  40.7 1.5 collective-permute-done.6.refs_8_
  42.2 0.8 copy-done
  43.0 0.0 all-gather.3.cloned.1.call-update
  43.1 3.7 %collective-permute-start.2 = (s16[520,128]{1,0:T(8,128)(2,1)}, s16[520,128]{1,0:T(8,128)(2,1)S(1)}, u32[]{:S(2)}, u32[]{:S(2)}) collective-permute-start(s16[520,128]{1,0:T(8,128)(2,1)} %get-tuple-element.74), channel_id=1, source_target_pairs={{0,8},{4,12},{8,0},{12,4},{16,24},{20,28},{24,16},{28,20},{1,9},{5... | collective-permute-start | bytes 399368 | tf_op jit(solution)/shard_map/ppermute | solution.py:490
  46.8 1.9 %collective-permute-start.5 = (s16[520,128]{1,0:T(8,128)(2,1)}, s16[520,128]{1,0:T(8,128)(2,1)S(1)}, u32[]{:S(2)}, u32[]{:S(2)}) collective-permute-start(s16[520,128]{1,0:T(8,128)(2,1)} %get-tuple-element.78), channel_id=1, source_target_pairs={{0,20},{4,16},{8,28},{12,24},{16,4},{20,0},{24,12},{28,8},{1,21},{... | collective-permute-start | bytes 399368 | tf_op jit(solution)/shard_map/ppermute | solution.py:490
  48.7 0.6 collective-permute-start.1
  49.3 2.2 %collective-permute-start.10 = (s16[520,128]{1,0:T(8,128)(2,1)}, s16[520,128]{1,0:T(8,128)(2,1)S(1)}, u32[]{:S(2)}, u32[]{:S(2)}) collective-permute-start(s16[520,128]{1,0:T(8,128)(2,1)} %get-tuple-element.90), channel_id=1, source_target_pairs={{0,28},{4,24},{8,20},{12,16},{16,12},{20,8},{24,4},{28,0},{1,29},{... | collective-permute-start | bytes 399368 | tf_op jit(solution)/shard_map/ppermute | solution.py:490
  51.5 2.1 %collective-permute-start.4 = (s16[520,128]{1,0:T(8,128)(2,1)}, s16[520,128]{1,0:T(8,128)(2,1)S(1)}, u32[]{:S(2)}, u32[]{:S(2)}) collective-permute-start(s16[520,128]{1,0:T(8,128)(2,1)} %get-tuple-element.77), channel_id=1, source_target_pairs={{0,16},{4,20},{8,24},{12,28},{16,0},{20,4},{24,8},{28,12},{1,17},{... | collective-permute-start | bytes 399368 | tf_op jit(solution)/shard_map/ppermute | solution.py:490
  53.6 1.0 collective-permute-start.16
  54.6 8.0 %collective-permute-done.5.refs_7_ = s16[520,128]{1,0:T(8,128)(2,1)S(1)} collective-permute-done((s16[520,128]{1,0:T(8,128)(2,1)}, s16[520,128]{1,0:T(8,128)(2,1)S(1)}, u32[]{:S(2)}, u32[]{:S(2)}) %collective-permute-start.5) | collective-permute-done | bytes 133152 | tf_op jit(solution)/shard_map/ppermute | solution.py:490
  62.6 2.2 %collective-permute-start.7 = (s16[520,128]{1,0:T(8,128)(2,1)}, s16[520,128]{1,0:T(8,128)(2,1)S(1)}, u32[]{:S(2)}, u32[]{:S(2)}) collective-permute-start(s16[520,128]{1,0:T(8,128)(2,1)} %get-tuple-element.84), channel_id=1, source_target_pairs={{0,24},{4,28},{8,16},{12,20},{16,8},{20,12},{24,0},{28,4},{1,25},{... | collective-permute-start | bytes 399368 | tf_op jit(solution)/shard_map/ppermute | solution.py:490
  64.8 0.0 collective-permute-done.1.refs_3_
  64.8 0.0 collective-permute-done.10.refs_9_
  64.8 2.9 %collective-permute-start.11 = (s16[520,128]{1,0:T(8,128)(2,1)}, s16[520,128]{1,0:T(8,128)(2,1)S(1)}, u32[]{:S(2)}, u32[]{:S(2)}) collective-permute-start(s16[520,128]{1,0:T(8,128)(2,1)} %get-tuple-element.91), channel_id=1, source_target_pairs={{0,4},{4,0},{8,12},{12,8},{16,20},{20,16},{24,28},{28,24},{1,5},{5... | collective-permute-start | bytes 399368 | tf_op jit(solution)/shard_map/ppermute | solution.py:490
  67.7 3.8 %collective-permute-done.4.refs_6_ = s16[520,128]{1,0:T(8,128)(2,1)S(1)} collective-permute-done((s16[520,128]{1,0:T(8,128)(2,1)}, s16[520,128]{1,0:T(8,128)(2,1)S(1)}, u32[]{:S(2)}, u32[]{:S(2)}) %collective-permute-start.4) | collective-permute-done | bytes 133152 | tf_op jit(solution)/shard_map/ppermute | solution.py:490
  71.5 0.0 collective-permute-start.19
  71.5 1.2 collective-permute-start.17
  72.8 8.9 %columns.2 = (s16[520,128]{1,0:T(8,128)(2,1)}, s16[520,128]{1,0:T(8,128)(2,1)}, s16[520,128]{1,0:T(8,128)(2,1)}, s16[520,128]{1,0:T(8,128)(2,1)}, s16[520,128]{1...) custom-call(s32[2]{0:T(128)} %pad_add_fusion.refs_0_, f32[2]{0:T(128)} %refs_1_.3, ...), custom_call_target="tpu_custom_call" | custom-call | tf_op jit(solution)/shard_map/columns/pallas_call | solution.py:592
  81.7 5.2 %collective-permute-start.8 = (s16[520,128]{1,0:T(8,128)(2,1)}, s16[520,128]{1,0:T(8,128)(2,1)S(1)}, u32[]{:S(2)}, u32[]{:S(2)}) collective-permute-start(s16[520,128]{1,0:T(8,128)(2,1)} %get-tuple-element.85), channel_id=1, source_target_pairs={{0,28},{4,24},{8,20},{12,16},{16,12},{20,8},{24,4},{28,0},{1,29},{... | collective-permute-start | bytes 399368 | tf_op jit(solution)/shard_map/ppermute | solution.py:490
  86.9 0.0 collective-permute-done.11.refs_3_
  86.9 0.1 collective-permute-start.12
  87.0 2.0 %collective-permute-start.20 = (s16[520,128]{1,0:T(8,128)(2,1)}, s16[520,128]{1,0:T(8,128)(2,1)S(1)}, u32[]{:S(2)}, u32[]{:S(2)}) collective-permute-start(s16[520,128]{1,0:T(8,128)(2,1)} %get-tuple-element.108), channel_id=1, source_target_pairs={{0,24},{4,28},{8,16},{12,20},{16,8},{20,12},{24,0},{28,4},{1,25},{... | collective-permute-start | bytes 399368 | tf_op jit(solution)/shard_map/ppermute | solution.py:490
  89.0 0.6 fusion.6
  90.8 0.0 collective-permute-done.17.refs_6_
  90.9 2.4 %collective-permute-start.18 = (s16[520,128]{1,0:T(8,128)(2,1)}, s16[520,128]{1,0:T(8,128)(2,1)S(1)}, u32[]{:S(2)}, u32[]{:S(2)}) collective-permute-start(s16[520,128]{1,0:T(8,128)(2,1)} %get-tuple-element.104), channel_id=1, source_target_pairs={{0,20},{4,16},{8,28},{12,24},{16,4},{20,0},{24,12},{28,8},{1,21},{... | collective-permute-start | bytes 399368 | tf_op jit(solution)/shard_map/ppermute | solution.py:490
  93.3 1.3 collective-permute-start.9
  94.6 8.9 %columns.3 = (s16[520,128]{1,0:T(8,128)(2,1)}, s16[520,128]{1,0:T(8,128)(2,1)}, s16[520,128]{1,0:T(8,128)(2,1)}, s16[520,128]{1,0:T(8,128)(2,1)}, s16[520,128]{1...) custom-call(s32[2]{0:T(128)} %pad_add_fusion.refs_0_, f32[2]{0:T(128)} %refs_1_.3, ...), custom_call_target="tpu_custom_call" | custom-call | tf_op jit(solution)/shard_map/columns/pallas_call | solution.py:592
  103.5 3.0 %collective-permute-start.15 = (s16[520,128]{1,0:T(8,128)(2,1)}, s16[520,128]{1,0:T(8,128)(2,1)S(1)}, u32[]{:S(2)}, u32[]{:S(2)}) collective-permute-start(s16[520,128]{1,0:T(8,128)(2,1)} %get-tuple-element.98), channel_id=1, source_target_pairs={{0,16},{4,20},{8,24},{12,28},{16,0},{20,4},{24,8},{28,12},{1,17},{... | collective-permute-start | bytes 399368 | tf_op jit(solution)/shard_map/ppermute | solution.py:490
  106.5 0.2 collective-permute-start.24
  106.7 2.6 %collective-permute-start.21 = (s16[520,128]{1,0:T(8,128)(2,1)}, s16[520,128]{1,0:T(8,128)(2,1)S(1)}, u32[]{:S(2)}, u32[]{:S(2)}) collective-permute-start(s16[520,128]{1,0:T(8,128)(2,1)} %get-tuple-element.113), channel_id=1, source_target_pairs={{0,28},{4,24},{8,20},{12,16},{16,12},{20,8},{24,4},{28,0},{1,29},{... | collective-permute-start | bytes 399368 | tf_op jit(solution)/shard_map/ppermute | solution.py:490
  109.3 2.9 %fusion.1 = f32[]{:T(128)} fusion(f32[1025]{0:T(1024)S(1)} %fusion.4, f32[1025]{0:T(1024)S(1)} %get-tuple-element.134, f32[1025]{0:T(1024)S(1)} %get-tuple-element.135), kind=kLoop, calls=%fused_computation.2 | loop fusion | flops 6303749 | bytes 12304 | tf_op jit(solution)/shard_map/reduce_sum | solution.py:483
  112.9 2.0 %collective-permute-start.27 = (s16[520,128]{1,0:T(8,128)(2,1)}, s16[520,128]{1,0:T(8,128)(2,1)S(1)}, u32[]{:S(2)}, u32[]{:S(2)}) collective-permute-start(s16[520,128]{1,0:T(8,128)(2,1)} %get-tuple-element.124), channel_id=1, source_target_pairs={{0,24},{4,28},{8,16},{12,20},{16,8},{20,12},{24,0},{28,4},{1,25},{... | collective-permute-start | bytes 399368 | tf_op jit(solution)/shard_map/ppermute | solution.py:490
  114.9 0.2 collective-permute-start.23
  115.1 2.9 %collective-permute-start.26 = (s16[520,128]{1,0:T(8,128)(2,1)}, s16[520,128]{1,0:T(8,128)(2,1)}, u32[]{:S(2)}, u32[]{:S(2)}) collective-permute-start(s16[520,128]{1,0:T(8,128)(2,1)} %get-tuple-element.122), channel_id=1, source_target_pairs={{0,20},{4,16},{8,28},{12,24},{16,4},{20,0},{24,12},{28,8},{1,21},{... | collective-permute-start | bytes 399368 | tf_op jit(solution)/shard_map/ppermute | solution.py:490
  118.1 0.2 collective-permute-start.25
  118.2 1.2 collective-permute-done.21.refs_17_
  119.4 1.2 collective-permute-start.22
  120.7 0.9 slice.17
  121.5 2.0 %slice.16 = bf16[4,8,16,16,128]{4,3,2,1,0:T(8,128)(2,1)S(1)} slice(bf16[4,8,17,16,128]{4,3,2,1,0:T(8,128)(2,1)} %bitcast.41), slice={[0:4], [0:8], [0:16], [0:16], [0:128]} | slice | bytes 4194304 | tf_op jit(solution)/shard_map/slice | solution.py:625
  123.5 0.1 constant_dynamic-slice_fusion
  123.6 0.7 reshape.96.refs_22_
  124.3 0.4 copy.35
  124.7 0.5 copy.43
  125.3 0.0 copy-start.27
  125.3 2.6 %copy.33.refs_21_ = bf16[2048,512]{1,0:T(8,128)(2,1)} copy(bf16[2048,512]{0,1:T(8,128)(2,1)S(1)} %bitcast.38) | data formatting | bytes 4194304 | tf_op jit(solution)/shard_map/reshape | solution.py:625
  127.8 2.1 %collective-permute-done.26.refs_15_ = s16[520,128]{1,0:T(8,128)(2,1)} collective-permute-done((s16[520,128]{1,0:T(8,128)(2,1)}, s16[520,128]{1,0:T(8,128)(2,1)}, u32[]{:S(2)}, u32[]{:S(2)}) %collective-permute-start.26) | collective-permute-done | bytes 133152 | tf_op jit(solution)/shard_map/ppermute | solution.py:490
  130.0 1.2 collective-permute-done.25.refs_14_
  131.2 10.4 %rows_back.1 = (f32[256,32,128]{2,1,0:T(8,128)}, f32[32,8,128]{2,1,0:T(8,128)}) custom-call(s32[2]{0:T(128)} %pad_add_fusion.refs_0_, f32[1]{0:T(128)} %bitcast.7.refs_1_, s16[520,128]{1,0:T(8,128)(2,1)} %get-tuple-element.80.refs_2_, s16[520,128]{1,0:T(8,128)(2,1)} %copy-done.7, s16[520,128]{1,0:T(8,128)(2,1)} %copy-done.4, s16[520,128]{1,0:T(8,128)(2,1)} %copy-done.3, ...), custom_call_target="tpu_custom_call" | custom-call | tf_op jit(solution)/shard_map/rows_back/pallas_call | solution.py:630
  141.6 3.8 %all-to-all-start.1 = ((f32[32,8,128]{2,1,0:T(8,128)}), f32[32,8,128]{2,1,0:T(8,128)S(1)}, u32[]{:S(2)}, u32[]{:S(2)}) async-start(f32[32,8,128]{2,1,0:T(8,128)} %get-tuple-element.127), calls=%async_computation.1 | async-start | bytes 262144 | tf_op jit(solution)/shard_map/all_to_all | solution.py:669
  145.4 1.0 fusion.2.refs_2_
  146.5 7.2 %all-to-all-done.1.refs_1_ = f32[32,8,128]{2,1,0:T(8,128)S(1)} async-done(((f32[32,8,128]{2,1,0:T(8,128)}), f32[32,8,128]{2,1,0:T(8,128)S(1)}, u32[]{:S(2)}, u32[]{:S(2)}) %all-to-all-start.1) | async-done | bytes 131104 | tf_op jit(solution)/shard_map/all_to_all | solution.py:669
  153.6 0.7 copy-done.1
  154.3 2.1 %factor_basis.1 = (f32[2,256]{1,0:T(2,128)}, f32[8,8]{1,0:T(8,128)}, f32[2,256]{1,0:T(2,128)}) custom-call(s32[2]{0:T(128)} %pad_add_fusion.refs_0_, f32[32,8,128]{2,1,0:T(8,128)} %copy-done.1, bf16[1024,256]{1,0:T(8,128)(2,1)} %fusion.2.refs_2_), custom_call_target="tpu_custom_call" | custom-call | tf_op jit(solution)/shard_map/factor_basis/pallas_call | solution.py:673
  (76 shorter events, 0.2 us)
Async XLA Ops:
  11.2 31.0 %all-to-all-start = ((bf16[8,17,16,128]{3,2,1,0:T(8,128)(2,1)}), bf16[8,17,16,128]{3,2,1,0:T(8,128)(2,1)S(1)}, u32[]{:S(2)}, u32[]{:S(2)}) async-start(bf16[8,17,16,128]{3,2,1,0:T(8,128)(2,1)} %get-tuple-element.68), calls=%async_computation | async-start | bytes 1114112 | tf_op jit(solution)/shard_map/all_to_all | solution.py:546
  18.4 102.2 %all-gather.3.cloned.1.call-start = ((), (), s32[]{:S(2)}) async-start(), calls=%async_computation.2 | async-start | bytes 2785280 | tf_op jit(solution)/shard_map/all_gather | solution.py:588
  18.5 70.5 %copy-start.26 = (f32[2]{0:T(128)S(1)}, f32[2]{0:T(128)}, u32[]{:S(2)}) copy-start(f32[2]{0:T(128)} %refs_1_.3) | copy-start | bytes 28
  28.3 7.8 %collective-permute-start.3 = (s16[520,128]{1,0:T(8,128)(2,1)}, s16[520,128]{1,0:T(8,128)(2,1)S(1)}, u32[]{:S(2)}, u32[]{:S(2)}) collective-permute-start(s16[520,128]{1,0:T(8,128)(2,1)} %get-tuple-element.75), channel_id=1, source_target_pairs={{0,12},{4,8},{8,4},{12,0},{16,28},{20,24},{24,20},{28,16},{1,13},{... | collective-permute-start | bytes 399368 | tf_op jit(solution)/shard_map/ppermute | solution.py:490
  31.2 9.5 %collective-permute-start = (s16[520,128]{1,0:T(8,128)(2,1)}, s16[520,128]{1,0:T(8,128)(2,1)S(1)}, u32[]{:S(2)}, u32[]{:S(2)}) collective-permute-start(s16[520,128]{1,0:T(8,128)(2,1)} %get-tuple-element.72), channel_id=1, source_target_pairs={{0,28},{4,24},{8,20},{12,16},{16,12},{20,8},{24,4},{28,0},{1,29},{... | collective-permute-start | bytes 399368 | tf_op jit(solution)/shard_map/ppermute | solution.py:490
  33.6 8.6 %collective-permute-start.6 = (s16[520,128]{1,0:T(8,128)(2,1)}, s16[520,128]{1,0:T(8,128)(2,1)S(1)}, u32[]{:S(2)}, u32[]{:S(2)}) collective-permute-start(s16[520,128]{1,0:T(8,128)(2,1)} %get-tuple-element.79), channel_id=1, source_target_pairs={{0,24},{4,28},{8,16},{12,20},{16,8},{20,12},{24,0},{28,4},{1,25},{... | collective-permute-start | bytes 399368 | tf_op jit(solution)/shard_map/ppermute | solution.py:490
  36.1 36.6 %copy-start.16 = (s16[520,128]{1,0:T(8,128)(2,1)}, s16[520,128]{1,0:T(8,128)(2,1)S(1)}, u32[]{:S(2)}) copy-start(s16[520,128]{1,0:T(8,128)(2,1)S(1)} %collective-permute-done.3.refs_5_) | copy-start | bytes 399364
  40.7 32.0 %copy-start.17 = (s16[520,128]{1,0:T(8,128)(2,1)}, s16[520,128]{1,0:T(8,128)(2,1)S(1)}, u32[]{:S(2)}) copy-start(s16[520,128]{1,0:T(8,128)(2,1)S(1)} %collective-permute-done.refs_9_) | copy-start | bytes 399364
  42.2 30.5 %copy-start.19 = (s16[520,128]{1,0:T(8,128)(2,1)}, s16[520,128]{1,0:T(8,128)(2,1)S(1)}, u32[]{:S(2)}) copy-start(s16[520,128]{1,0:T(8,128)(2,1)S(1)} %collective-permute-done.6.refs_8_) | copy-start | bytes 399364
  42.2 0.8 copy-start
  43.1 10.5 %collective-permute-start.2 = (s16[520,128]{1,0:T(8,128)(2,1)}, s16[520,128]{1,0:T(8,128)(2,1)S(1)}, u32[]{:S(2)}, u32[]{:S(2)}) collective-permute-start(s16[520,128]{1,0:T(8,128)(2,1)} %get-tuple-element.74), channel_id=1, source_target_pairs={{0,8},{4,12},{8,0},{12,4},{16,24},{20,28},{24,16},{28,20},{1,9},{5... | collective-permute-start | bytes 399368 | tf_op jit(solution)/shard_map/ppermute | solution.py:490
  46.8 15.8 %collective-permute-start.5 = (s16[520,128]{1,0:T(8,128)(2,1)}, s16[520,128]{1,0:T(8,128)(2,1)S(1)}, u32[]{:S(2)}, u32[]{:S(2)}) collective-permute-start(s16[520,128]{1,0:T(8,128)(2,1)} %get-tuple-element.78), channel_id=1, source_target_pairs={{0,20},{4,16},{8,28},{12,24},{16,4},{20,0},{24,12},{28,8},{1,21},{... | collective-permute-start | bytes 399368 | tf_op jit(solution)/shard_map/ppermute | solution.py:490
  48.7 16.1 %collective-permute-start.1 = (s16[520,128]{1,0:T(8,128)(2,1)}, s16[520,128]{1,0:T(8,128)(2,1)S(1)}, u32[]{:S(2)}, u32[]{:S(2)}) collective-permute-start(s16[520,128]{1,0:T(8,128)(2,1)} %get-tuple-element.73), channel_id=1, source_target_pairs={{0,4},{4,0},{8,12},{12,8},{16,20},{20,16},{24,28},{28,24},{1,5},{5... | collective-permute-start | bytes 399368 | tf_op jit(solution)/shard_map/ppermute | solution.py:490
  49.3 15.5 %collective-permute-start.10 = (s16[520,128]{1,0:T(8,128)(2,1)}, s16[520,128]{1,0:T(8,128)(2,1)S(1)}, u32[]{:S(2)}, u32[]{:S(2)}) collective-permute-start(s16[520,128]{1,0:T(8,128)(2,1)} %get-tuple-element.90), channel_id=1, source_target_pairs={{0,28},{4,24},{8,20},{12,16},{16,12},{20,8},{24,4},{28,0},{1,29},{... | collective-permute-start | bytes 399368 | tf_op jit(solution)/shard_map/ppermute | solution.py:490
  51.5 20.0 %collective-permute-start.4 = (s16[520,128]{1,0:T(8,128)(2,1)}, s16[520,128]{1,0:T(8,128)(2,1)S(1)}, u32[]{:S(2)}, u32[]{:S(2)}) collective-permute-start(s16[520,128]{1,0:T(8,128)(2,1)} %get-tuple-element.77), channel_id=1, source_target_pairs={{0,16},{4,20},{8,24},{12,28},{16,0},{20,4},{24,8},{28,12},{1,17},{... | collective-permute-start | bytes 399368 | tf_op jit(solution)/shard_map/ppermute | solution.py:490
  53.6 19.2 %copy-start.22 = (s16[520,128]{1,0:T(8,128)(2,1)}, s16[520,128]{1,0:T(8,128)(2,1)S(1)}, u32[]{:S(2)}) copy-start(s16[520,128]{1,0:T(8,128)(2,1)S(1)} %collective-permute-done.2.refs_4_) | copy-start | bytes 399364
  53.6 17.9 %collective-permute-start.16 = (s16[520,128]{1,0:T(8,128)(2,1)}, s16[520,128]{1,0:T(8,128)(2,1)S(1)}, u32[]{:S(2)}, u32[]{:S(2)}) collective-permute-start(s16[520,128]{1,0:T(8,128)(2,1)} %get-tuple-element.102), channel_id=1, source_target_pairs={{0,12},{4,8},{8,4},{12,0},{16,28},{20,24},{24,20},{28,16},{1,13},{... | collective-permute-start | bytes 399368 | tf_op jit(solution)/shard_map/ppermute | solution.py:490
  62.6 10.2 %copy-start.23 = (s16[520,128]{1,0:T(8,128)(2,1)}, s16[520,128]{1,0:T(8,128)(2,1)S(1)}, u32[]{:S(2)}) copy-start(s16[520,128]{1,0:T(8,128)(2,1)S(1)} %collective-permute-done.5.refs_7_) | copy-start | bytes 399364
  62.6 19.1 %collective-permute-start.7 = (s16[520,128]{1,0:T(8,128)(2,1)}, s16[520,128]{1,0:T(8,128)(2,1)S(1)}, u32[]{:S(2)}, u32[]{:S(2)}) collective-permute-start(s16[520,128]{1,0:T(8,128)(2,1)} %get-tuple-element.84), channel_id=1, source_target_pairs={{0,24},{4,28},{8,16},{12,20},{16,8},{20,12},{24,0},{28,4},{1,25},{... | collective-permute-start | bytes 399368 | tf_op jit(solution)/shard_map/ppermute | solution.py:490
  64.8 8.0 %copy-start.24 = (s16[520,128]{1,0:T(8,128)(2,1)}, s16[520,128]{1,0:T(8,128)(2,1)S(1)}, u32[]{:S(2)}) copy-start(s16[520,128]{1,0:T(8,128)(2,1)S(1)} %collective-permute-done.1.refs_3_) | copy-start | bytes 399364
  64.8 22.1 %collective-permute-start.13 = (s16[520,128]{1,0:T(8,128)(2,1)}, s16[520,128]{1,0:T(8,128)(2,1)S(1)}, u32[]{:S(2)}, u32[]{:S(2)}) collective-permute-start(s16[520,128]{1,0:T(8,128)(2,1)} %get-tuple-element.95), channel_id=1, source_target_pairs={{0,8},{4,12},{8,0},{12,4},{16,24},{20,28},{24,16},{28,20},{1,9},{5... | collective-permute-start | bytes 399368 | tf_op jit(solution)/shard_map/ppermute | solution.py:490
  64.8 29.7 %copy-start.10 = (s16[520,128]{1,0:T(8,128)(2,1)}, s16[520,128]{1,0:T(8,128)(2,1)S(1)}, u32[]{:S(2)}) copy-start(s16[520,128]{1,0:T(8,128)(2,1)S(1)} %collective-permute-done.10.refs_9_) | copy-start | bytes 399364
  64.8 22.1 %collective-permute-start.11 = (s16[520,128]{1,0:T(8,128)(2,1)}, s16[520,128]{1,0:T(8,128)(2,1)S(1)}, u32[]{:S(2)}, u32[]{:S(2)}) collective-permute-start(s16[520,128]{1,0:T(8,128)(2,1)} %get-tuple-element.91), channel_id=1, source_target_pairs={{0,4},{4,0},{8,12},{12,8},{16,20},{20,16},{24,28},{28,24},{1,5},{5... | collective-permute-start | bytes 399368 | tf_op jit(solution)/shard_map/ppermute | solution.py:490
  71.5 1.3 copy-start.25
  71.5 15.5 %collective-permute-start.19 = (s16[520,128]{1,0:T(8,128)(2,1)}, s16[520,128]{1,0:T(8,128)(2,1)S(1)}, u32[]{:S(2)}, u32[]{:S(2)}) collective-permute-start(s16[520,128]{1,0:T(8,128)(2,1)} %get-tuple-element.107), channel_id=1, source_target_pairs={{0,20},{4,16},{8,28},{12,24},{16,4},{20,0},{24,12},{28,8},{1,21},{... | collective-permute-start | bytes 399368 | tf_op jit(solution)/shard_map/ppermute | solution.py:490
  71.5 23.0 %copy-start.12 = (s16[520,128]{1,0:T(8,128)(2,1)}, s16[520,128]{1,0:T(8,128)(2,1)S(1)}, u32[]{:S(2)}) copy-start(s16[520,128]{1,0:T(8,128)(2,1)S(1)} %collective-permute-done.16.refs_5_) | copy-start | bytes 399364
  71.5 19.3 %collective-permute-start.17 = (s16[520,128]{1,0:T(8,128)(2,1)}, s16[520,128]{1,0:T(8,128)(2,1)S(1)}, u32[]{:S(2)}, u32[]{:S(2)}) collective-permute-start(s16[520,128]{1,0:T(8,128)(2,1)} %get-tuple-element.103), channel_id=1, source_target_pairs={{0,16},{4,20},{8,24},{12,28},{16,0},{20,4},{24,8},{28,12},{1,17},{... | collective-permute-start | bytes 399368 | tf_op jit(solution)/shard_map/ppermute | solution.py:490
  81.7 12.9 %copy-start.13 = (s16[520,128]{1,0:T(8,128)(2,1)}, s16[520,128]{1,0:T(8,128)(2,1)S(1)}, u32[]{:S(2)}) copy-start(s16[520,128]{1,0:T(8,128)(2,1)S(1)} %collective-permute-done.7.refs_8_) | copy-start | bytes 399364
  81.7 11.6 %collective-permute-start.8 = (s16[520,128]{1,0:T(8,128)(2,1)}, s16[520,128]{1,0:T(8,128)(2,1)S(1)}, u32[]{:S(2)}, u32[]{:S(2)}) collective-permute-start(s16[520,128]{1,0:T(8,128)(2,1)} %get-tuple-element.85), channel_id=1, source_target_pairs={{0,28},{4,24},{8,20},{12,16},{16,12},{20,8},{24,4},{28,0},{1,29},{... | collective-permute-start | bytes 399368 | tf_op jit(solution)/shard_map/ppermute | solution.py:490
  86.9 7.7 %copy-start.14 = (s16[520,128]{1,0:T(8,128)(2,1)}, s16[520,128]{1,0:T(8,128)(2,1)S(1)}, u32[]{:S(2)}) copy-start(s16[520,128]{1,0:T(8,128)(2,1)S(1)} %collective-permute-done.13.refs_4_) | copy-start | bytes 399364
  86.9 16.6 %collective-permute-start.14 = (s16[520,128]{1,0:T(8,128)(2,1)}, s16[520,128]{1,0:T(8,128)(2,1)S(1)}, u32[]{:S(2)}, u32[]{:S(2)}) collective-permute-start(s16[520,128]{1,0:T(8,128)(2,1)} %get-tuple-element.96), channel_id=1, source_target_pairs={{0,12},{4,8},{8,4},{12,0},{16,28},{20,24},{24,20},{28,16},{1,13},{... | collective-permute-start | bytes 399368 | tf_op jit(solution)/shard_map/ppermute | solution.py:490
  86.9 7.7 %copy-start.15 = (s16[520,128]{1,0:T(8,128)(2,1)}, s16[520,128]{1,0:T(8,128)(2,1)S(1)}, u32[]{:S(2)}) copy-start(s16[520,128]{1,0:T(8,128)(2,1)S(1)} %collective-permute-done.11.refs_3_) | copy-start | bytes 399364
  86.9 19.6 %collective-permute-start.12 = (s16[520,128]{1,0:T(8,128)(2,1)}, s16[520,128]{1,0:T(8,128)(2,1)S(1)}, u32[]{:S(2)}, u32[]{:S(2)}) collective-permute-start(s16[520,128]{1,0:T(8,128)(2,1)} %get-tuple-element.92), channel_id=1, source_target_pairs={{0,8},{4,12},{8,0},{12,4},{16,24},{20,28},{24,16},{28,20},{1,9},{5... | collective-permute-start | bytes 399368 | tf_op jit(solution)/shard_map/ppermute | solution.py:490
  87.0 7.6 %copy-start.18 = (s16[520,128]{1,0:T(8,128)(2,1)}, s16[520,128]{1,0:T(8,128)(2,1)S(1)}, u32[]{:S(2)}) copy-start(s16[520,128]{1,0:T(8,128)(2,1)S(1)} %collective-permute-done.19.refs_7_) | copy-start | bytes 399364
  87.0 19.7 %collective-permute-start.20 = (s16[520,128]{1,0:T(8,128)(2,1)}, s16[520,128]{1,0:T(8,128)(2,1)S(1)}, u32[]{:S(2)}, u32[]{:S(2)}) collective-permute-start(s16[520,128]{1,0:T(8,128)(2,1)} %get-tuple-element.108), channel_id=1, source_target_pairs={{0,24},{4,28},{8,16},{12,20},{16,8},{20,12},{24,0},{28,4},{1,25},{... | collective-permute-start | bytes 399368 | tf_op jit(solution)/shard_map/ppermute | solution.py:490
  90.8 3.7 %copy-start.20 = (s16[520,128]{1,0:T(8,128)(2,1)}, s16[520,128]{1,0:T(8,128)(2,1)S(1)}, u32[]{:S(2)}) copy-start(s16[520,128]{1,0:T(8,128)(2,1)S(1)} %collective-permute-done.17.refs_6_) | copy-start | bytes 399364
  90.9 22.0 %collective-permute-start.18 = (s16[520,128]{1,0:T(8,128)(2,1)}, s16[520,128]{1,0:T(8,128)(2,1)S(1)}, u32[]{:S(2)}, u32[]{:S(2)}) collective-permute-start(s16[520,128]{1,0:T(8,128)(2,1)} %get-tuple-element.104), channel_id=1, source_target_pairs={{0,20},{4,16},{8,28},{12,24},{16,4},{20,0},{24,12},{28,8},{1,21},{... | collective-permute-start | bytes 399368 | tf_op jit(solution)/shard_map/ppermute | solution.py:490
  93.3 30.2 %copy-start.2 = (s16[520,128]{1,0:T(8,128)(2,1)}, s16[520,128]{1,0:T(8,128)(2,1)S(1)}, u32[]{:S(2)}) copy-start(s16[520,128]{1,0:T(8,128)(2,1)S(1)} %collective-permute-done.8.refs_9_) | copy-start | bytes 399364
  93.3 21.6 %collective-permute-start.9 = (s16[520,128]{1,0:T(8,128)(2,1)}, s16[520,128]{1,0:T(8,128)(2,1)S(1)}, u32[]{:S(2)}, u32[]{:S(2)}) collective-permute-start(s16[520,128]{1,0:T(8,128)(2,1)} %get-tuple-element.86), channel_id=1, source_target_pairs={{0,4},{4,0},{8,12},{12,8},{16,20},{20,16},{24,28},{28,24},{1,5},{5... | collective-permute-start | bytes 399368 | tf_op jit(solution)/shard_map/ppermute | solution.py:490
  103.5 21.1 %copy-start.3 = (s16[520,128]{1,0:T(8,128)(2,1)}, s16[520,128]{1,0:T(8,128)(2,1)S(1)}, u32[]{:S(2)}) copy-start(s16[520,128]{1,0:T(8,128)(2,1)S(1)} %collective-permute-done.14.refs_5_) | copy-start | bytes 399364
  103.5 11.6 %collective-permute-start.15 = (s16[520,128]{1,0:T(8,128)(2,1)}, s16[520,128]{1,0:T(8,128)(2,1)S(1)}, u32[]{:S(2)}, u32[]{:S(2)}) collective-permute-start(s16[520,128]{1,0:T(8,128)(2,1)} %get-tuple-element.98), channel_id=1, source_target_pairs={{0,16},{4,20},{8,24},{12,28},{16,0},{20,4},{24,8},{28,12},{1,17},{... | collective-permute-start | bytes 399368 | tf_op jit(solution)/shard_map/ppermute | solution.py:490
  106.5 18.1 %copy-start.4 = (s16[520,128]{1,0:T(8,128)(2,1)}, s16[520,128]{1,0:T(8,128)(2,1)S(1)}, u32[]{:S(2)}) copy-start(s16[520,128]{1,0:T(8,128)(2,1)S(1)} %collective-permute-done.12.refs_4_) | copy-start | bytes 399364
  106.5 11.5 %collective-permute-start.24 = (s16[520,128]{1,0:T(8,128)(2,1)}, s16[520,128]{1,0:T(8,128)(2,1)S(1)}, u32[]{:S(2)}, u32[]{:S(2)}) collective-permute-start(s16[520,128]{1,0:T(8,128)(2,1)} %get-tuple-element.118), channel_id=1, source_target_pairs={{0,12},{4,8},{8,4},{12,0},{16,28},{20,24},{24,20},{28,16},{1,13},{... | collective-permute-start | bytes 399368 | tf_op jit(solution)/shard_map/ppermute | solution.py:490
  106.7 17.9 %copy-start.5 = (s16[520,128]{1,0:T(8,128)(2,1)}, s16[520,128]{1,0:T(8,128)(2,1)S(1)}, u32[]{:S(2)}) copy-start(s16[520,128]{1,0:T(8,128)(2,1)S(1)} %collective-permute-done.20.refs_8_) | copy-start | bytes 399364
  106.7 12.7 %collective-permute-start.21 = (s16[520,128]{1,0:T(8,128)(2,1)}, s16[520,128]{1,0:T(8,128)(2,1)S(1)}, u32[]{:S(2)}, u32[]{:S(2)}) collective-permute-start(s16[520,128]{1,0:T(8,128)(2,1)} %get-tuple-element.113), channel_id=1, source_target_pairs={{0,28},{4,24},{8,20},{12,16},{16,12},{20,8},{24,4},{28,0},{1,29},{... | collective-permute-start | bytes 399368 | tf_op jit(solution)/shard_map/ppermute | solution.py:490
  112.9 11.8 %copy-start.6 = (s16[520,128]{1,0:T(8,128)(2,1)}, s16[520,128]{1,0:T(8,128)(2,1)S(1)}, u32[]{:S(2)}) copy-start(s16[520,128]{1,0:T(8,128)(2,1)S(1)} %collective-permute-done.18.refs_7_) | copy-start | bytes 399364
  112.9 14.9 %collective-permute-start.27 = (s16[520,128]{1,0:T(8,128)(2,1)}, s16[520,128]{1,0:T(8,128)(2,1)S(1)}, u32[]{:S(2)}, u32[]{:S(2)}) collective-permute-start(s16[520,128]{1,0:T(8,128)(2,1)} %get-tuple-element.124), channel_id=1, source_target_pairs={{0,24},{4,28},{8,16},{12,20},{16,8},{20,12},{24,0},{28,4},{1,25},{... | collective-permute-start | bytes 399368 | tf_op jit(solution)/shard_map/ppermute | solution.py:490
  114.9 9.8 %copy-start.7 = (s16[520,128]{1,0:T(8,128)(2,1)}, s16[520,128]{1,0:T(8,128)(2,1)S(1)}, u32[]{:S(2)}) copy-start(s16[520,128]{1,0:T(8,128)(2,1)S(1)} %collective-permute-done.9.refs_3_) | copy-start | bytes 399364
  114.9 12.9 %collective-permute-start.23 = (s16[520,128]{1,0:T(8,128)(2,1)}, s16[520,128]{1,0:T(8,128)(2,1)}, u32[]{:S(2)}, u32[]{:S(2)}) collective-permute-start(s16[520,128]{1,0:T(8,128)(2,1)} %get-tuple-element.116), channel_id=1, source_target_pairs={{0,8},{4,12},{8,0},{12,4},{16,24},{20,28},{24,16},{28,20},{1,9},{5... | collective-permute-start | bytes 399368 | tf_op jit(solution)/shard_map/ppermute | solution.py:490
  115.1 9.5 %copy-start.8 = (s16[520,128]{1,0:T(8,128)(2,1)}, s16[520,128]{1,0:T(8,128)(2,1)S(1)}, u32[]{:S(2)}) copy-start(s16[520,128]{1,0:T(8,128)(2,1)S(1)} %collective-permute-done.15.refs_6_) | copy-start | bytes 399364
  115.1 14.8 %collective-permute-start.26 = (s16[520,128]{1,0:T(8,128)(2,1)}, s16[520,128]{1,0:T(8,128)(2,1)}, u32[]{:S(2)}, u32[]{:S(2)}) collective-permute-start(s16[520,128]{1,0:T(8,128)(2,1)} %get-tuple-element.122), channel_id=1, source_target_pairs={{0,20},{4,16},{8,28},{12,24},{16,4},{20,0},{24,12},{28,8},{1,21},{... | collective-permute-start | bytes 399368 | tf_op jit(solution)/shard_map/ppermute | solution.py:490
  118.1 6.6 %copy-start.9 = (s16[520,128]{1,0:T(8,128)(2,1)}, s16[520,128]{1,0:T(8,128)(2,1)S(1)}, u32[]{:S(2)}) copy-start(s16[520,128]{1,0:T(8,128)(2,1)S(1)} %collective-permute-done.24.refs_13_) | copy-start | bytes 399364
  118.1 13.1 %collective-permute-start.25 = (s16[520,128]{1,0:T(8,128)(2,1)}, s16[520,128]{1,0:T(8,128)(2,1)}, u32[]{:S(2)}, u32[]{:S(2)}) collective-permute-start(s16[520,128]{1,0:T(8,128)(2,1)} %get-tuple-element.120), channel_id=1, source_target_pairs={{0,16},{4,20},{8,24},{12,28},{16,0},{20,4},{24,8},{28,12},{1,17},{... | collective-permute-start | bytes 399368 | tf_op jit(solution)/shard_map/ppermute | solution.py:490
  119.4 5.3 %copy-start.11 = (s16[520,128]{1,0:T(8,128)(2,1)}, s16[520,128]{1,0:T(8,128)(2,1)S(1)}, u32[]{:S(2)}) copy-start(s16[520,128]{1,0:T(8,128)(2,1)S(1)} %collective-permute-done.21.refs_17_) | copy-start | bytes 399364
  119.4 11.8 %collective-permute-start.22 = (s16[520,128]{1,0:T(8,128)(2,1)}, s16[520,128]{1,0:T(8,128)(2,1)}, u32[]{:S(2)}, u32[]{:S(2)}) collective-permute-start(s16[520,128]{1,0:T(8,128)(2,1)} %get-tuple-element.114), channel_id=1, source_target_pairs={{0,4},{4,0},{8,12},{12,8},{16,20},{20,16},{24,28},{28,24},{1,5},{5... | collective-permute-start | bytes 399368 | tf_op jit(solution)/shard_map/ppermute | solution.py:490
  125.3 20.2 %copy-start.27 = (s32[1,256]{1,0:T(1,128)S(1)}, s32[1,256]{1,0:T(1,128)}, u32[]{:S(2)}) copy-start(s32[1,256]{1,0:T(1,128)} %get-tuple-element.128) | copy-start | bytes 3076
  127.8 3.4 %copy-start.21 = (s16[520,128]{1,0:T(8,128)(2,1)}, s16[520,128]{1,0:T(8,128)(2,1)S(1)}, u32[]{:S(2)}) copy-start(s16[520,128]{1,0:T(8,128)(2,1)S(1)} %collective-permute-done.27.refs_16_) | copy-start | bytes 399364
  141.6 12.0 %all-to-all-start.1 = ((f32[32,8,128]{2,1,0:T(8,128)}), f32[32,8,128]{2,1,0:T(8,128)S(1)}, u32[]{:S(2)}, u32[]{:S(2)}) async-start(f32[32,8,128]{2,1,0:T(8,128)} %get-tuple-element.127), calls=%async_computation.1 | async-start | bytes 262144 | tf_op jit(solution)/shard_map/all_to_all | solution.py:669
  153.6 0.7 copy-start.1
Sparse Core Ops, SparseCore 0:
  43.2 25.5 all-gather.2
